TPU v7x, 32 devices: a whole 2x2x4 slice. The times are simulated.
32 devices in a mesh: dp: 16 (over z, y, core), tensor: 2 (over x).
Axes of the slice: x: 2, y: 2, z: 4, core: 2. Of those that a mesh axis runs over, the one named last changes fastest.
Arguments:
- tokens: bfloat16 [24576, 896], P('dp'), may hold values from -6 to 6
- cotangent: bfloat16 [24576, 896], P('dp'), may hold values from -6 to 6
- order: int32 [16, 1536], P('dp'), may hold values from 0 to 1535, each once within a row
- lengths: int32 [16, 3], P('dp'), may hold values from 1 to 1024, 1536 in all within a row
- adapter_ids: int32 [16, 3], P('dp'), may hold values from 0 to 7
- norm_gains: bfloat16 [2, 896], replicated, may hold values from 0.099609375 to 1.8984375
- w_query: bfloat16 [896, 896], P(None, 'tensor'), may hold values from -0.25 to 0.25
- w_key: bfloat16 [896, 128], P(None, 'tensor'), may hold values from -0.25 to 0.25
- w_value: bfloat16 [896, 128], P(None, 'tensor'), may hold values from -0.1875 to 0.1875
- b_query: bfloat16 [896], P('tensor'), may hold values from -3 to 3
- b_key: bfloat16 [128], P('tensor'), may hold values from -3 to 3
- b_value: bfloat16 [128], P('tensor'), may hold values from -3 to 3
- w_out: bfloat16 [896, 896], P('tensor'), may hold values from -0.25 to 0.25
- w_gate: bfloat16 [896, 4864], P(None, 'tensor'), may hold values from -0.1875 to 0.1875
- w_up: bfloat16 [896, 4864], P(None, 'tensor'), may hold values from -0.1875 to 0.1875
- w_down: bfloat16 [4864, 896], P('tensor'), may hold values from -0.078125 to 0.078125
- adapters: float32 [22912, 128], P(('dp', 'tensor'))
- first_moment: float32 [22912, 128], P(('dp', 'tensor'))
- second_moment: float32 [22912, 128], P(('dp', 'tensor')), as said below
Outputs:
- layer_output: bfloat16 [24576, 896], P('dp')
- input_grad: bfloat16 [24576, 896], P('dp')
- adapter_grad: float32 [22912, 128], P(('dp', 'tensor'))
- first_moment_new: float32 [22912, 128], P(('dp', 'tensor'))
- second_moment_new: float32 [22912, 128], P(('dp', 'tensor'))
- adapters_new: float32 [22912, 128], P(('dp', 'tensor'))
- adapter_copy: bfloat16 [22912, 128], P(('dp', 'tensor'))
Inputs may be any that keep to these rules, and one draw needn't show every extreme that they name: Each row of order is a permutation of 0 to 1535. Each row of lengths sums to 1536 and holds a sequence of exactly 1024 tokens. `second_moment`: positive.
All inputs are finite; a program needn't handle non-finite values.
Results may differ from a plain program's by a relative error of at most 0.017.
Values may be sent and summed in bfloat16 or wider, within the bound.
A program may use at most 256 MiB of HBM per device.

v0:
```python
import jax
import jax.numpy as jnp
from jax import lax
from jax.sharding import PartitionSpec as P

HEAD_DIMENSION = 64
RANK = 16
QUERY_BLOCK_ROWS = 512
STEP = 3


ADAPTER_SCALE = 2.0
NORM_EPS = 1e-06
ROPE_BASE = 1000000.0
BETA_ONE = 0.5
BETA_TWO = 0.6
LEARN_RATE = 0.04
WEIGHT_DECAY = 0.01
ADAM_EPS = 1e-08
MASKED_SCORE = -1e30


def dot_plain(left, right):
    return jnp.dot(left, right, preferred_element_type=jnp.float32)


def dot_last(left, right):
    return lax.dot_general(
        left, right, (((1,), (1,)), ((), ())), preferred_element_type=jnp.float32
    )


def dot_rows(left, right):
    return lax.dot_general(
        left, right, (((0,), (0,)), ((), ())), preferred_element_type=jnp.float32
    )


def own_part(values, tensor_parts, tensor_part, axis_number):
    size_each = values.shape[axis_number] // tensor_parts
    return lax.dynamic_slice_in_dim(values, tensor_part * size_each, size_each, axis_number)


def spread(block_rows, tensor_parts, tensor_part):
    slots = jnp.arange(tensor_parts, dtype=jnp.int32)[:, None, None] == tensor_part
    placed = jnp.where(slots, block_rows[None], 0.0)
    return placed.reshape(tensor_parts * block_rows.shape[0], block_rows.shape[1])


def section_list(model_width, query_width, pair_width, hidden_width):
    return [
        (model_width, query_width),
        (model_width, pair_width),
        (model_width, pair_width),
        (query_width, model_width),
        (model_width, hidden_width),
        (model_width, hidden_width),
        (hidden_width, model_width),
    ]


def section_row_list(packed_rows, shape_list):
    pieces = []
    cursor = 0
    for fan_in, fan_out in shape_list:
        pieces.append(
            (
                packed_rows[cursor : cursor + fan_in],
                packed_rows[cursor + fan_in : cursor + fan_in + fan_out],
            )
        )
        cursor = cursor + fan_in + fan_out
    return pieces


def rms_scale(values, gain):
    return values * lax.rsqrt(jnp.mean(values * values, axis=-1, keepdims=True) + NORM_EPS) * gain


def norm_back(values, gain, grad_normed):
    inverse = lax.rsqrt(jnp.mean(values * values, axis=-1, keepdims=True) + NORM_EPS)
    weighted = grad_normed * gain
    return inverse * weighted - values * inverse * inverse * inverse * jnp.mean(
        weighted * values, axis=-1, keepdims=True
    )


def turn_half(values):
    half_size = values.shape[-1] // 2
    return jnp.concatenate([-values[..., half_size:], values[..., :half_size]], axis=-1)


def rotate_pairs(values, cosine_lookup, sine_lookup):
    return values * cosine_lookup + turn_half(values) * sine_lookup


def unrotate(values, cosine_lookup, sine_lookup):
    return values * cosine_lookup - turn_half(values) * sine_lookup


def token_tables(lengths_row, adapter_row, count_of_rows):
    seq_ends = jnp.cumsum(lengths_row)
    starts = seq_ends - lengths_row
    places = jnp.arange(count_of_rows, dtype=jnp.int32)
    member = ((places[:, None] >= starts[None, :]) & (places[:, None] < seq_ends[None, :])).astype(
        jnp.int32
    )
    seq_index = jnp.arange(lengths_row.shape[0], dtype=jnp.int32)
    segment = jnp.sum(member * seq_index[None, :], axis=1)
    position = places - jnp.sum(member * starts[None, :], axis=1)
    chosen = jnp.sum(member * adapter_row[None, :], axis=1)
    return (segment, position, chosen)


def rope_tables(position, head_size):
    freq_index = jnp.arange(head_size // 2, dtype=jnp.float32)
    inv_freq = jnp.power(jnp.float32(ROPE_BASE), -2.0 * freq_index / head_size)
    angles = position.astype(jnp.float32)[:, None] * inv_freq[None, :]
    angles = jnp.concatenate([angles, angles], axis=1)
    return (jnp.cos(angles)[:, None, :], jnp.sin(angles)[:, None, :])


def adapter_mask(chosen, rank_all):
    columns = jnp.arange(rank_all, dtype=jnp.int32) // RANK
    return (columns[None, :] == chosen[:, None]).astype(jnp.float32)


def allowed_mask(segment, key_index, row_start):
    query_index = row_start + jnp.arange(QUERY_BLOCK_ROWS, dtype=jnp.int32)
    query_segment = lax.dynamic_slice_in_dim(segment, row_start, QUERY_BLOCK_ROWS)
    return (key_index[None, :] <= query_index[:, None]) & (
        segment[None, :] == query_segment[:, None]
    )


def attend_forward(query_rows, key_vectors, value_vectors, segment, score_scale):
    count_of_rows = key_vectors.shape[0]
    key_index = jnp.arange(count_of_rows, dtype=jnp.int32)
    blocks = count_of_rows // QUERY_BLOCK_ROWS
    query_blocks = query_rows.reshape((blocks, QUERY_BLOCK_ROWS) + query_rows.shape[1:])

    def one_block(block_in):
        query_block, row_start = block_in
        allowed = allowed_mask(segment, key_index, row_start)
        scores = (
            jnp.einsum(
                "qkgd,skd->kgqs", query_block, key_vectors, preferred_element_type=jnp.float32
            )
            * score_scale
        )
        scores = jnp.where(allowed[None, None], scores, MASKED_SCORE)
        highest = jnp.max(scores, axis=-1, keepdims=True)
        exponent = jnp.exp(scores - highest)
        totals = jnp.sum(exponent, axis=-1, keepdims=True)
        probabilities = (exponent / totals).astype(jnp.bfloat16)
        result = jnp.einsum(
            "kgqs,skd->qkgd", probabilities, value_vectors, preferred_element_type=jnp.float32
        )
        return (result, highest[..., 0] + jnp.log(totals[..., 0]))

    starts = jnp.arange(blocks, dtype=jnp.int32) * QUERY_BLOCK_ROWS
    results, log_totals = lax.map(one_block, (query_blocks, starts))
    return (results.reshape(query_rows.shape), log_totals)


def attend_backward(
    query_rows, key_vectors, value_vectors, grad_attn, log_totals, segment, score_scale
):
    count_of_rows = key_vectors.shape[0]
    key_index = jnp.arange(count_of_rows, dtype=jnp.int32)
    blocks = count_of_rows // QUERY_BLOCK_ROWS
    query_blocks = query_rows.reshape((blocks, QUERY_BLOCK_ROWS) + query_rows.shape[1:])
    grad_blocks = grad_attn.reshape((blocks, QUERY_BLOCK_ROWS) + grad_attn.shape[1:])
    starts = jnp.arange(blocks, dtype=jnp.int32) * QUERY_BLOCK_ROWS

    def one_block(carry, block_in):
        grad_keys, grad_values = carry
        query_block, grad_block, log_block, row_start = block_in
        allowed = allowed_mask(segment, key_index, row_start)
        scores = (
            jnp.einsum(
                "qkgd,skd->kgqs", query_block, key_vectors, preferred_element_type=jnp.float32
            )
            * score_scale
        )
        scores = jnp.where(allowed[None, None], scores, MASKED_SCORE)
        probabilities = jnp.where(allowed[None, None], jnp.exp(scores - log_block[..., None]), 0.0)
        grad_probs = jnp.einsum(
            "qkgd,skd->kgqs", grad_block, value_vectors, preferred_element_type=jnp.float32
        )
        row_dot = jnp.sum(probabilities * grad_probs, axis=-1, keepdims=True)
        grad_scores = (probabilities * (grad_probs - row_dot)).astype(jnp.bfloat16)
        grad_query = (
            jnp.einsum(
                "kgqs,skd->qkgd", grad_scores, key_vectors, preferred_element_type=jnp.float32
            )
            * score_scale
        )
        grad_keys = (
            grad_keys
            + jnp.einsum(
                "kgqs,qkgd->skd", grad_scores, query_block, preferred_element_type=jnp.float32
            )
            * score_scale
        )
        grad_values = grad_values + jnp.einsum(
            "kgqs,qkgd->skd",
            probabilities.astype(jnp.bfloat16),
            grad_block,
            preferred_element_type=jnp.float32,
        )
        return ((grad_keys, grad_values), grad_query)

    zero_keys = jnp.zeros(key_vectors.shape, jnp.float32)
    (grad_keys, grad_values), grad_query = lax.scan(
        one_block, (zero_keys, zero_keys), (query_blocks, grad_blocks, log_totals, starts)
    )
    return (grad_query.reshape(query_rows.shape), grad_keys, grad_values)


def per_device(
    tokens,
    cotangent,
    order,
    lengths,
    adapter_ids,
    norm_gains,
    w_query,
    w_key,
    w_value,
    b_query,
    b_key,
    b_value,
    w_out,
    w_gate,
    w_up,
    w_down,
    adapters,
    first_moment,
    second_moment,
):
    tensor_parts = lax.axis_size("tensor")
    tensor_part = lax.axis_index("tensor")
    moved_rows, moved_back = (
        lax.all_to_all(tokens, "dp", split_axis=0, concat_axis=0, tiled=True),
        lax.all_to_all(cotangent, "dp", split_axis=0, concat_axis=0, tiled=True),
    )
    copies = lax.all_gather(adapters.astype(jnp.bfloat16), ("dp", "tensor"), axis=0, tiled=True)
    row_order = order[0]
    residual = moved_rows[row_order].astype(jnp.float32)
    grad_output = moved_back[row_order]
    count_of_rows, model_width = residual.shape
    segment, position, chosen = token_tables(lengths[0], adapter_ids[0], count_of_rows)
    cosine_lookup, sine_lookup = rope_tables(position, HEAD_DIMENSION)
    rank_all = adapters.shape[1]
    rank_mask = adapter_mask(chosen, rank_all)
    mask_low = rank_mask.astype(jnp.bfloat16)
    query_local = w_query.shape[1]
    pair_local = w_key.shape[1]
    hidden_local = w_gate.shape[1]
    shape_list = section_list(
        model_width,
        query_local * tensor_parts,
        pair_local * tensor_parts,
        hidden_local * tensor_parts,
    )
    adapter_row_list = section_row_list(copies, shape_list)
    enter_query, leave_query = adapter_row_list[0]
    enter_key, leave_key = adapter_row_list[1]
    enter_value, leave_value = adapter_row_list[2]
    enter_out, leave_out = adapter_row_list[3]
    enter_gate, leave_gate = adapter_row_list[4]
    enter_up, leave_up = adapter_row_list[5]
    enter_down, leave_down = adapter_row_list[6]
    leave_query_own = own_part(leave_query, tensor_parts, tensor_part, 0)
    leave_key_own = own_part(leave_key, tensor_parts, tensor_part, 0)
    leave_value_own = own_part(leave_value, tensor_parts, tensor_part, 0)
    enter_out_own = own_part(enter_out, tensor_parts, tensor_part, 0)
    leave_gate_own = own_part(leave_gate, tensor_parts, tensor_part, 0)
    leave_up_own = own_part(leave_up, tensor_parts, tensor_part, 0)
    enter_down_own = own_part(enter_down, tensor_parts, tensor_part, 0)

    def low_rank(inputs, enter_rows):
        return (rank_mask * dot_plain(inputs, enter_rows)).astype(jnp.bfloat16)

    gain_one = norm_gains[0].astype(jnp.float32)
    gain_two = norm_gains[1].astype(jnp.float32)
    normed = rms_scale(residual, gain_one).astype(jnp.bfloat16)
    rank_query = low_rank(normed, enter_query)
    rank_key = low_rank(normed, enter_key)
    rank_value = low_rank(normed, enter_value)
    query_pre = (
        dot_plain(normed, w_query)
        + b_query.astype(jnp.float32)
        + ADAPTER_SCALE * dot_last(rank_query, leave_query_own)
    )
    key_pre = (
        dot_plain(normed, w_key)
        + b_key.astype(jnp.float32)
        + ADAPTER_SCALE * dot_last(rank_key, leave_key_own)
    )
    value_pre = (
        dot_plain(normed, w_value)
        + b_value.astype(jnp.float32)
        + ADAPTER_SCALE * dot_last(rank_value, leave_value_own)
    )
    head_local = query_local // HEAD_DIMENSION
    kv_local = pair_local // HEAD_DIMENSION
    group_width = head_local // kv_local
    query_rows = rotate_pairs(
        query_pre.reshape(count_of_rows, head_local, HEAD_DIMENSION), cosine_lookup, sine_lookup
    ).astype(jnp.bfloat16)
    query_rows = query_rows.reshape(count_of_rows, kv_local, group_width, HEAD_DIMENSION)
    key_vectors = rotate_pairs(
        key_pre.reshape(count_of_rows, kv_local, HEAD_DIMENSION), cosine_lookup, sine_lookup
    ).astype(jnp.bfloat16)
    value_vectors = value_pre.astype(jnp.bfloat16).reshape(count_of_rows, kv_local, HEAD_DIMENSION)
    score_scale = HEAD_DIMENSION ** (-0.5)
    attended, log_totals = attend_forward(
        query_rows, key_vectors, value_vectors, segment, score_scale
    )
    attended = attended.reshape(count_of_rows, query_local).astype(jnp.bfloat16)
    branch_part = dot_plain(attended, w_out)
    rank_out_part = dot_plain(attended, enter_out_own)
    branch_sum, rank_out_sum = lax.psum((branch_part, rank_out_part), "tensor")
    rank_out = (rank_mask * rank_out_sum).astype(jnp.bfloat16)
    middle = residual + (branch_sum + ADAPTER_SCALE * dot_last(rank_out, leave_out))
    normed_two = rms_scale(middle, gain_two).astype(jnp.bfloat16)
    rank_gate = low_rank(normed_two, enter_gate)
    rank_up = low_rank(normed_two, enter_up)
    gate_pre, up_pre = (
        dot_plain(normed_two, w_gate) + ADAPTER_SCALE * dot_last(rank_gate, leave_gate_own),
        dot_plain(normed_two, w_up) + ADAPTER_SCALE * dot_last(rank_up, leave_up_own),
    )
    hidden = (jax.nn.silu(gate_pre) * up_pre).astype(jnp.bfloat16)
    down_part = dot_plain(hidden, w_down)
    rank_down_part = dot_plain(hidden, enter_down_own)
    down_sum, rank_down_sum = lax.psum((down_part, rank_down_part), "tensor")
    rank_down = (rank_mask * rank_down_sum).astype(jnp.bfloat16)
    layer_out = middle + (down_sum + ADAPTER_SCALE * dot_last(rank_down, leave_down))
    back_down = (ADAPTER_SCALE * dot_plain(grad_output, leave_down)).astype(jnp.bfloat16) * mask_low
    grad_enter_down = dot_rows(hidden, back_down)
    grad_leave_down = ADAPTER_SCALE * dot_rows(
        own_part(grad_output, tensor_parts, tensor_part, 1), rank_down
    )
    grad_hidden = dot_last(grad_output, w_down) + dot_last(back_down, enter_down_own)
    sigmoid_gate = jax.nn.sigmoid(gate_pre)
    grad_gate = (
        grad_hidden * up_pre * sigmoid_gate * (1.0 + gate_pre * (1.0 - sigmoid_gate))
    ).astype(jnp.bfloat16)
    grad_up = (grad_hidden * gate_pre * sigmoid_gate).astype(jnp.bfloat16)
    normed_two_part = dot_last(grad_gate, w_gate) + dot_last(grad_up, w_up)
    rank_gate_part = ADAPTER_SCALE * dot_plain(grad_gate, leave_gate_own)
    rank_up_part = ADAPTER_SCALE * dot_plain(grad_up, leave_up_own)
    grad_leave_gate = ADAPTER_SCALE * dot_rows(grad_gate, rank_gate)
    grad_leave_up = ADAPTER_SCALE * dot_rows(grad_up, rank_up)
    normed_two_sum, rank_gate_sum, rank_up_sum = lax.psum(
        (normed_two_part, rank_gate_part, rank_up_part), "tensor"
    )
    back_gate = rank_gate_sum.astype(jnp.bfloat16) * mask_low
    back_up = rank_up_sum.astype(jnp.bfloat16) * mask_low
    normed_two_own = own_part(normed_two, tensor_parts, tensor_part, 1)
    grad_enter_gate = dot_rows(normed_two_own, back_gate)
    grad_enter_up = dot_rows(normed_two_own, back_up)
    grad_normed_two = normed_two_sum + dot_last(back_gate, enter_gate) + dot_last(back_up, enter_up)
    grad_middle = grad_output.astype(jnp.float32) + norm_back(middle, gain_two, grad_normed_two)
    grad_branch = grad_middle.astype(jnp.bfloat16)
    back_out = (ADAPTER_SCALE * dot_plain(grad_branch, leave_out)).astype(jnp.bfloat16) * mask_low
    grad_leave_out = ADAPTER_SCALE * dot_rows(
        own_part(grad_branch, tensor_parts, tensor_part, 1), rank_out
    )
    grad_enter_out = dot_rows(attended, back_out)
    grad_attended = (dot_last(grad_branch, w_out) + dot_last(back_out, enter_out_own)).astype(
        jnp.bfloat16
    )
    grad_queries, grad_keys, grad_values = attend_backward(
        query_rows,
        key_vectors,
        value_vectors,
        grad_attended.reshape(count_of_rows, kv_local, group_width, HEAD_DIMENSION),
        log_totals,
        segment,
        score_scale,
    )
    grad_query_pre = unrotate(
        grad_queries.reshape(count_of_rows, head_local, HEAD_DIMENSION), cosine_lookup, sine_lookup
    )
    grad_query_pre = grad_query_pre.astype(jnp.bfloat16).reshape(count_of_rows, query_local)
    grad_key_pre = (
        unrotate(grad_keys, cosine_lookup, sine_lookup)
        .astype(jnp.bfloat16)
        .reshape(count_of_rows, pair_local)
    )
    grad_value_pre = grad_values.astype(jnp.bfloat16).reshape(count_of_rows, pair_local)
    normed_part = (
        dot_last(grad_query_pre, w_query)
        + dot_last(grad_key_pre, w_key)
        + dot_last(grad_value_pre, w_value)
    )
    rank_query_part = ADAPTER_SCALE * dot_plain(grad_query_pre, leave_query_own)
    rank_key_part = ADAPTER_SCALE * dot_plain(grad_key_pre, leave_key_own)
    rank_value_part = ADAPTER_SCALE * dot_plain(grad_value_pre, leave_value_own)
    grad_leave_query = ADAPTER_SCALE * dot_rows(grad_query_pre, rank_query)
    grad_leave_key = ADAPTER_SCALE * dot_rows(grad_key_pre, rank_key)
    grad_leave_value = ADAPTER_SCALE * dot_rows(grad_value_pre, rank_value)
    normed_sum, rank_query_sum, rank_key_sum, rank_value_sum = (
        lax.psum(normed_part.astype(jnp.bfloat16), "tensor").astype(jnp.float32),
        lax.psum(rank_query_part.astype(jnp.bfloat16), "tensor").astype(jnp.float32),
        lax.psum(rank_key_part.astype(jnp.bfloat16), "tensor").astype(jnp.float32),
        lax.psum(rank_value_part.astype(jnp.bfloat16), "tensor").astype(jnp.float32),
    )
    back_query = rank_query_sum.astype(jnp.bfloat16) * mask_low
    back_key = rank_key_sum.astype(jnp.bfloat16) * mask_low
    back_value = rank_value_sum.astype(jnp.bfloat16) * mask_low
    normed_own = own_part(normed, tensor_parts, tensor_part, 1)
    grad_enter_query = dot_rows(normed_own, back_query)
    grad_enter_key = dot_rows(normed_own, back_key)
    grad_enter_value = dot_rows(normed_own, back_value)
    grad_normed = (
        normed_sum
        + dot_last(back_query, enter_query)
        + dot_last(back_key, enter_key)
        + dot_last(back_value, enter_value)
    )
    grad_input = grad_middle + norm_back(residual, gain_one, grad_normed)
    local_pieces = [
        grad_enter_query,
        grad_leave_query,
        grad_enter_key,
        grad_leave_key,
        grad_enter_value,
        grad_leave_value,
        grad_enter_out,
        grad_leave_out,
        grad_enter_gate,
        grad_leave_gate,
        grad_enter_up,
        grad_leave_up,
        grad_enter_down,
        grad_leave_down,
    ]
    grad_full = jnp.concatenate(
        [spread(piece_rows, tensor_parts, tensor_part) for piece_rows in local_pieces], axis=0
    )
    reduced = lax.psum_scatter(grad_full, ("dp", "tensor"), scatter_dimension=0, tiled=True)
    moment_one = BETA_ONE * first_moment + (1.0 - BETA_ONE) * reduced
    moment_two = BETA_TWO * second_moment + (1.0 - BETA_TWO) * reduced * reduced
    corrected_one = moment_one / (1.0 - BETA_ONE**STEP)
    corrected_two = moment_two / (1.0 - BETA_TWO**STEP)
    updated = adapters - LEARN_RATE * (
        corrected_one / (jnp.sqrt(corrected_two) + ADAM_EPS) + WEIGHT_DECAY * adapters
    )
    placed_out = (
        jnp.zeros((count_of_rows, model_width), jnp.bfloat16)
        .at[row_order]
        .set(layer_out.astype(jnp.bfloat16))
    )
    placed_grad = (
        jnp.zeros((count_of_rows, model_width), jnp.bfloat16)
        .at[row_order]
        .set(grad_input.astype(jnp.bfloat16))
    )
    arrival_out, arrival_grad = (
        lax.all_to_all(placed_out, "dp", split_axis=0, concat_axis=0, tiled=True),
        lax.all_to_all(placed_grad, "dp", split_axis=0, concat_axis=0, tiled=True),
    )
    return (
        arrival_out,
        arrival_grad,
        reduced,
        moment_one,
        moment_two,
        updated,
        updated.astype(jnp.bfloat16),
    )


def solution(mesh):
    return jax.shard_map(
        per_device,
        mesh=mesh,
        in_specs=(
            P("dp", None),
            P("dp", None),
            P("dp", None),
            P("dp", None),
            P("dp", None),
            P(),
            P(None, "tensor"),
            P(None, "tensor"),
            P(None, "tensor"),
            P("tensor"),
            P("tensor"),
            P("tensor"),
            P("tensor", None),
            P(None, "tensor"),
            P(None, "tensor"),
            P("tensor", None),
            P(("dp", "tensor"), None),
            P(("dp", "tensor"), None),
            P(("dp", "tensor"), None),
        ),
        out_specs=(
            P("dp", None),
            P("dp", None),
            P(("dp", "tensor"), None),
            P(("dp", "tensor"), None),
            P(("dp", "tensor"), None),
            P(("dp", "tensor"), None),
            P(("dp", "tensor"), None),
        ),
        check_vma=False,
    )
```

profile of v0, /device:TPU:1, one launch (start us, length us, event | category | flops | bytes accessed | tf_op | source)
XLA Modules:
  0.0 1554.2 jit_solution(13365620031752517127)
XLA Ops:
  35.6 45.3 %all-to-all-done = bf16[16,96,896]{2,1,0:T(8,128)(2,1)S(1)} async-done(((bf16[16,96,896]{2,1,0:T(8,128)(2,1)}), bf16[16,96,896]{2,1,0:T(8,128)(2,1)S(1)}, u32[]{:S(2)}, u32[]{:S(2)}) %all-to-all-start) | async-done | bytes 2752544 | tf_op jit(solution)/shard_map/all_to_all | solution.py:245
  80.9 14.5 all-to-all-start.2
  110.1 18.2 %all-gather.3.cloned.1.call-done = bf16[32,716,128]{2,1,0:T(8,128)(2,1)} async-done(((bf16[1,716,128]{2,1,0:T(8,128)(2,1)}), bf16[32,716,128]{2,1,0:T(8,128)(2,1)}) %all-gather.3.cloned.1.call-update) | async-done | bytes 5865488 | tf_op jit(solution)/shard_map/all_gather | solution.py:248
  177.3 67.9 %while.28 = (s32[]{:T(128)}, bf16[3,512,1,7,64]{1,4,3,2,0:T(8,128)(2,1)}, f32[3,1,7,512]{3,2,1,0:T(8,128)}, s32[3]{0:T(128)}, s32[1536]{0:T(1024)}, /*index=5*/b...) while((s32[]{:T(128)}, ...), condition=%wide.region_8.9_spmd.clone, body=%wide.region_5.8_spmd.clone.sunk | while | flops 1455682560 | bytes 81336592 | solution.py:162
  262.7 14.0 fusion.231
  280.9 42.2 %all-reduce.16 = bf16[1536,128]{1,0:T(8,128)(2,1)} all-reduce(f32[1536,128]{1,0:T(8,128)} %fusion.176), channel_id=1, replica_groups=mesh['dp'=16,'tensor'=2] {'tensor'}, use_global_device_ids=true, to_apply=%region_10.11 | all-reduce | flops 196608 | bytes 1179648 | tf_op jit(solution)/shard_map/psum | solution.py:325
  327.1 81.8 %all-reduce.11.cloned.1.call-done = f32[1536,896]{1,0:T(8,128)} async-done(((f32[1536,896]{1,0:T(8,128)}), f32[1536,896]{1,0:T(8,128)}) %all-reduce.11.cloned.1.call-update) | async-done | bytes 5505040 | tf_op jit(solution)/shard_map/psum | solution.py:325
  419.6 11.1 fusion.229
  439.3 12.7 multiply_add_fusion
  459.4 22.9 %multiply_convert_fusion = (bf16[1536,2432]{1,0:T(8,128)(2,1)}, bf16[1536,2432]{1,0:T(8,128)(2,1)}, bf16[1536,2432]{1,0:T(8,128)(2,1)}) fusion(f32[1536,2432]{1,0:T(8,128)} %multiply_add_fusion.1, f32[1536,2432]{1,0:T(8,128)} %multiply_add_fusion, f32[1536,2432]{1,0:T(8,128)} %fusion.231, bf16[1536,128]{1,0:T(8,128)(2,1)S(1)} %copy-done.69, ...), kind=kOutput, calls=%fused_computation.64 | convolution fusion | flops 1019805696 | bytes 68255744 | tf_op jit(solution)/shard_map/dot_general | solution.py:28
  482.4 13.4 fusion.232
  495.8 12.1 fusion.230
  508.0 11.7 convolution_add_fusion.1
  537.3 109.7 %all-reduce.17 = (bf16[1536,128]{1,0:T(8,128)(2,1)}, bf16[1536,128]{1,0:T(8,128)(2,1)}, bf16[1536,128]{1,0:T(8,128)(2,1)}) all-reduce(f32[1536,128]{1,0:T(8,128)} %fusion.124, f32[1536,128]{1,0:T(8,128)S(1)} %copy-done.57, f32[1536,128]{1,0:T(8,128)S(1)} %convolution_multiply_fusion.5), channel_id=1, replica_groups=mesh['dp'=16,'tensor'=2] {'tensor'}, use_global_device_ids=true, to_apply=%region_13.14 | all-reduce | flops 589824 | bytes 3538944 | tf_op jit(solution)/shard_map/psum | solution.py:338
  651.5 173.9 %all-reduce.13.cloned.1.call-done = (f32[1536,896]{1,0:T(8,128)}, f32[1536,896]{1,0:T(8,128)}) async-done(((f32[1536,896]{1,0:T(8,128)}, f32[1536,896]{1,0:T(8,128)}), (f32[1536,896]{1,0:T(8,128)}, f32[1536,896]{1,0:T(8,128)})) %all-reduce.13.cloned.1.call-update) | async-done | bytes 11010064 | tf_op jit(solution)/shard_map/psum | solution.py:338
  843.9 242.1 %while.29 = (s32[]{:T(128)}, f32[1536,1,64]{0,2,1:T(8,128)S(1)}, f32[1536,1,64]{0,2,1:T(8,128)S(1)}, f32[3,512,1,7,64]{1,0,4,3,2:T(4,128)}, bf16[3,512,1,7,64]{1...) while((s32[]{:T(128)}, f32[1536,1,64]{0,2,1:T(8,128)S(1)}, ...), condition=%wide.region_21.22_spmd.clone, body=%wide.region_19.21_spmd.clone.sunk | while | flops 3581342720 | bytes 180904192 | solution.py:215
  858.0 18.1 %fusion.333 = (f32[7,512]{1,0:T(8,128)S(1)}, f32[1,7,512,1536]{3,2,1,0:T(8,128)}) fusion(f32[512,7,1536]{2,0,1:T(8,128)} %fusion.331, f32[7,512]{1,0:T(8,128)S(1)} %dynamic-slice_bitcast_fusion.2, bf16[1536,1,64]{0,2,1:T(8,128)(2,1)S(1)} %get-tuple-element.545, bf16[3,512,1,7,64]{1,4,3,2,0:T(8,128)(2,1)S(1)} %copy-done.7, s32[]{:T(128)S(6)} %copy.111, ...), kind=kOutput, calls=%fused_computation.29.clone.1 | convolution fusion | flops 737669632 | bytes 45512708 | tf_op jit(solution)/shard_map/while/body/eval_jaxpr/qkgd,skd->kgqs/dot_general | solution.py:181
  876.1 14.3 fusion.334
  890.4 9.3 fusion.336
  906.2 18.6 %dynamic_update_slice.21 = f32[3,512,1,7,64]{1,0,4,3,2:T(4,128)} dynamic-update-slice(f32[3,512,1,7,64]{1,0,4,3,2:T(4,128)} %get-tuple-element.527, f32[1,512,1,7,64]{1,0,4,3,2:T(1,128)S(1)} %copy.87, s32[]{:T(128)S(6)} %copy.111, s32[]{:T(128)} %constant.72.clone.1..sunk.1, s32[]{:T(128)} %constant.72.clone.1..sunk.1, s32[]{:T(128)} %constant.72.clone.1..sunk.1, s32[]{:T(128)} %constant.72.clone.1..sunk.1) | dynamic-update-slice | bytes 1835012 | tf_op jit(solution)/shard_map/while/body/jit(dynamic_update_index_in_dim)/dynamic_update_slice | solution.py:162
  938.6 18.1 %fusion.333 = (f32[7,512]{1,0:T(8,128)S(1)}, f32[1,7,512,1536]{3,2,1,0:T(8,128)}) fusion(f32[512,7,1536]{2,0,1:T(8,128)} %fusion.331, f32[7,512]{1,0:T(8,128)S(1)} %dynamic-slice_bitcast_fusion.2, bf16[1536,1,64]{0,2,1:T(8,128)(2,1)S(1)} %get-tuple-element.545, bf16[3,512,1,7,64]{1,4,3,2,0:T(8,128)(2,1)S(1)} %copy-done.7, s32[]{:T(128)S(6)} %copy.111, ...), kind=kOutput, calls=%fused_computation.29.clone.1 | convolution fusion | flops 737669632 | bytes 45512708 | tf_op jit(solution)/shard_map/while/body/eval_jaxpr/qkgd,skd->kgqs/dot_general | solution.py:181
  956.7 14.3 fusion.334
  971.1 9.3 fusion.336
  986.9 18.6 %dynamic_update_slice.21 = f32[3,512,1,7,64]{1,0,4,3,2:T(4,128)} dynamic-update-slice(f32[3,512,1,7,64]{1,0,4,3,2:T(4,128)} %get-tuple-element.527, f32[1,512,1,7,64]{1,0,4,3,2:T(1,128)S(1)} %copy.87, s32[]{:T(128)S(6)} %copy.111, s32[]{:T(128)} %constant.72.clone.1..sunk.1, s32[]{:T(128)} %constant.72.clone.1..sunk.1, s32[]{:T(128)} %constant.72.clone.1..sunk.1, s32[]{:T(128)} %constant.72.clone.1..sunk.1) | dynamic-update-slice | bytes 1835012 | tf_op jit(solution)/shard_map/while/body/jit(dynamic_update_index_in_dim)/dynamic_update_slice | solution.py:162
  1019.3 18.1 %fusion.333 = (f32[7,512]{1,0:T(8,128)S(1)}, f32[1,7,512,1536]{3,2,1,0:T(8,128)}) fusion(f32[512,7,1536]{2,0,1:T(8,128)} %fusion.331, f32[7,512]{1,0:T(8,128)S(1)} %dynamic-slice_bitcast_fusion.2, bf16[1536,1,64]{0,2,1:T(8,128)(2,1)S(1)} %get-tuple-element.545, bf16[3,512,1,7,64]{1,4,3,2,0:T(8,128)(2,1)S(1)} %copy-done.7, s32[]{:T(128)S(6)} %copy.111, ...), kind=kOutput, calls=%fused_computation.29.clone.1 | convolution fusion | flops 737669632 | bytes 45512708 | tf_op jit(solution)/shard_map/while/body/eval_jaxpr/qkgd,skd->kgqs/dot_general | solution.py:181
  1037.4 14.3 fusion.334
  1051.7 9.3 fusion.336
  1067.5 18.6 %dynamic_update_slice.21 = f32[3,512,1,7,64]{1,0,4,3,2:T(4,128)} dynamic-update-slice(f32[3,512,1,7,64]{1,0,4,3,2:T(4,128)} %get-tuple-element.527, f32[1,512,1,7,64]{1,0,4,3,2:T(1,128)S(1)} %copy.87, s32[]{:T(128)S(6)} %copy.111, s32[]{:T(128)} %constant.72.clone.1..sunk.1, s32[]{:T(128)} %constant.72.clone.1..sunk.1, s32[]{:T(128)} %constant.72.clone.1..sunk.1, s32[]{:T(128)} %constant.72.clone.1..sunk.1) | dynamic-update-slice | bytes 1835012 | tf_op jit(solution)/shard_map/while/body/jit(dynamic_update_index_in_dim)/dynamic_update_slice | solution.py:162
  1136.1 10.0 scatter_custom_fusion
  1159.6 51.8 %all-reduce.15.cloned.1.call-done = (bf16[1536,128]{1,0:T(8,128)(2,1)}, bf16[1536,128]{1,0:T(8,128)(2,1)}, bf16[1536,896]{1,0:T(8,128)(2,1)}, bf16[1536,128]{1,0:T(8,128)(2,1)}) async-done(((bf16[1536,128]{1,0:T(8,128)(2,1)}, bf16[1536,128]{1,0:T(8,128)(2,1)}, bf16[1536,896]{1,0:T(8,128)(2,1)}, bf16[1536,128]{1,0:T(8,128)(2,1)}), (bf16[1536,128]{1,0:T(8,128)(2,1)}, bf16[1536,128]{1,0:T(8,128)(2,1)}, ...) | async-done | bytes 3932176 | tf_op jit(solution)/shard_map/psum | solution.py:409
  1220.8 14.0 scatter_custom_fusion.1
  1265.4 265.1 %fusion.4 = f32[720,128]{1,0:T(8,128)S(1)} fusion(f32[22912,128]{1,0:T(8,128)} %constant_dynamic-update-slice_fusion), kind=kCustom, calls=%all-reduce-scatter | all-reduce-scatter fusion | flops 2949121 | bytes 12099584
  (486 shorter events, 420.3 us)
Async XLA Ops:
  7.2 242.1 %copy-start = (bf16[448,896]{1,0:T(8,128)(2,1)S(1)}, bf16[448,896]{1,0:T(8,128)(2,1)}, u32[]{:S(2)}) copy-start(bf16[448,896]{1,0:T(8,128)(2,1)} %param.35) | copy-start | bytes 2408452
  7.2 121.1 %all-gather.3.cloned.1.call-start = ((), (), s32[]{:S(2)}) async-start(), calls=%async_computation.5 | async-start | bytes 6082560 | tf_op jit(solution)/shard_map/all_gather | solution.py:248
  9.0 71.9 %all-to-all-start = ((bf16[16,96,896]{2,1,0:T(8,128)(2,1)}), bf16[16,96,896]{2,1,0:T(8,128)(2,1)S(1)}, u32[]{:S(2)}, u32[]{:S(2)}) async-start(bf16[16,96,896]{2,1,0:T(8,128)(2,1)} %bitcast.373), calls=%async_computation | async-start | bytes 5505024 | tf_op jit(solution)/shard_map/all_to_all | solution.py:245
  80.9 172.9 %all-to-all-start.2 = ((bf16[16,96,896]{2,1,0:T(8,128)(2,1)}), bf16[16,96,896]{2,1,0:T(8,128)(2,1)}, u32[]{:S(2)}, u32[]{:S(2)}) async-start(bf16[16,96,896]{2,1,0:T(8,128)(2,1)} %bitcast.374), calls=%async_computation.2 | async-start | bytes 5505024 | tf_op jit(solution)/shard_map/all_to_all | solution.py:246
  95.4 313.5 %all-reduce.11.cloned.1.call-start = ((), (), s32[]{:S(2)}) async-start(), calls=%async_computation.4 | async-start | bytes 11010048 | tf_op jit(solution)/shard_map/psum | solution.py:325
  107.0 66.3 %copy-start.5 = (bf16[1536,896]{1,0:T(8,128)(2,1)}, bf16[1536,896]{1,0:T(8,128)(2,1)S(1)}, u32[]{:S(2)}) copy-start(bf16[1536,896]{1,0:T(8,128)(2,1)S(1)} %fusion.59) | copy-start | bytes 8257540
  253.7 571.8 %all-reduce.13.cloned.1.call-start = ((), (), s32[]{:S(2)}) async-start(), calls=%async_computation.6 | async-start | bytes 22020096 | tf_op jit(solution)/shard_map/psum | solution.py:338
  262.7 15.6 %copy-start.8 = (bf16[1536,896]{1,0:T(8,128)(2,1)}, bf16[1536,896]{1,0:T(8,128)(2,1)S(1)}, u32[]{:S(2)}) copy-start(bf16[1536,896]{1,0:T(8,128)(2,1)S(1)} %gather_fusion.1) | copy-start | bytes 8257540
  262.7 14.1 copy-start.15
  262.7 14.1 copy-start.53
  262.7 15.6 %copy-start.62 = (s32[1536]{0:T(1024)S(1)}, s32[1536]{0:T(1024)}, u32[]{:S(2)}) copy-start(s32[1536]{0:T(1024)} %get-tuple-element.251) | copy-start | bytes 18436
  262.7 15.6 %copy-start.98 = (s32[128]{0:T(128)S(1)}, s32[128]{0:T(128)}, u32[]{:S(2)}) copy-start(s32[128]{0:T(128)} %and_select_fusion) | copy-start | bytes 1540
  280.9 128.0 %copy-start.3 = (bf16[1536,896]{1,0:T(8,128)(2,1)S(1)}, bf16[1536,896]{1,0:T(8,128)(2,1)}, u32[]{:S(2)}) copy-start(bf16[1536,896]{1,0:T(8,128)(2,1)} %gather_fusion) | copy-start | bytes 8257540
  413.2 419.3 %copy-start.87 = (f32[1536]{0:T(1024)}, f32[1536]{0:T(1024)S(1)}, u32[]{:S(2)}) copy-start(f32[1536]{0:T(1024)S(1)} %add_rsqrt_fusion) | copy-start | bytes 18436
  413.9 16.8 %copy-start.33 = (bf16[1536,896]{1,0:T(8,128)(2,1)}, bf16[1536,896]{1,0:T(8,128)(2,1)S(1)}, u32[]{:S(2)}) copy-start(bf16[1536,896]{1,0:T(8,128)(2,1)S(1)} %multiply_convert_fusion.3) | copy-start | bytes 8257540
  417.1 22.2 %copy-start.26 = (bf16[1536,128]{1,0:T(8,128)(2,1)}, bf16[1536,128]{1,0:T(8,128)(2,1)S(1)}, u32[]{:S(2)}) copy-start(bf16[1536,128]{1,0:T(8,128)(2,1)S(1)} %fusion.82) | copy-start | bytes 1179652
  417.1 13.6 slice-start.12
  419.6 32.5 %copy-start.24 = (bf16[1536,128]{1,0:T(8,128)(2,1)}, bf16[1536,128]{1,0:T(8,128)(2,1)S(1)}, u32[]{:S(2)}) copy-start(bf16[1536,128]{1,0:T(8,128)(2,1)S(1)} %fusion.81) | copy-start | bytes 1179652
  482.4 13.4 copy-start.19
  482.4 25.5 %slice-start.6 = ((s8[7471104]{0:T(1024)(128)(4,1)}), s8[4194304]{0:T(1024)(128)(4,1)S(1)}, s32[]{:S(2)}) async-start(s8[7471104]{0:T(1024)(128)(4,1)} %bitcast.365), calls=%async_computation.14 | async-start | bytes 8388608
  482.4 25.5 %slice-start.16 = ((s8[4358144]{0:T(1024)(128)(4,1)}), s8[4194304]{0:T(1024)(128)(4,1)S(1)}, s32[]{:S(2)}) async-start(s8[4358144]{0:T(1024)(128)(4,1)} %bitcast.381), calls=%async_computation.24 | async-start | bytes 8388608
  519.7 691.7 %all-reduce.15.cloned.1.call-start = ((), (), s32[]{:S(2)}) async-start(), calls=%async_computation.7 | async-start | bytes 7864320 | tf_op jit(solution)/shard_map/psum | solution.py:409
  537.3 288.1 %copy-start.95 = (f32[896]{0:T(1024)S(1)}, f32[896]{0:T(1024)}, u32[]{:S(2)}) copy-start(f32[896]{0:T(1024)} %get-tuple-element.248) | copy-start | bytes 10756
  647.0 178.4 %copy-start.75 = (bf16[1536,128]{1,0:T(8,128)(2,1)S(1)}, bf16[1536,128]{1,0:T(8,128)(2,1)}, u32[]{:S(2)}) copy-start(bf16[1536,128]{1,0:T(8,128)(2,1)} %get-tuple-element.293) | copy-start | bytes 1179652
  647.0 185.5 %slice-start = ((s8[5505024]{0:T(1024)(128)(4,1)}), s8[1310720]{0:T(1024)(128)(4,1)S(1)}, s32[]{:S(2)}) async-start(s8[5505024]{0:T(1024)(128)(4,1)} %bitcast.350), calls=%async_computation.8 | async-start | bytes 2621440
  1136.1 16.3 %copy-start.41 = (bf16[1536,128]{1,0:T(8,128)(2,1)S(1)}, bf16[1536,128]{1,0:T(8,128)(2,1)}, u32[]{:S(2)}) copy-start(bf16[1536,128]{1,0:T(8,128)(2,1)} %copy-done.40) | copy-start | bytes 1179652
  1136.1 16.5 %copy-start.39 = (bf16[1536,128]{1,0:T(8,128)(2,1)S(1)}, bf16[1536,128]{1,0:T(8,128)(2,1)}, u32[]{:S(2)}) copy-start(bf16[1536,128]{1,0:T(8,128)(2,1)} %fusion.80) | copy-start | bytes 1179652
  1136.1 16.7 %copy-start.107 = (pred[128]{0:T(512)(128)(4,1)S(1)}, pred[128]{0:T(512)(128)(4,1)}, u32[]{:S(2)}) copy-start(pred[128]{0:T(512)(128)(4,1)} %broadcast_in_dim.325) | copy-start | bytes 388
  1146.1 108.9 %all-to-all-start.1 = ((bf16[16,96,896]{2,1,0:T(8,128)(2,1)}), bf16[16,96,896]{2,1,0:T(8,128)(2,1)}, u32[]{:S(2)}, u32[]{:S(2)}) async-start(bf16[16,96,896]{2,1,0:T(8,128)(2,1)} %bitcast.360), calls=%async_computation.1 | async-start | bytes 5505024 | tf_op jit(solution)/shard_map/all_to_all | solution.py:464
  1220.8 17.1 %copy-start.72 = (bf16[1536,128]{1,0:T(8,128)(2,1)S(1)}, bf16[1536,128]{1,0:T(8,128)(2,1)}, u32[]{:S(2)}) copy-start(bf16[1536,128]{1,0:T(8,128)(2,1)} %get-tuple-element.297) | copy-start | bytes 1179652
  1255.0 287.3 %all-to-all-start.3 = ((bf16[16,96,896]{2,1,0:T(8,128)(2,1)}), bf16[16,96,896]{2,1,0:T(8,128)(2,1)S(1)}, u32[]{:S(2)}, u32[]{:S(2)}) async-start(bf16[16,96,896]{2,1,0:T(8,128)(2,1)} %bitcast.362), calls=%async_computation.3 | async-start | bytes 5505024 | tf_op jit(solution)/shard_map/all_to_all | solution.py:465
  1530.6 5.7 collective-permute-start
  (114 other events, 627.3 us)
Sparse Core Ops, SparseCore 0:
  11.5 116.7 all-gather.2
  253.8 155.0 all-reduce.10
  519.8 305.5 all-reduce.12
  1107.9 103.4 all-reduce.14
where the time goes:
time: 1580 us; the launch traced here: 1550 us
  blocking collectives  417 us (26%)
  matrix products  390 us (25%)
  waiting for transfers between devices  373 us (24%)
  local copies, waits for them, and re-layouts  171 us (11%)
  other arithmetic  136 us (9%)
  starting transfers between devices  38.5 us (2%)
    unnamed x1, blocking collectives  265 us
    psum x1, waiting for transfers between devices, per_device(): down_sum, rank_down_sum = lax.psum((down_part, rank_down_part), 'tensor')  174 us
    dot_general x21, matrix products, dot_last(): lax.dot_general(left, right, (((1,), (1,)), ((), ())), preferred_element_...  121 us
    psum x1, blocking collectives, per_device(): down_sum, rank_down_sum = lax.psum((down_part, rank_down_part), 'tensor')  110 us
    psum x1, waiting for transfers between devices, per_device(): branch_sum, rank_out_sum = lax.psum((branch_part, rank_out_part), 'tensor')  81.8 us
    dot_general x21, matrix products, dot_plain(): return jnp.dot(left, right, preferred_element_type=jnp.float32)  77.6 us
    dot_general x6, matrix products, one_block(): jnp.einsum('qkgd,skd->kgqs', query_block, key_vectors, preferred_element_...  69.1 us
    dynamic_update_slice x6, local copies, waits for them, and re-layouts, attend_forward(): results, log_totals = lax.map(one_block, (query_blocks, starts))  58.5 us
  transfers between devices with their start and end apart: 9, of which 6 were waited for; matrix products, arithmetic and copies ran while one was open for 36% of the time, Pallas kernels for 0%

commit v1 on v0

v1 whole, which is shorter than its diff:
```python
import functools

import jax
import jax.numpy as jnp
from jax import lax
from jax.experimental import pallas as pl
from jax.experimental.pallas import tpu as pltpu
from jax.sharding import PartitionSpec as P

HEAD = 64
RANK = 16
STEP = 3

ADAPTER_SCALE = 2.0
NORM_EPS = 1e-06
ROPE_BASE = 1000000.0
BETA_ONE = 0.5
BETA_TWO = 0.6
LEARN_RATE = 0.04
WEIGHT_DECAY = 0.01
ADAM_EPS = 1e-08
MASKED_SCORE = -1e30

LANES = 128
ROW_TILE = 256
QUERY_TILE = 128
KEY_TILE = 256
HIDDEN_TILE = 512

F32 = jnp.float32
BF16 = jnp.bfloat16
I32 = jnp.int32


def nn(left, right):
    return lax.dot_general(left, right, (((1,), (0,)), ((), ())), preferred_element_type=F32)


def nt(left, right):
    return lax.dot_general(left, right, (((1,), (1,)), ((), ())), preferred_element_type=F32)


def tn(left, right):
    return lax.dot_general(left, right, (((0,), (0,)), ((), ())), preferred_element_type=F32)


def lane_iota(shape):
    return lax.broadcasted_iota(I32, shape, 1)


def row_iota(shape):
    return lax.broadcasted_iota(I32, shape, 0)


def whole(array):
    return pl.BlockSpec(array.shape, lambda *_: (0,) * array.ndim)


def row_blocks(array, tile):
    return pl.BlockSpec((tile, array.shape[1]), lambda i, *_: (i, 0))


def rank_mask(adapter_col, width):
    return jnp.where(lane_iota((adapter_col.shape[0], width)) // RANK == adapter_col, 1.0, 0.0)


def turn(values):
    lanes = lane_iota(values.shape) % HEAD
    return jnp.where(
        lanes < HEAD // 2,
        -pltpu.roll(values, LANES - HEAD // 2, 1),
        pltpu.roll(values, HEAD // 2, 1),
    )


def rms(values):
    return lax.rsqrt(jnp.mean(values * values, axis=-1, keepdims=True) + NORM_EPS)


def norm_back(values, gain, grad):
    inverse = rms(values)
    weighted = grad * gain
    return inverse * weighted - values * inverse * inverse * inverse * jnp.mean(
        weighted * values, axis=-1, keepdims=True
    )


def pick_rows(place_col, slots):
    hit = place_col == lane_iota((place_col.shape[0], slots))
    return jnp.where(hit, 1.0, 0.0).astype(BF16)


def place_rows(place_row, slots):
    hit = row_iota((slots, place_row.shape[1])) == place_row
    return jnp.where(hit, 1.0, 0.0).astype(BF16)


def params(**more):
    return pltpu.CompilerParams(vmem_limit_bytes=60 * 1024 * 1024, **more)


def cost(flops, moved):
    return pl.CostEstimate(flops=int(flops), bytes_accessed=int(moved), transcendentals=0)


def project_kernel(
    x_ref, meta_ref, cos_ref, sin_ref, gain_ref, w_ref, bias_ref, bq_ref, bk_ref, bv_ref,
    xs_ref, n_ref, q_ref, kv_ref, z_ref,
):
    rows = meta_ref.shape[0]
    qw, kw = bq_ref.shape[0], bk_ref.shape[0]
    rank = bq_ref.shape[1]
    values = nn(pick_rows(meta_ref[:, 0:1], x_ref.shape[0]), x_ref[...])
    xs_ref[...] = values.astype(BF16)
    normed = (values * rms(values) * gain_ref[...]).astype(BF16)
    n_ref[...] = normed
    base = nn(normed, w_ref[...])
    mask = rank_mask(meta_ref[:, 1:2], rank)
    low = qw + 2 * kw
    lows = [(base[:, low + i * rank : low + (i + 1) * rank] * mask).astype(BF16) for i in range(3)]
    for i in range(3):
        z_ref[:, i * rank : (i + 1) * rank] = lows[i]
    cos, sin = cos_ref[...], sin_ref[...]
    queries = base[:, :qw] + bias_ref[:, :qw] + ADAPTER_SCALE * nt(lows[0], bq_ref[...])
    for pair in range(qw // LANES):
        part = queries[:, pair * LANES : (pair + 1) * LANES]
        turned = (part * cos + turn(part) * sin) * HEAD**-0.5
        q_ref[:, pair * LANES : (pair + 1) * LANES] = turned.astype(BF16)
    keys = base[:, qw : qw + kw] + bias_ref[:, qw : qw + kw] + ADAPTER_SCALE * nt(lows[1], bk_ref[...])
    kv_ref[:, :kw] = (keys * cos + turn(keys) * sin).astype(BF16)
    vals = (
        base[:, qw + kw : low]
        + bias_ref[:, qw + kw : low]
        + ADAPTER_SCALE * nt(lows[2], bv_ref[...])
    )
    kv_ref[:, kw:] = vals.astype(BF16)


def project(x, meta, cos, sin, gain, w_cat, bias, b_q, b_k, b_v):
    rows, width = x.shape
    qw, kw, rank = b_q.shape[0], b_k.shape[0], b_q.shape[1]
    tile = ROW_TILE
    args = (x, meta, cos, sin, gain, w_cat, bias, b_q, b_k, b_v)
    specs = [whole(x), row_blocks(meta, tile), row_blocks(cos, tile), row_blocks(sin, tile)]
    specs += [whole(a) for a in args[4:]]
    outs = [
        jax.ShapeDtypeStruct((rows, width), BF16),
        jax.ShapeDtypeStruct((rows, width), BF16),
        jax.ShapeDtypeStruct((rows, qw), BF16),
        jax.ShapeDtypeStruct((rows, 2 * kw), BF16),
        jax.ShapeDtypeStruct((rows, 3 * rank), BF16),
    ]
    return pl.pallas_call(
        project_kernel,
        grid=(rows // tile,),
        in_specs=specs,
        out_specs=[row_blocks(o, tile) for o in outs],
        out_shape=outs,
        compiler_params=params(),
        cost_estimate=cost(2 * rows * width * (w_cat.shape[1] + rows), 9e6),
        name="project",
    )(*args)


def cotangent_kernel(g_ref, meta_ref, bd_ref, out_ref):
    width = g_ref.shape[1]
    rank = bd_ref.shape[1]
    grad = nn(pick_rows(meta_ref[:, 0:1], g_ref.shape[0]), g_ref[...]).astype(BF16)
    back = ADAPTER_SCALE * nn(grad, bd_ref[...]) * rank_mask(meta_ref[:, 1:2], rank)
    out_ref[:, :width] = grad
    out_ref[:, width:] = back.astype(BF16)


def sort_cotangent(grad, meta, b_down):
    rows, width = grad.shape
    tile = ROW_TILE
    out = jax.ShapeDtypeStruct((rows, width + b_down.shape[1]), BF16)
    return pl.pallas_call(
        cotangent_kernel,
        grid=(rows // tile,),
        in_specs=[whole(grad), row_blocks(meta, tile), whole(b_down)],
        out_specs=row_blocks(out, tile),
        out_shape=out,
        compiler_params=params(),
        cost_estimate=cost(2 * rows * width * (rows + 128), 4e6),
        name="cotangent",
    )(grad, meta, b_down)


def head_groups(heads, kv_heads):
    width = heads // kv_heads
    groups = {}
    for head in range(heads):
        groups.setdefault((head // width, head % 2), []).append(head)
    return [(kv, half, members) for (kv, half), members in sorted(groups.items())]


def spread_heads(tile_f32, kv, half):
    lanes = lane_iota(tile_f32.shape)
    moved = tile_f32 if kv % 2 == half else pltpu.roll(tile_f32, HEAD, 1)
    keep = (lanes >= HEAD) if half else (lanes < HEAD)
    return jnp.where(keep, moved, 0.0).astype(BF16)


def fill_heads(groups, source, keys_ref, values_ref):
    total = keys_ref.shape[1]
    for start in range(0, total, KEY_TILE):
        part = source(start).astype(F32)
        for number, (kv, half, _) in enumerate(groups):
            keys_ref[number, start : start + KEY_TILE, :] = spread_heads(part[:, :LANES], kv, half)
            values_ref[number, start : start + KEY_TILE, :] = spread_heads(
                part[:, LANES:], kv, half
            )


def attend_kernel(
    heads, kv_heads, bounds_ref, q_ref, meta_ref, own_ref, other_ref, column_ref,
    o_ref, log_ref, merged_ref, keys, values, acc, top, total,
):
    step = pl.program_id(0)
    groups = head_groups(heads, kv_heads)
    rows = q_ref.shape[0]

    @pl.when(step == 0)
    def _():
        both = jnp.concatenate([own_ref[...], other_ref[...]], axis=0)

        def merged(start):
            picks = pick_rows(column_ref[start : start + KEY_TILE, :], both.shape[0])
            part = nn(picks, both)
            merged_ref[start : start + KEY_TILE, :] = part.astype(BF16)
            return part

        fill_heads(groups, merged, keys, values)

    acc[...] = jnp.zeros_like(acc)
    total[...] = jnp.zeros_like(total)
    top[...] = jnp.full_like(top, MASKED_SCORE)
    first, last = meta_ref[:, 2:3], meta_ref[:, 3:4]
    offsets = []
    cursor = 0
    for _, _, members in groups:
        offsets.append(cursor)
        cursor += len(members) * rows

    def one_tile(number, carry):
        start = pl.multiple_of(number * KEY_TILE, KEY_TILE)
        index = start + lane_iota((rows, KEY_TILE))
        bias = jnp.where((index >= first) & (index <= last), 0.0, MASKED_SCORE)
        for group, (_, _, members) in enumerate(groups):
            count = len(members)
            span = pl.ds(offsets[group], count * rows)
            stack = jnp.concatenate(
                [q_ref[:, (h // 2) * LANES : (h // 2 + 1) * LANES] for h in members], axis=0
            )
            scores = nt(stack, keys[group, pl.ds(start, KEY_TILE), :])
            scores = scores + jnp.concatenate([bias] * count, axis=0)
            old = top[span, :]
            new = jnp.maximum(old, jnp.max(scores, axis=1, keepdims=True))
            weights = jnp.exp(scores - new)
            shrink = jnp.exp(old - new)
            total[span, :] = total[span, :] * shrink + jnp.sum(weights, axis=1, keepdims=True)
            acc[span, :] = acc[span, :] * shrink + nn(
                weights.astype(BF16), values[group, pl.ds(start, KEY_TILE), :]
            )
            top[span, :] = new
        return carry

    lax.fori_loop(bounds_ref[0, step], bounds_ref[1, step], one_tile, 0)
    pairs = [None] * (heads // 2)
    logs = jnp.zeros((rows, LANES), F32)
    lanes = lane_iota((rows, LANES))
    for group, (_, _, members) in enumerate(groups):
        for at, head in enumerate(members):
            span = pl.ds(offsets[group] + at * rows, rows)
            sums = total[span, :]
            part = acc[span, :] / sums
            logs = jnp.where(lanes == head, top[span, :] + jnp.log(sums), logs)
            pair = head // 2
            pairs[pair] = part if pairs[pair] is None else pairs[pair] + part
    for pair, part in enumerate(pairs):
        o_ref[:, pair * LANES : (pair + 1) * LANES] = part.astype(BF16)
    log_ref[...] = jnp.transpose(logs)[: log_ref.shape[0], :]


def attend(bounds, q, meta, own_kv, other_kv, column, heads, kv_heads):
    rows, qw = q.shape
    tile = QUERY_TILE
    keys = 2 * rows
    groups = len(head_groups(heads, kv_heads))
    outs = [
        jax.ShapeDtypeStruct((rows, qw), BF16),
        jax.ShapeDtypeStruct((16, rows), F32),
        jax.ShapeDtypeStruct((keys, own_kv.shape[1]), BF16),
    ]
    return pl.pallas_call(
        functools.partial(attend_kernel, heads, kv_heads),
        grid_spec=pltpu.PrefetchScalarGridSpec(
            num_scalar_prefetch=1,
            grid=(rows // tile,),
            in_specs=[
                row_blocks(q, tile),
                row_blocks(meta, tile),
                whole(own_kv),
                whole(other_kv),
                whole(column),
            ],
            out_specs=[
                row_blocks(outs[0], tile),
                pl.BlockSpec((16, tile), lambda i, *_: (0, i)),
                whole(outs[2]),
            ],
            scratch_shapes=[
                pltpu.VMEM((groups, keys, LANES), BF16),
                pltpu.VMEM((groups, keys, LANES), BF16),
                pltpu.VMEM((heads * tile, LANES), F32),
                pltpu.VMEM((heads * tile, 1), F32),
                pltpu.VMEM((heads * tile, 1), F32),
            ],
        ),
        out_shape=outs,
        compiler_params=params(),
        cost_estimate=cost(heads * rows * keys * 256, 6e6),
        name="attend",
    )(bounds, q, meta, own_kv, other_kv, column)


def attend_back_kernel(
    heads, kv_heads, bounds_ref, q_ref, g_ref, o_ref, log_ref, metar_ref, cos_ref, sin_ref,
    merged_ref, column_ref,
    gq_ref, own_ref, other_ref, keys, values, dkeys, dvalues, dq, dots,
):
    step = pl.program_id(0)
    groups = head_groups(heads, kv_heads)
    rows = q_ref.shape[0]

    @pl.when(step == 0)
    def _():
        fill_heads(groups, lambda at: merged_ref[at : at + KEY_TILE, :], keys, values)
        dkeys[...] = jnp.zeros_like(dkeys)
        dvalues[...] = jnp.zeros_like(dvalues)

    dq[...] = jnp.zeros_like(dq)
    for pair in range(heads // 2):
        lanes = slice(pair * LANES, (pair + 1) * LANES)
        product = jnp.transpose(g_ref[:, lanes].astype(F32) * o_ref[:, lanes].astype(F32))
        dots[2 * pair : 2 * pair + 1, :] = jnp.sum(product[:HEAD], axis=0, keepdims=True)
        dots[2 * pair + 1 : 2 * pair + 2, :] = jnp.sum(product[HEAD:], axis=0, keepdims=True)
    first, last = metar_ref[2:3, :], metar_ref[3:4, :]

    def one_tile(number, carry):
        start = pl.multiple_of(number * KEY_TILE, KEY_TILE)
        index = start + row_iota((KEY_TILE, rows))
        bias = jnp.where((index >= first) & (index <= last), 0.0, MASKED_SCORE)
        for group, (_, half, members) in enumerate(groups):
            count = len(members)
            span = pl.ds(start, KEY_TILE)
            cut = [slice((h // 2) * LANES, (h // 2 + 1) * LANES) for h in members]
            stack = jnp.concatenate([q_ref[:, c] for c in cut], axis=0)
            grads = jnp.concatenate([g_ref[:, c] for c in cut], axis=0)
            logs = jnp.concatenate([log_ref[h : h + 1, :] for h in members], axis=1)
            drop = jnp.concatenate([dots[h : h + 1, :] for h in members], axis=1)
            key_part = keys[group, span, :]
            scores = nt(key_part, stack) + jnp.concatenate([bias] * count, axis=1)
            weights = jnp.exp(scores - logs)
            change = nt(values[group, span, :], grads)
            dscores = (weights * (change - drop)).astype(BF16)
            dvalues[group, span, :] += nn(weights.astype(BF16), grads)
            dkeys[group, span, :] += nn(dscores, stack)
            back = tn(dscores, key_part)
            for at, head in enumerate(members):
                dq[head // 2, :, :] += back[at * rows : (at + 1) * rows, :]
        return carry

    lax.fori_loop(bounds_ref[0, step], bounds_ref[1, step], one_tile, 0)
    cos, sin = cos_ref[...], sin_ref[...]
    for pair in range(heads // 2):
        grad = dq[pair, :, :] * HEAD**-0.5
        grad = grad * cos - turn(grad) * sin
        gq_ref[:, pair * LANES : (pair + 1) * LANES] = grad.astype(BF16)

    @pl.when(step == pl.num_programs(0) - 1)
    def _():
        total = dkeys.shape[1]

        def join(ref):
            out = None
            for group, (kv, half, _) in enumerate(groups):
                part = ref[group, :, :]
                lanes = lane_iota(part.shape)
                part = jnp.where((lanes >= HEAD) if half else (lanes < HEAD), part, 0.0)
                if kv % 2 != half:
                    part = pltpu.roll(part, HEAD, 1)
                out = part if out is None else out + part
            return out.astype(BF16)

        both = jnp.concatenate([join(dkeys), join(dvalues)], axis=1)
        half_rows = own_ref.shape[0]
        for at in range(0, total, KEY_TILE):
            hit = (at + row_iota((KEY_TILE, total))) == column_ref[...]
            part = nn(jnp.where(hit, 1.0, 0.0).astype(BF16), both).astype(BF16)
            if at < half_rows:
                own_ref[at : at + KEY_TILE, :] = part
            else:
                other_ref[at - half_rows : at - half_rows + KEY_TILE, :] = part


def attend_back(bounds, q, grad, o, logs, meta_rows, cos, sin, merged, column_row, heads, kv_heads):
    rows, qw = q.shape
    tile = QUERY_TILE
    keys, kvw = merged.shape
    groups = len(head_groups(heads, kv_heads))
    outs = [
        jax.ShapeDtypeStruct((rows, qw), BF16),
        jax.ShapeDtypeStruct((rows, kvw), BF16),
        jax.ShapeDtypeStruct((rows, kvw), BF16),
    ]
    return pl.pallas_call(
        functools.partial(attend_back_kernel, heads, kv_heads),
        grid_spec=pltpu.PrefetchScalarGridSpec(
            num_scalar_prefetch=1,
            grid=(rows // tile,),
            in_specs=[
                row_blocks(q, tile),
                row_blocks(grad, tile),
                row_blocks(o, tile),
                pl.BlockSpec((16, tile), lambda i, *_: (0, i)),
                pl.BlockSpec((8, tile), lambda i, *_: (0, i)),
                row_blocks(cos, tile),
                row_blocks(sin, tile),
                whole(merged),
                whole(column_row),
            ],
            out_specs=[row_blocks(outs[0], tile), whole(outs[1]), whole(outs[2])],
            scratch_shapes=[
                pltpu.VMEM((groups, keys, LANES), BF16),
                pltpu.VMEM((groups, keys, LANES), BF16),
                pltpu.VMEM((groups, keys, LANES), F32),
                pltpu.VMEM((groups, keys, LANES), F32),
                pltpu.VMEM((heads // 2, tile, LANES), F32),
                pltpu.VMEM((16, tile), F32),
            ],
        ),
        out_shape=outs,
        compiler_params=params(),
        cost_estimate=cost(heads * rows * keys * 640, 9e6),
        name="attend_back",
    )(bounds, q, grad, o, logs, meta_rows, cos, sin, merged, column_row)


def middle_kernel(o_ref, x_ref, meta_ref, w_ref, b_ref, gain_ref, a_ref, y_ref, xg_ref, xu_ref, z_ref):
    width = x_ref.shape[1]
    rank = b_ref.shape[1]
    mask = rank_mask(meta_ref[:, 1:2], rank)
    base = nn(o_ref[...], w_ref[...])
    low = (base[:, width:] * mask).astype(BF16)
    z_ref[...] = low
    values = x_ref[...].astype(F32) + (base[:, :width] + ADAPTER_SCALE * nt(low, b_ref[...]))
    y_ref[...] = values
    normed = (values * rms(values) * gain_ref[...]).astype(BF16)
    lows = nn(normed, a_ref[...])
    xg_ref[:, :width] = normed
    xu_ref[:, :width] = normed
    xg_ref[:, width:] = (lows[:, :rank] * mask).astype(BF16)
    xu_ref[:, width:] = (lows[:, rank:] * mask).astype(BF16)


def middle(o, x, meta, w_out, b_out, gain, a_pair):
    rows, width = x.shape
    rank = b_out.shape[1]
    tile = ROW_TILE
    outs = [
        jax.ShapeDtypeStruct((rows, width), F32),
        jax.ShapeDtypeStruct((rows, width + rank), BF16),
        jax.ShapeDtypeStruct((rows, width + rank), BF16),
        jax.ShapeDtypeStruct((rows, rank), BF16),
    ]
    return pl.pallas_call(
        middle_kernel,
        grid=(rows // tile,),
        in_specs=[row_blocks(a, tile) for a in (o, x, meta)]
        + [whole(a) for a in (w_out, b_out, gain, a_pair)],
        out_specs=[row_blocks(a, tile) for a in outs],
        out_shape=outs,
        compiler_params=params(),
        cost_estimate=cost(2 * rows * width * 1400, 12e6),
        name="middle",
    )(o, x, meta, w_out, b_out, gain, a_pair)


def finish_kernel(ya_ref, yb_ref, y1_ref, dy_ref, meta_ref, metar_ref, b_ref, out_ref, gb_ref, acc, gacc):
    step = pl.program_id(0)
    width = y1_ref.shape[1]
    rank = b_ref.shape[1]

    @pl.when(step == 0)
    def _():
        acc[...] = jnp.zeros_like(acc)
        gacc[...] = jnp.zeros_like(gacc)

    mask = rank_mask(meta_ref[:, 1:2], rank)
    low = ((ya_ref[:, width:] + yb_ref[:, width:]) * mask).astype(BF16)
    values = y1_ref[...] + (
        (ya_ref[:, :width] + yb_ref[:, :width]) + ADAPTER_SCALE * nt(low, b_ref[...])
    )
    acc[...] += nn(place_rows(metar_ref[0:1, :], acc.shape[0]), values.astype(BF16))
    gacc[...] += ADAPTER_SCALE * tn(dy_ref[:, :width], low)

    @pl.when(step == pl.num_programs(0) - 1)
    def _():
        out_ref[...] = acc[...].astype(BF16)
        gb_ref[...] = gacc[...].astype(gb_ref.dtype)


def finish(y_first, y_second, y1, dy, meta, meta_rows, b_down):
    rows, width = y1.shape
    rank = b_down.shape[1]
    tile = ROW_TILE
    outs = [
        jax.ShapeDtypeStruct((rows, width), BF16),
        jax.ShapeDtypeStruct((width, rank), BF16),
    ]
    return pl.pallas_call(
        finish_kernel,
        grid=(rows // tile,),
        in_specs=[row_blocks(a, tile) for a in (y_first, y_second, y1, dy, meta)]
        + [pl.BlockSpec((8, tile), lambda i: (0, i)), whole(b_down)],
        out_specs=[whole(a) for a in outs],
        out_shape=outs,
        scratch_shapes=[pltpu.VMEM((rows, width), F32), pltpu.VMEM((width, rank), F32)],
        compiler_params=params(),
        cost_estimate=cost(2 * rows * width * (rows + 256), 13e6),
        name="finish",
    )(y_first, y_second, y1, dy, meta, meta_rows, b_down)


def middle_back_kernel(
    da_ref, db_ref, y1_ref, dy_ref, xg_ref, o_ref, z_ref, meta_ref, a_ref, b_ref, w_ref, gain_ref,
    dy1_ref, dar_ref, ga_ref, gbo_ref, gao_ref, acc_a, acc_bo, acc_ao,
):
    step = pl.program_id(0)
    width = y1_ref.shape[1]
    rank = b_ref.shape[1]

    @pl.when(step == 0)
    def _():
        acc_a[...] = jnp.zeros_like(acc_a)
        acc_bo[...] = jnp.zeros_like(acc_bo)
        acc_ao[...] = jnp.zeros_like(acc_ao)

    mask = rank_mask(meta_ref[:, 1:2], rank)
    back = (da_ref[:, width:] + db_ref[:, width:]) * jnp.concatenate([mask, mask], axis=1)
    back = back.astype(BF16)
    grad = da_ref[:, :width] + db_ref[:, :width] + nt(back, a_ref[...])
    values = y1_ref[...]
    dy1 = dy_ref[:, :width].astype(F32) + norm_back(values, gain_ref[...], grad)
    dy1_ref[...] = dy1
    low_grad = dy1.astype(BF16)
    back_out = (ADAPTER_SCALE * nn(low_grad, b_ref[...]) * mask).astype(BF16)
    both = jnp.concatenate([low_grad, back_out], axis=1)
    dar_ref[...] = nt(both, w_ref[...]).astype(BF16)
    acc_a[...] += tn(xg_ref[:, :width], back)
    acc_bo[...] += ADAPTER_SCALE * tn(low_grad, z_ref[...])
    acc_ao[...] += tn(o_ref[...], back_out)

    @pl.when(step == pl.num_programs(0) - 1)
    def _():
        ga_ref[...] = acc_a[...].astype(ga_ref.dtype)
        gbo_ref[...] = acc_bo[...].astype(gbo_ref.dtype)
        gao_ref[...] = acc_ao[...].astype(gao_ref.dtype)


def middle_back(d_first, d_second, y1, dy, xg, o, z, meta, a_pair, b_out, w_out, gain):
    rows, width = y1.shape
    rank = b_out.shape[1]
    qw = o.shape[1]
    tile = ROW_TILE
    outs = [
        jax.ShapeDtypeStruct((rows, width), F32),
        jax.ShapeDtypeStruct((rows, qw), BF16),
        jax.ShapeDtypeStruct((width, 2 * rank), BF16),
        jax.ShapeDtypeStruct((width, rank), BF16),
        jax.ShapeDtypeStruct((qw, rank), BF16),
    ]
    return pl.pallas_call(
        middle_back_kernel,
        grid=(rows // tile,),
        in_specs=[row_blocks(a, tile) for a in (d_first, d_second, y1, dy, xg, o, z, meta)]
        + [whole(a) for a in (a_pair, b_out, w_out, gain)],
        out_specs=[row_blocks(a, tile) for a in outs[:2]] + [whole(a) for a in outs[2:]],
        out_shape=outs,
        scratch_shapes=[
            pltpu.VMEM((width, 2 * rank), F32),
            pltpu.VMEM((width, rank), F32),
            pltpu.VMEM((qw, rank), F32),
        ],
        compiler_params=params(),
        cost_estimate=cost(2 * rows * width * 1900, 20e6),
        name="middle_back",
    )(d_first, d_second, y1, dy, xg, o, z, meta, a_pair, b_out, w_out, gain)


def feed_kernel(
    valid, xg_ref, xu_ref, dy_ref, wg_ref, wu_ref, wd_ref, bg_ref, bu_ref, ad_ref,
    y_ref, d_ref, gbg_ref, gbu_ref, gad_ref, wga, wua, wda,
):
    step = pl.program_id(0)
    width = wd_ref.shape[1]
    tile = wd_ref.shape[0]
    rank = ad_ref.shape[1]
    rows = xg_ref.shape[0]
    wga[:width, :] = wg_ref[...]
    wua[:width, :] = wu_ref[...]
    wga[width:, :] = jnp.transpose(bg_ref[...].astype(F32) * ADAPTER_SCALE).astype(BF16)
    wua[width:, :] = jnp.transpose(bu_ref[...].astype(F32) * ADAPTER_SCALE).astype(BF16)
    wda[:, :width] = wd_ref[...]
    wda[:, width:] = ad_ref[...]
    steps = pl.cdiv(valid, tile)
    rest = valid - (steps - 1) * tile
    if rest < tile:

        @pl.when(step == steps - 1)
        def _():
            wga[:, rest:] = jnp.zeros((width + rank, tile - rest), BF16)
            wua[:, rest:] = jnp.zeros((width + rank, tile - rest), BF16)
            wda[rest:, :] = jnp.zeros((tile - rest, width + rank), BF16)

    @pl.when(step == 0)
    def _():
        y_ref[...] = jnp.zeros_like(y_ref)
        d_ref[...] = jnp.zeros_like(d_ref)

    hids, dgs, dus = [], [], []
    for at in range(0, rows, ROW_TILE):
        span = slice(at, at + ROW_TILE)
        gate = nn(xg_ref[span, :], wga[...])
        up = nn(xu_ref[span, :], wua[...])
        dhid = nt(dy_ref[span, :], wda[...])
        sig = 1.0 / (1.0 + jnp.exp(-gate))
        silu = gate * sig
        hid = (silu * up).astype(BF16)
        dg = (dhid * up * (sig * (1.0 + gate * (1.0 - sig)))).astype(BF16)
        du = (dhid * silu).astype(BF16)
        y_ref[span, :] += nn(hid, wda[...])
        dga = nt(dg, wga[...])
        dua = nt(du, wua[...])
        d_ref[span, :width] += dga[:, :width] + dua[:, :width]
        d_ref[span, width : width + rank] += dga[:, width:]
        d_ref[span, width + rank :] += dua[:, width:]
        hids.append(hid)
        dgs.append(dg)
        dus.append(du)
    hid, dg, du = (jnp.concatenate(v, axis=0) for v in (hids, dgs, dus))
    gbg_ref[...] = (ADAPTER_SCALE * tn(dg, xg_ref[:, width:])).astype(gbg_ref.dtype)
    gbu_ref[...] = (ADAPTER_SCALE * tn(du, xu_ref[:, width:])).astype(gbu_ref.dtype)
    gad_ref[...] = tn(hid, dy_ref[:, width:]).astype(gad_ref.dtype)


def feed(xg, xu, dy, w_gate, w_up, w_down, b_gate, b_up, a_down):
    rows = xg.shape[0]
    hidden, width = w_down.shape
    rank = a_down.shape[1]
    tile = HIDDEN_TILE
    across = pl.BlockSpec((width, tile), lambda i: (0, i))
    down = pl.BlockSpec((tile, width), lambda i: (i, 0))
    thin = pl.BlockSpec((tile, rank), lambda i: (i, 0))
    outs = [
        jax.ShapeDtypeStruct((rows, width + rank), F32),
        jax.ShapeDtypeStruct((rows, width + 2 * rank), F32),
        jax.ShapeDtypeStruct((hidden, rank), BF16),
        jax.ShapeDtypeStruct((hidden, rank), BF16),
        jax.ShapeDtypeStruct((hidden, rank), BF16),
    ]
    return pl.pallas_call(
        functools.partial(feed_kernel, hidden),
        grid=(pl.cdiv(hidden, tile),),
        in_specs=[whole(xg), whole(xu), whole(dy), across, across, down, thin, thin, thin],
        out_specs=[whole(outs[0]), whole(outs[1]), thin, thin, thin],
        out_shape=outs,
        scratch_shapes=[
            pltpu.VMEM((width + rank, tile), BF16),
            pltpu.VMEM((width + rank, tile), BF16),
            pltpu.VMEM((tile, width + rank), BF16),
        ],
        compiler_params=params(),
        cost_estimate=cost(2 * rows * hidden * (6 * width + 9 * rank), 30e6),
        name="feed",
    )(xg, xu, dy, w_gate, w_up, w_down, b_gate, b_up, a_down)


def input_kernel(
    gq_ref, own_ref, got_ref, x_ref, n_ref, z_ref, dy1_ref, meta_ref, metar_ref, cos_ref, sin_ref,
    gain_ref, w_ref, bq_ref, bk_ref, bv_ref,
    out_ref, ga_ref, gb_ref, acc, acc_a, acc_b,
):
    step = pl.program_id(0)
    qw, kw, rank = bq_ref.shape[0], bk_ref.shape[0], bq_ref.shape[1]

    @pl.when(step == 0)
    def _():
        acc[...] = jnp.zeros_like(acc)
        acc_a[...] = jnp.zeros_like(acc_a)
        acc_b[...] = jnp.zeros_like(acc_b)

    mask = rank_mask(meta_ref[:, 1:2], rank)
    both = own_ref[...].astype(F32) + got_ref[...].astype(F32)
    dk = both[:, :kw]
    gq = gq_ref[...]
    gk = (dk * cos_ref[...] - turn(dk) * sin_ref[...]).astype(BF16)
    gv = both[:, kw:].astype(BF16)
    backs = [
        (ADAPTER_SCALE * nn(g, b[...]) * mask).astype(BF16)
        for g, b in ((gq, bq_ref), (gk, bk_ref), (gv, bv_ref))
    ]
    grads = jnp.concatenate([gq, gk, gv] + backs, axis=1)
    dn = nt(grads, w_ref[...])
    values = x_ref[...].astype(F32)
    dx = dy1_ref[...] + norm_back(values, gain_ref[...], dn)
    acc[...] += nn(place_rows(metar_ref[0:1, :], acc.shape[0]), dx.astype(BF16))
    acc_a[...] += tn(n_ref[...], jnp.concatenate(backs, axis=1))
    low = z_ref[...]
    acc_b[:qw, :] += tn(gq, low[:, :rank])
    acc_b[qw : qw + kw, :] += tn(gk, low[:, rank : 2 * rank])
    acc_b[qw + kw :, :] += tn(gv, low[:, 2 * rank :])

    @pl.when(step == pl.num_programs(0) - 1)
    def _():
        out_ref[...] = acc[...].astype(BF16)
        ga_ref[...] = acc_a[...].astype(ga_ref.dtype)
        gb_ref[...] = (ADAPTER_SCALE * acc_b[...]).astype(gb_ref.dtype)


def input_back(gq, own, got, x, n1, z, dy1, meta, meta_rows, cos, sin, gain, w_cat, b_q, b_k, b_v):
    rows, width = x.shape
    qw, kw, rank = b_q.shape[0], b_k.shape[0], b_q.shape[1]
    tile = ROW_TILE
    outs = [
        jax.ShapeDtypeStruct((rows, width), BF16),
        jax.ShapeDtypeStruct((width, 3 * rank), BF16),
        jax.ShapeDtypeStruct((qw + 2 * kw, rank), BF16),
    ]
    return pl.pallas_call(
        input_kernel,
        grid=(rows // tile,),
        in_specs=[row_blocks(a, tile) for a in (gq, own, got, x, n1, z, dy1, meta)]
        + [pl.BlockSpec((8, tile), lambda i: (0, i))]
        + [row_blocks(a, tile) for a in (cos, sin)]
        + [whole(a) for a in (gain, w_cat, b_q, b_k, b_v)],
        out_specs=[whole(a) for a in outs],
        out_shape=outs,
        scratch_shapes=[
            pltpu.VMEM((rows, width), F32),
            pltpu.VMEM((width, 3 * rank), F32),
            pltpu.VMEM((qw + 2 * kw, rank), F32),
        ],
        compiler_params=params(),
        cost_estimate=cost(2 * rows * width * 2900, 14e6),
        name="input_back",
    )(gq, own, got, x, n1, z, dy1, meta, meta_rows, cos, sin, gain, w_cat, b_q, b_k, b_v)


def row_tables(order_row, lengths_row, adapter_row, part, parts, each):
    total = order_row.shape[0]
    piece = each // parts
    local = total // parts
    places = jnp.arange(total, dtype=I32)
    own = (order_row % each) // piece == part
    slot = (order_row // each) * piece + order_row % piece
    upto = jnp.sum((own[None, :] & (places[None, :] <= places[:, None])).astype(I32), axis=1)
    column = jnp.where(own, upto - 1, local + places - upto)
    picks = column[None, :] == jnp.arange(local, dtype=I32)[:, None]
    balanced = jnp.sum(jnp.where(picks, places[None, :], 0), axis=1)
    slots = jnp.sum(jnp.where(picks, slot[None, :], 0), axis=1)
    ends = jnp.cumsum(lengths_row)
    starts = ends - lengths_row
    member = (balanced[:, None] >= starts[None, :]) & (balanced[:, None] < ends[None, :])
    first = jnp.sum(jnp.where(member, starts[None, :], 0), axis=1)
    chosen = jnp.sum(jnp.where(member, adapter_row[None, :], 0), axis=1)
    bounds = jnp.stack(
        [
            first[::QUERY_TILE] // KEY_TILE,
            balanced[QUERY_TILE - 1 :: QUERY_TILE] // KEY_TILE + 1,
        ]
    )
    return slots, chosen, first, balanced, column, bounds


def rope_tables(position):
    freq_index = jnp.arange(HEAD // 2, dtype=F32)
    inv_freq = jnp.power(jnp.float32(ROPE_BASE), -2.0 * freq_index / HEAD)
    angles = position.astype(F32)[:, None] * inv_freq[None, :]
    return (
        jnp.concatenate([jnp.cos(angles)] * 4, axis=1),
        jnp.concatenate([jnp.sin(angles)] * 4, axis=1),
    )


def per_device(
    tokens, cotangent, order, lengths, adapter_ids, norm_gains, w_query, w_key, w_value,
    b_query, b_key, b_value, w_out, w_gate, w_up, w_down, adapters, first_moment, second_moment,
):
    parts = lax.axis_size("tensor")
    part = lax.axis_index("tensor")
    devices = lax.axis_size("dp")
    place = lax.axis_index("dp")
    core = place % 2
    total, width = tokens.shape
    each = total // devices
    piece = each // parts
    local = total // parts
    rank = adapters.shape[1]
    swap = [(i, parts - 1 - i) for i in range(parts)]
    cores = [(i, i ^ 1) for i in range(devices)]
    first_part = part == 0

    def across(values):
        return lax.ppermute(values, "tensor", swap)

    def in_order(mine, theirs, axis):
        return jnp.concatenate(
            [jnp.where(first_part, mine, theirs), jnp.where(first_part, theirs, mine)], axis=axis
        )

    def fetch(values):
        rows = values.shape[0] // 2
        got = across(lax.dynamic_slice_in_dim(values, core * rows, rows, 0))
        more = lax.ppermute(got, "dp", cores)
        return jnp.concatenate(
            [jnp.where(core == 0, got, more), jnp.where(core == 0, more, got)], axis=0
        )

    def receive(values):
        sent = values.reshape(devices, parts, piece, width)
        sent = lax.dynamic_index_in_dim(sent, part, 1, keepdims=False)
        got = lax.all_to_all(sent, "dp", split_axis=0, concat_axis=0, tiled=True)
        return got.reshape(local, width)

    def give_back(values):
        got = lax.all_to_all(
            values.reshape(devices, piece, width), "dp", split_axis=0, concat_axis=0, tiled=True
        )
        theirs = across(got)
        return in_order(got[:, None], theirs[:, None], 1).reshape(total, width)

    moved = receive(tokens)
    moved_back = receive(cotangent)
    small = in_order(
        jnp.concatenate([w_query, w_key, w_value], axis=1)[None],
        across(jnp.concatenate([w_query, w_key, w_value], axis=1))[None],
        0,
    )
    qh, kh = w_query.shape[1], w_key.shape[1]
    w_qkv = [
        jnp.concatenate([small[0, :, a:b], small[1, :, a:b]], axis=1)
        for a, b in ((0, qh), (qh, qh + kh), (qh + kh, qh + 2 * kh))
    ]
    bias = jnp.concatenate([b_query, b_key, b_value])[None].astype(F32)
    bias = in_order(bias, across(bias), 0)
    bias = jnp.concatenate(
        [bias[:, a:b].reshape(1, -1) for a, b in ((0, qh), (qh, qh + kh), (qh + kh, qh + 2 * kh))],
        axis=1,
    )
    copies = lax.all_gather(adapters.astype(BF16), ("dp", "tensor"), axis=0, tiled=True)
    w_out_all = in_order(w_out, across(w_out), 0)
    w_gate_far = fetch(w_gate)
    w_up_far = fetch(w_up)
    w_down_far = fetch(w_down)

    qw, kw, hidden = parts * qh, parts * kh, parts * w_gate.shape[1]
    half = w_gate.shape[1]
    sections = []
    cursor = 0
    for size in (width, qw, width, kw, width, kw, qw, width, width, hidden, width, hidden, hidden, width):
        sections.append(copies[cursor : cursor + size])
        cursor += size
    a_q, b_q, a_k, b_k, a_v, b_v, a_o, b_o, a_g, b_g, a_u, b_u, a_d, b_d = sections

    def near(rows):
        return lax.dynamic_slice_in_dim(rows, part * half, half, 0)

    def far(rows):
        return lax.dynamic_slice_in_dim(rows, (parts - 1 - part) * half, half, 0)

    slots, chosen, first, balanced, column, bounds = row_tables(
        order[0], lengths[0], adapter_ids[0], part, parts, each
    )
    cos, sin = rope_tables(balanced - first)
    meta = jnp.stack([slots, chosen, first, balanced], axis=1)
    meta = jnp.concatenate([meta, jnp.zeros((local, 4), I32)], axis=1)
    meta_rows = meta.T
    gain_one = norm_gains[0:1].astype(F32)
    gain_two = norm_gains[1:2].astype(F32)
    heads, kv_heads = qw // HEAD, kw // HEAD

    w_cat = jnp.concatenate(w_qkv + [a_q, a_k, a_v], axis=1)
    w_out_cat = jnp.concatenate([w_out_all, a_o], axis=1)
    a_pair = jnp.concatenate([a_g, a_u], axis=1)

    xs, n1, q, kv, z = project(moved, meta, cos, sin, gain_one, w_cat, bias, b_q, b_k, b_v)
    other_kv = across(kv)
    dy = sort_cotangent(moved_back, meta, b_d)
    o, logs, merged = attend(bounds, q, meta, kv, other_kv, column[:, None], heads, kv_heads)
    y1, xg, xu, z_out = middle(o, xs, meta, w_out_cat, b_o, gain_two, a_pair)
    y_a, d_a, gbg_a, gbu_a, gad_a = feed(
        xg, xu, dy, w_gate, w_up, w_down, near(b_g), near(b_u), near(a_d)
    )
    y_b, d_b, gbg_b, gbu_b, gad_b = feed(
        xg, xu, dy, w_gate_far, w_up_far, w_down_far, far(b_g), far(b_u), far(a_d)
    )
    out_rows, grad_b_d = finish(y_a, y_b, y1, dy, meta, meta_rows, b_d)
    layer_out = give_back(out_rows)
    dy1, dar, grad_pair, grad_b_o, grad_a_o = middle_back(
        d_a, d_b, y1, dy, xg, o, z_out, meta, a_pair, b_o, w_out_cat, gain_two
    )
    early = jnp.concatenate(
        [
            jnp.zeros((3 * width + qw + 2 * kw, rank), BF16),
            grad_a_o,
            grad_b_o,
            grad_pair[:, :rank],
            in_order(gbg_a, gbg_b, 0),
            grad_pair[:, rank:],
            in_order(gbu_a, gbu_b, 0),
            in_order(gad_a, gad_b, 0),
            grad_b_d,
        ],
        axis=0,
    )
    reduced_early = lax.psum_scatter(early, ("dp", "tensor"), scatter_dimension=0, tiled=True)
    gq, dkv_own, dkv_other = attend_back(
        bounds, q, dar, o, logs, meta_rows, cos, sin, merged, column[None, :], heads, kv_heads
    )
    dkv_got = across(dkv_other)
    dx_rows, grad_a_qkv, grad_b_qkv = input_back(
        gq, dkv_own, dkv_got, xs, n1, z, dy1, meta, meta_rows, cos, sin, gain_one, w_cat,
        b_q, b_k, b_v,
    )
    input_grad = give_back(dx_rows)
    late = jnp.concatenate(
        [
            grad_a_qkv[:, :rank],
            grad_b_qkv[:qw],
            grad_a_qkv[:, rank : 2 * rank],
            grad_b_qkv[qw : qw + kw],
            grad_a_qkv[:, 2 * rank :],
            grad_b_qkv[qw + kw :],
        ],
        axis=0,
    )
    late = lax.psum(late, ("dp", "tensor"))
    own_rows = adapters.shape[0]
    flat = place * parts + part
    late = jnp.concatenate(
        [late, jnp.zeros((copies.shape[0] - late.shape[0], rank), BF16)], axis=0
    )
    reduced_late = lax.dynamic_slice_in_dim(late, flat * own_rows, own_rows, 0)
    reduced = reduced_early.astype(F32) + reduced_late.astype(F32)
    moment_one = BETA_ONE * first_moment + (1.0 - BETA_ONE) * reduced
    moment_two = BETA_TWO * second_moment + (1.0 - BETA_TWO) * reduced * reduced
    corrected_one = moment_one / (1.0 - BETA_ONE**STEP)
    corrected_two = moment_two / (1.0 - BETA_TWO**STEP)
    updated = adapters - LEARN_RATE * (
        corrected_one / (jnp.sqrt(corrected_two) + ADAM_EPS) + WEIGHT_DECAY * adapters
    )
    return (
        layer_out,
        input_grad,
        reduced,
        moment_one,
        moment_two,
        updated,
        updated.astype(BF16),
    )


def solution(mesh):
    both = P(("dp", "tensor"), None)
    rows = P("dp", None)
    return jax.shard_map(
        per_device,
        mesh=mesh,
        in_specs=(rows, rows, rows, rows, rows, P())
        + (P(None, "tensor"),) * 3
        + (P("tensor"),) * 3
        + (P("tensor", None), P(None, "tensor"), P(None, "tensor"), P("tensor", None))
        + (both,) * 3,
        out_specs=(rows, rows) + (both,) * 5,
        check_vma=False,
    )
```

time: 1580 us -> 775 us (0.49)
  matrix products: 390 us -> 0 us
  blocking collectives: 417 us -> 162 us
  Pallas kernels: 0 us -> 204 us
  waiting for transfers between devices: 373 us -> 202 us
  local copies, waits for them, and re-layouts: 171 us -> 55 us
  other arithmetic: 136 us -> 51 us
  starting transfers between devices: 38.5 us -> 74.3 us
    dot_general x77 -> x0, matrix products: 390 us -> none  [the longest x21 121 us: dot_last(): lax.dot_general(left, right, (((1,), (1,)), ((), ())), preferred_element_...]
    psum x3 -> x1, waiting for transfers between devices: 308 us -> 0.02 us  [per_device(): late = lax.psum(late, ('dp', 'tensor'))]
    pallas_call x0 -> x10, Pallas kernels: none -> 204 us  [the longest x2 73.8 us: feed(): pl.pallas_call(functools.partial(feed_kernel, hidden), grid=(pl.cdiv(hidd...]
    ppermute x0 -> x13, waiting for transfers between devices: none -> 163 us  [the longest x10 163 us: across(): return lax.ppermute(values, 'tensor', swap)]
    psum x2 -> x0, blocking collectives: 152 us -> none  [the longest x1 110 us: per_device(): down_sum, rank_down_sum = lax.psum((down_part, rank_down_part), 'tensor')]
    unnamed x1, blocking collectives: 265 us -> 162 us
    dynamic_update_slice x6 -> x0, local copies, waits for them, and re-layouts: 58.5 us -> none  [attend_forward(): results, log_totals = lax.map(one_block, (query_blocks, starts))]
    another operation x6 -> x3, other arithmetic: 44.3 us -> 0.78 us  [the longest x2 0.61 us: row_tables(): jnp.stack([first[::QUERY_TILE] // KEY_TILE, balanced[QUERY_TILE - 1::QUER...]
  transfers between devices with their start and end apart: 9 -> 20, of which waited for: 6 -> 6; matrix products, arithmetic and copies ran while one was open for 36% -> 34% of each run, Pallas kernels for 0% -> 5%
where the time goes in v1:
time: 775 us; the launch traced here: 762 us
  Pallas kernels  204 us (26%)
  waiting for transfers between devices  202 us (26%)
  blocking collectives  162 us (21%)
  starting transfers between devices  74.3 us (10%)
  local copies, waits for them, and re-layouts  55 us (7%)
  other arithmetic  51 us (7%)
  between operations  14.8 us (2%)
    ppermute x10, waiting for transfers between devices, across(): return lax.ppermute(values, 'tensor', swap)  163 us
    unnamed x1, blocking collectives  162 us
    pallas_call x2, Pallas kernels, feed(): pl.pallas_call(functools.partial(feed_kernel, hidden), grid=(pl.cdiv(hidd...  73.8 us
    pallas_call x1, Pallas kernels, attend(): pl.pallas_call(functools.partial(attend_kernel, heads, kv_heads), grid_sp...  41.2 us
    ppermute x10, starting transfers between devices, across(): return lax.ppermute(values, 'tensor', swap)  35.5 us
    all_to_all x2, waiting for transfers between devices, give_back(): lax.all_to_all(values.reshape(devices, piece, width), 'dp', split_axis=0,...  34.5 us
    pallas_call x1, Pallas kernels, attend_back(): pl.pallas_call(functools.partial(attend_back_kernel, heads, kv_heads), gr...  32.5 us
    all_to_all x2, starting transfers between devices, give_back(): lax.all_to_all(values.reshape(devices, piece, width), 'dp', split_axis=0,...  20.2 us
  transfers between devices with their start and end apart: 20, of which 6 were waited for; matrix products, arithmetic and copies ran while one was open for 34% of the time, Pallas kernels for 5%

profile of v1, /device:TPU:1, one launch (start us, length us, event | category | flops | bytes accessed | tf_op | source)
XLA Modules:
  0.0 761.9 jit_solution(2157169078065349057)
XLA Ops:
  9.1 3.3 constant_dynamic-slice_fusion.4
  19.9 7.4 all-to-all-start
  27.6 3.2 constant_dynamic-slice_fusion.3
  36.4 2.6 dynamic-slice_bitcast_fusion
  44.1 145.6 %collective-permute-done.8 = bf16[1216,896]{1,0:T(8,128)(2,1)} collective-permute-done((bf16[1216,896]{1,0:T(8,128)(2,1)}, bf16[1216,896]{1,0:T(8,128)(2,1)}, u32[]{:S(2)}, u32[]{:S(2)}) %collective-permute-start.8) | collective-permute-done | bytes 2179104 | tf_op jit(solution)/shard_map/ppermute | solution.py:817
  199.2 2.4 broadcast_select_fusion.7
  201.6 17.5 %collective-permute-done = bf16[896,576]{0,1:T(8,128)(2,1)S(1)} collective-permute-done((bf16[896,576]{0,1:T(8,128)(2,1)}, bf16[896,576]{0,1:T(8,128)(2,1)S(1)}, u32[]{:S(2)}, u32[]{:S(2)}) %collective-permute-start) | collective-permute-done | bytes 1032224 | tf_op jit(solution)/shard_map/ppermute | solution.py:817
  225.5 2.7 broadcast_select_fusion.1
  228.2 2.3 pad_maximum_fusion.2.wd_ref
  234.6 9.1 %pad_maximum_fusion = (bf16[896,2432]{1,0:T(8,128)(2,1)}, bf16[896,2432]{1,0:T(8,128)(2,1)}) fusion(bf16[448,2432]{1,0:T(8,128)(2,1)S(1)} %get-tuple-element.108, bf16[448,2432]{1,0:T(8,128)(2,1)S(1)} %get-tuple-element.107, bf16[448,2432]{1,0:T(8,128)(2,1)S(1)} %get-tuple-element.106, bf16[448,2432]{1,0:T(8,128)(2,1)S(1)} %get-tuple-element.105), kind=kLoop, calls=%fused_computation.7 | loop fusion | flops 17432576 | bytes 17432576 | tf_op jit(solution)/shard_map/concatenate | solution.py:828
  243.7 7.9 %reshape.226 = bf16[22912,128]{1,0:T(8,128)(2,1)} reshape(bf16[32,716,128]{2,1,0:T(8,128)(2,1)} %all-gather.3.cloned.1.call-done) | data formatting | bytes 11730944
  251.6 6.6 all-to-all-start.1
  258.2 3.0 fusion.17
  261.2 5.3 concatenate.75.w_ref
  267.9 10.7 %project.1 = (bf16[768,896]{1,0:T(8,128)(2,1)}, bf16[768,896]{1,0:T(8,128)(2,1)}, bf16[768,896]{1,0:T(8,128)(2,1)}, bf16[768,256]{1,0:T(8,128)(2,1)}, bf16[768,384]{1,0:T(8,128)(2,1)}) custom-call(bf16[768,896]{1,0:T(8,128)(2,1)} %bitcast.8.x_ref, s32[768,8]{1,0:T(8,128)} %copy.83.meta_ref, f32[768,128]{1,0:T(8,128)} %get-tuple-element.139.cos_ref, ...), custom_call_target="tpu_custom_call" | custom-call | flops 3170893824 | bytes 9000000 | tf_op jit(solution)/shard_map/project/pallas_call | solution.py:153
  287.2 4.9 cotangent.1.dy_ref
  293.2 41.2 %attend.1 = (bf16[768,896]{1,0:T(8,128)(2,1)}, f32[16,768]{1,0:T(8,128)}, bf16[1536,256]{1,0:T(8,128)(2,1)}) custom-call(s32[2,6]{1,0:T(2,128)} %pad_add_fusion.bounds_ref, bf16[768,896]{1,0:T(8,128)(2,1)} %get-tuple-element.42.q_ref, s32[768,8]{1,0:T(8,128)} %copy.83.meta_ref, bf16[768,256]{1,0:T(8,128)(2,1)} %get-tuple-element.43.own_ref, ...), custom_call_target="tpu_custom_call" | custom-call | flops 4227858432 | bytes 6000000 | tf_op jit(solution)/shard_map/attend/pallas_call | solution.py:296
  334.4 7.6 middle.1
  341.9 36.8 %feed.2 = (f32[768,1024]{1,0:T(8,128)}, f32[768,1152]{1,0:T(8,128)}, bf16[2432,128]{1,0:T(8,128)(2,1)}, bf16[2432,128]{1,0:T(8,128)(2,1)}, bf16[2432,128]{1,0:T(8,128)(2,1)}) custom-call(bf16[768,1024]{1,0:T(8,128)(2,1)} %get-tuple-element.46.xg_ref, bf16[768,1024]{1,0:T(8,128)(2,1)} %get-tuple-element.47.xu_ref, bf16[768,1024]{1,0:T(8,128)(2,1)} %cotangent.1.dy_ref, ...), custom_call_target="tpu_custom_call" | custom-call | flops 24385683456 | bytes 30000000 | tf_op jit(solution)/shard_map/feed/pallas_call | solution.py:674
  378.8 37.0 %feed.3 = (f32[768,1024]{1,0:T(8,128)}, f32[768,1152]{1,0:T(8,128)}, bf16[2432,128]{1,0:T(8,128)(2,1)}, bf16[2432,128]{1,0:T(8,128)(2,1)}, bf16[2432,128]{1,0:T(8,128)(2,1)}) custom-call(bf16[768,1024]{1,0:T(8,128)(2,1)} %get-tuple-element.46.xg_ref, bf16[768,1024]{1,0:T(8,128)(2,1)} %get-tuple-element.47.xu_ref, bf16[768,1024]{1,0:T(8,128)(2,1)} %cotangent.1.dy_ref, ...), custom_call_target="tpu_custom_call" | custom-call | flops 24385683456 | bytes 30000000 | tf_op jit(solution)/shard_map/feed/pallas_call | solution.py:674
  415.8 12.2 %middle_back.1 = (f32[768,896]{1,0:T(8,128)}, bf16[768,896]{1,0:T(8,128)(2,1)}, bf16[896,256]{1,0:T(8,128)(2,1)}, bf16[896,128]{1,0:T(8,128)(2,1)}, bf16[896,128]{1,0:T(8,128)(2,1)}) custom-call(f32[768,1152]{1,0:T(8,128)} %get-tuple-element.52.da_ref, f32[768,1152]{1,0:T(8,128)} %get-tuple-element.53.db_ref, f32[768,896]{1,0:T(8,128)} %get-tuple-element.50.y1_ref, ...), custom_call_target="tpu_custom_call" | custom-call | flops 2614886400 | bytes 20000000 | tf_op jit(solution)/shard_map/middle_back/pallas_call | solution.py:585
  427.9 32.5 %attend_back.1 = (bf16[768,896]{1,0:T(8,128)(2,1)}, bf16[768,256]{1,0:T(8,128)(2,1)}, bf16[768,256]{1,0:T(8,128)(2,1)}) custom-call(s32[2,6]{1,0:T(2,128)} %pad_add_fusion.bounds_ref, bf16[768,896]{1,0:T(8,128)(2,1)} %get-tuple-element.42.q_ref, bf16[768,896]{1,0:T(8,128)(2,1)} %get-tuple-element.55.g_ref, bf16[768,896]{1,0:T(8,128)(2,1)} %get-tuple-element.44.o_ref, ...), custom_call_target="tpu_custom_call" | custom-call | flops 10569646080 | bytes 9000000 | tf_op jit(solution)/shard_map/attend_back/pallas_call | solution.py:418
  460.5 24.6 %collective-permute-start.11 = (bf16[768,256]{1,0:T(8,128)(2,1)}, bf16[768,256]{1,0:T(8,128)(2,1)}, u32[]{:S(2)}, u32[]{:S(2)}) collective-permute-start(bf16[768,256]{1,0:T(8,128)(2,1)} %get-tuple-element.60), channel_id=1, source_target_pairs={{0,1},{1,0},{2,3},{3,2},{4,5},{5,4},{6,7},{7,6},{8,9},{9,8},{10,11... | collective-permute-start | bytes 1179656 | tf_op jit(solution)/shard_map/ppermute | solution.py:817
  485.1 8.3 %finish.1 = (bf16[768,896]{1,0:T(8,128)(2,1)}, bf16[896,128]{1,0:T(8,128)(2,1)}) custom-call(f32[768,1024]{1,0:T(8,128)} %get-tuple-element.48.ya_ref, f32[768,1024]{1,0:T(8,128)} %get-tuple-element.49.yb_ref, f32[768,896]{1,0:T(8,128)} %get-tuple-element.50.y1_ref, bf16[768,1024]{1,0:T(8,128)(2,1)} %cotangent.1.dy_ref, s32[768,8]{1,0:T(8,128)} %copy.83.meta_ref, ...), custom_call_target="tpu_custom_call" | custom-call | flops 1409286144 | bytes 13000000 | tf_op jit(solution)/shard_map/finish/pallas_call | solution.py:523
  493.4 12.3 %all-to-all-start.2 = ((bf16[16,48,896]{2,1,0:T(8,128)(2,1)}), bf16[16,48,896]{2,1,0:T(8,128)(2,1)S(1)}, u32[]{:S(2)}, u32[]{:S(2)}) async-start(bf16[16,48,896]{2,1,0:T(8,128)(2,1)} %bitcast.60), calls=%async_computation.2 | async-start | bytes 2752512 | tf_op jit(solution)/shard_map/all_to_all | solution.py:839
  513.6 12.4 %input_back.1 = (bf16[768,896]{1,0:T(8,128)(2,1)}, bf16[896,384]{1,0:T(8,128)(2,1)}, bf16[1152,128]{1,0:T(8,128)(2,1)}) custom-call(bf16[768,896]{1,0:T(8,128)(2,1)} %get-tuple-element.58.gq_ref, bf16[768,256]{1,0:T(8,128)(2,1)} %get-tuple-element.59.own_ref, bf16[768,256]{1,0:T(8,128)(2,1)} %collective-permute-done.11.got_ref, ...), custom_call_target="tpu_custom_call" | custom-call | flops 3991142400 | bytes 14000000 | tf_op jit(solution)/shard_map/input_back/pallas_call | solution.py:742
  526.1 8.6 %all-to-all-done.2 = bf16[16,48,896]{2,1,0:T(8,128)(2,1)S(1)} async-done(((bf16[16,48,896]{2,1,0:T(8,128)(2,1)}), bf16[16,48,896]{2,1,0:T(8,128)(2,1)S(1)}, u32[]{:S(2)}, u32[]{:S(2)}) %all-to-all-start.2) | async-done | bytes 1376288 | tf_op jit(solution)/shard_map/all_to_all | solution.py:839
  534.6 7.9 %all-to-all-start.3 = ((bf16[16,48,896]{2,1,0:T(8,128)(2,1)}), bf16[16,48,896]{2,1,0:T(8,128)(2,1)}, u32[]{:S(2)}, u32[]{:S(2)}) async-start(bf16[16,48,896]{2,1,0:T(8,128)(2,1)} %bitcast.59), calls=%async_computation.3 | async-start | bytes 2752512 | tf_op jit(solution)/shard_map/all_to_all | solution.py:839
  548.1 25.9 %all-to-all-done.3 = bf16[16,48,896]{2,1,0:T(8,128)(2,1)} async-done(((bf16[16,48,896]{2,1,0:T(8,128)(2,1)}), bf16[16,48,896]{2,1,0:T(8,128)(2,1)}, u32[]{:S(2)}, u32[]{:S(2)}) %all-to-all-start.3) | async-done | bytes 1376288 | tf_op jit(solution)/shard_map/all_to_all | solution.py:839
  575.6 161.7 %fusion = bf16[720,128]{1,0:T(8,128)(2,1)S(1)} fusion(bf16[22912,128]{1,0:T(8,128)(2,1)} %constant_dynamic-update-slice_fusion), kind=kCustom, calls=%all-reduce-scatter | all-reduce-scatter fusion | flops 2949121 | bytes 6049792
  737.4 2.5 collective-permute-start.13
  739.9 2.7 collective-permute-done.13
  (196 shorter events, 78.6 us)
Async XLA Ops:
  7.2 236.5 %all-gather.3.cloned.1.call-start = ((), (), s32[]{:S(2)}) async-start(), calls=%async_computation.5 | async-start | bytes 6082560 | tf_op jit(solution)/shard_map/all_gather | solution.py:863
  12.4 208.1 %collective-permute-start.6 = (bf16[448,2432]{1,0:T(8,128)(2,1)}, bf16[448,2432]{1,0:T(8,128)(2,1)}, u32[]{:S(2)}, u32[]{:S(2)}) collective-permute-start(bf16[448,2432]{1,0:T(8,128)(2,1)} %constant_dynamic-slice_fusion.4), channel_id=1, source_target_pairs={{0,1},{1,0},{2,3},{3,2},{4,5},{5,4},{6,7},{7,6},{8,9},{9,8},{10,11... | collective-permute-start | bytes 6537224 | tf_op jit(solution)/shard_map/ppermute | solution.py:817
  15.9 209.5 %collective-permute-start.4 = (bf16[448,2432]{1,0:T(8,128)(2,1)}, bf16[448,2432]{1,0:T(8,128)(2,1)}, u32[]{:S(2)}, u32[]{:S(2)}) collective-permute-start(bf16[448,2432]{1,0:T(8,128)(2,1)} %constant_dynamic-slice_fusion.5), channel_id=1, source_target_pairs={{0,1},{1,0},{2,3},{3,2},{4,5},{5,4},{6,7},{7,6},{8,9},{9,8},{10,11... | collective-permute-start | bytes 6537224 | tf_op jit(solution)/shard_map/ppermute | solution.py:817
  17.2 177.2 %collective-permute-start.1 = (f32[1,576]{1,0:T(1,128)}, f32[1,576]{1,0:T(1,128)}, u32[]{:S(2)}, u32[]{:S(2)}) collective-permute-start(f32[1,576]{1,0:T(1,128)} %maximum_convert_fusion), channel_id=1, source_target_pairs={{0,1},{1,0},{2,3},{3,2},{4,5},{5,4},{6,7},{7,6},{8,9},{9,8},{10,11... | collective-permute-start | bytes 6920 | tf_op jit(solution)/shard_map/ppermute | solution.py:817
  19.9 231.7 %all-to-all-start = ((bf16[16,48,896]{2,1,0:T(8,128)(2,1)}), bf16[16,48,896]{2,1,0:T(8,128)(2,1)}, u32[]{:S(2)}, u32[]{:S(2)}) async-start(bf16[16,48,896]{2,1,0:T(8,128)(2,1)} %dynamic-slice_bitcast_fusion.1), calls=%async_computation | async-start | bytes 2752512 | tf_op jit(solution)/shard_map/all_to_all | solution.py:835
  27.3 171.9 %collective-permute-start.3 = (bf16[448,896]{1,0:T(8,128)(2,1)S(1)}, bf16[448,896]{1,0:T(8,128)(2,1)}, u32[]{:S(2)}, u32[]{:S(2)}) collective-permute-start(bf16[448,896]{1,0:T(8,128)(2,1)S(1)} %copy-done.18), channel_id=1, source_target_pairs={{0,1},{1,0},{2,3},{3,2},{4,5},{5,4},{6,7},{7,6},{8,9},{9,8},{10,11... | collective-permute-start | bytes 2408456 | tf_op jit(solution)/shard_map/ppermute | solution.py:817
  30.8 158.8 %collective-permute-start.8 = (bf16[1216,896]{1,0:T(8,128)(2,1)}, bf16[1216,896]{1,0:T(8,128)(2,1)}, u32[]{:S(2)}, u32[]{:S(2)}) collective-permute-start(bf16[1216,896]{1,0:T(8,128)(2,1)} %constant_dynamic-slice_fusion.3), channel_id=1, source_target_pairs={{0,1},{1,0},{2,3},{3,2},{4,5},{5,4},{6,7},{7,6},{8,9},{9,8},{10,11... | collective-permute-start | bytes 6537224 | tf_op jit(solution)/shard_map/ppermute | solution.py:817
  189.6 35.9 %collective-permute-start.9 = (bf16[1216,896]{1,0:T(8,128)(2,1)}, bf16[1216,896]{1,0:T(8,128)(2,1)}, u32[]{:S(2)}, u32[]{:S(2)}) collective-permute-start(bf16[1216,896]{1,0:T(8,128)(2,1)} %collective-permute-done.8), channel_id=1, source_target_pairs={{0,2},{2,0},{4,6},{6,4},{8,10},{10,8},{12,14},{14,12},{16,18},{18,... | collective-permute-start | bytes 6537224 | tf_op jit(solution)/shard_map/ppermute | solution.py:827
  194.4 24.7 %collective-permute-start = (bf16[896,576]{0,1:T(8,128)(2,1)}, bf16[896,576]{0,1:T(8,128)(2,1)S(1)}, u32[]{:S(2)}, u32[]{:S(2)}) collective-permute-start(bf16[896,576]{0,1:T(8,128)(2,1)} %copy.80), channel_id=1, source_target_pairs={{0,1},{1,0},{2,3},{3,2},{4,5},{5,4},{6,7},{7,6},{8,9},{9,8},{10,11... | collective-permute-start | bytes 3096584 | tf_op jit(solution)/shard_map/ppermute | solution.py:817
  196.6 23.9 %copy-start.27 = (s32[768,8]{0,1:T(8,128)}, s32[768,8]{0,1:T(8,128)S(1)}, u32[]{:S(2)}) copy-start(s32[768,8]{0,1:T(8,128)S(1)} %concatenate.71) | copy-start | bytes 73732
  220.5 10.0 %collective-permute-start.7 = (bf16[448,2432]{1,0:T(8,128)(2,1)}, bf16[448,2432]{1,0:T(8,128)(2,1)S(1)}, u32[]{:S(2)}, u32[]{:S(2)}) collective-permute-start(bf16[448,2432]{1,0:T(8,128)(2,1)} %collective-permute-done.6), channel_id=1, source_target_pairs={{0,2},{2,0},{4,6},{6,4},{8,10},{10,8},{12,14},{14,12},{16,18},{18,... | collective-permute-start | bytes 6537224 | tf_op jit(solution)/shard_map/ppermute | solution.py:827
  225.5 7.1 collective-permute-start.5
  251.6 35.6 %all-to-all-start.1 = ((bf16[16,48,896]{2,1,0:T(8,128)(2,1)}), bf16[16,48,896]{2,1,0:T(8,128)(2,1)}, u32[]{:S(2)}, u32[]{:S(2)}) async-start(bf16[16,48,896]{2,1,0:T(8,128)(2,1)} %dynamic-slice_bitcast_fusion), calls=%async_computation.1 | async-start | bytes 2752512 | tf_op jit(solution)/shard_map/all_to_all | solution.py:835
  267.9 11.9 %copy-start.17 = (bf16[896,128]{1,0:T(8,128)(2,1)S(1)}, bf16[896,128]{1,0:T(8,128)(2,1)}, u32[]{:S(2)}) copy-start(bf16[896,128]{1,0:T(8,128)(2,1)} %get-tuple-element.94) | copy-start | bytes 688132
  267.9 12.7 %copy-start.4 = (bf16[448,896]{1,0:T(8,128)(2,1)S(1)}, bf16[448,896]{1,0:T(8,128)(2,1)}, u32[]{:S(2)}) copy-start(bf16[448,896]{1,0:T(8,128)(2,1)} %get-tuple-element.116) | copy-start | bytes 2408452
  278.5 14.7 %collective-permute-start.2 = (bf16[768,256]{1,0:T(8,128)(2,1)}, bf16[768,256]{1,0:T(8,128)(2,1)}, u32[]{:S(2)}, u32[]{:S(2)}) collective-permute-start(bf16[768,256]{1,0:T(8,128)(2,1)} %get-tuple-element.43.own_ref), channel_id=1, source_target_pairs={{0,1},{1,0},{2,3},{3,2},{4,5},{5,4},{6,7},{7,6},{8,9},{9,8},{10,11... | collective-permute-start | bytes 1179656 | tf_op jit(solution)/shard_map/ppermute | solution.py:817
  460.5 53.1 %collective-permute-start.11 = (bf16[768,256]{1,0:T(8,128)(2,1)}, bf16[768,256]{1,0:T(8,128)(2,1)}, u32[]{:S(2)}, u32[]{:S(2)}) collective-permute-start(bf16[768,256]{1,0:T(8,128)(2,1)} %get-tuple-element.60), channel_id=1, source_target_pairs={{0,1},{1,0},{2,3},{3,2},{4,5},{5,4},{6,7},{7,6},{8,9},{9,8},{10,11... | collective-permute-start | bytes 1179656 | tf_op jit(solution)/shard_map/ppermute | solution.py:817
  493.4 12.3 %copy-start.26 = (bf16[896,128]{1,0:T(8,128)(2,1)S(1)}, bf16[896,128]{1,0:T(8,128)(2,1)}, u32[]{:S(2)}) copy-start(bf16[896,128]{1,0:T(8,128)(2,1)} %get-tuple-element.65) | copy-start | bytes 688132
  493.4 13.0 %copy-start.25 = (bf16[896,128]{1,0:T(8,128)(2,1)S(1)}, bf16[896,128]{1,0:T(8,128)(2,1)}, u32[]{:S(2)}) copy-start(bf16[896,128]{1,0:T(8,128)(2,1)} %get-tuple-element.66) | copy-start | bytes 688132
  493.4 15.5 %copy-start.8 = (bf16[2432,128]{1,0:T(8,128)(2,1)S(1)}, bf16[2432,128]{1,0:T(8,128)(2,1)}, u32[]{:S(2)}) copy-start(bf16[2432,128]{1,0:T(8,128)(2,1)} %get-tuple-element.68) | copy-start | bytes 1867780
  493.4 15.5 %copy-start.10 = (bf16[2432,128]{1,0:T(8,128)(2,1)S(1)}, bf16[2432,128]{1,0:T(8,128)(2,1)}, u32[]{:S(2)}) copy-start(bf16[2432,128]{1,0:T(8,128)(2,1)} %get-tuple-element.69) | copy-start | bytes 1867780
  493.4 41.2 %all-to-all-start.2 = ((bf16[16,48,896]{2,1,0:T(8,128)(2,1)}), bf16[16,48,896]{2,1,0:T(8,128)(2,1)S(1)}, u32[]{:S(2)}, u32[]{:S(2)}) async-start(bf16[16,48,896]{2,1,0:T(8,128)(2,1)} %bitcast.60), calls=%async_computation.2 | async-start | bytes 2752512 | tf_op jit(solution)/shard_map/all_to_all | solution.py:839
  526.0 16.6 %copy-start.5 = (bf16[2432,128]{1,0:T(8,128)(2,1)S(1)}, bf16[2432,128]{1,0:T(8,128)(2,1)}, u32[]{:S(2)}) copy-start(bf16[2432,128]{1,0:T(8,128)(2,1)} %get-tuple-element.72) | copy-start | bytes 1867780
  526.1 16.6 %copy-start.6 = (bf16[2432,128]{1,0:T(8,128)(2,1)S(1)}, bf16[2432,128]{1,0:T(8,128)(2,1)}, u32[]{:S(2)}) copy-start(bf16[2432,128]{1,0:T(8,128)(2,1)} %get-tuple-element.73) | copy-start | bytes 1867780
  534.6 39.3 %all-to-all-start.3 = ((bf16[16,48,896]{2,1,0:T(8,128)(2,1)}), bf16[16,48,896]{2,1,0:T(8,128)(2,1)}, u32[]{:S(2)}, u32[]{:S(2)}) async-start(bf16[16,48,896]{2,1,0:T(8,128)(2,1)} %bitcast.59), calls=%async_computation.3 | async-start | bytes 2752512 | tf_op jit(solution)/shard_map/all_to_all | solution.py:839
  542.6 201.0 %all-reduce.5.cloned.1.call-start = ((), (), s32[]{:S(2)}) async-start(), calls=%async_computation.4 | async-start | bytes 1966080 | tf_op jit(solution)/shard_map/psum | solution.py:950
  546.5 197.1 %copy-start.12 = (f32[716,128]{1,0:T(8,128)S(1)}, f32[716,128]{1,0:T(8,128)}, u32[]{:S(2)}) copy-start(f32[716,128]{1,0:T(8,128)} %param.35) | copy-start | bytes 1099780
  546.5 197.1 %copy-start.13 = (f32[716,128]{1,0:T(8,128)S(1)}, f32[716,128]{1,0:T(8,128)}, u32[]{:S(2)}) copy-start(f32[716,128]{1,0:T(8,128)} %param.36) | copy-start | bytes 1099780
  546.5 197.1 %copy-start.22 = (f32[716,128]{1,0:T(8,128)S(1)}, f32[716,128]{1,0:T(8,128)}, u32[]{:S(2)}) copy-start(f32[716,128]{1,0:T(8,128)} %param.37) | copy-start | bytes 1099780
  546.6 200.2 %collective-permute-start.10 = (bf16[16,48,896]{2,1,0:T(8,128)(2,1)S(1)}, bf16[16,48,896]{2,1,0:T(8,128)(2,1)}, u32[]{:S(2)}, u32[]{:S(2)}) collective-permute-start(bf16[16,48,896]{2,1,0:T(8,128)(2,1)S(1)} %all-to-all-done.2), channel_id=1, source_target_pairs={{0,1},{1,0},{2,3},{3,2},{4,5},{5,4},{6,7},{7,6},{8,9},{9,8},{10,11... | collective-permute-start | bytes 4128776 | tf_op jit(solution)/shard_map/ppermute | solution.py:817
  574.0 176.4 %collective-permute-start.12 = (bf16[16,48,896]{2,1,0:T(8,128)(2,1)}, bf16[16,48,896]{2,1,0:T(8,128)(2,1)}, u32[]{:S(2)}, u32[]{:S(2)}) collective-permute-start(bf16[16,48,896]{2,1,0:T(8,128)(2,1)} %all-to-all-done.3), channel_id=1, source_target_pairs={{0,1},{1,0},{2,3},{3,2},{4,5},{5,4},{6,7},{7,6},{8,9},{9,8},{10,11... | collective-permute-start | bytes 4128776 | tf_op jit(solution)/shard_map/ppermute | solution.py:817
  737.4 5.2 collective-permute-start.13
  (29 other events, 145.9 us)
Sparse Core Ops, SparseCore 0:
  11.5 95.1 all-gather.2
  549.2 136.7 all-reduce.4

commit v2 on v1

v2 whole, which is shorter than its diff:
```python
import functools

import jax
import jax.numpy as jnp
from jax import lax
from jax.experimental import pallas as pl
from jax.experimental.pallas import tpu as pltpu
from jax.sharding import PartitionSpec as P

HEAD = 64
RANK = 16
STEP = 3

ADAPTER_SCALE = 2.0
NORM_EPS = 1e-06
ROPE_BASE = 1000000.0
BETA_ONE = 0.5
BETA_TWO = 0.6
LEARN_RATE = 0.04
WEIGHT_DECAY = 0.01
ADAM_EPS = 1e-08
MASKED_SCORE = -1e30
PLANES = 4
MESH = pl.DeviceIdType.MESH

LANES = 128
ROW_TILE = 256
QUERY_TILE = 128
KEY_TILE = 256
HIDDEN_TILE = 512

F32 = jnp.float32
BF16 = jnp.bfloat16
I32 = jnp.int32


def nn(left, right):
    return lax.dot_general(left, right, (((1,), (0,)), ((), ())), preferred_element_type=F32)


def nt(left, right):
    return lax.dot_general(left, right, (((1,), (1,)), ((), ())), preferred_element_type=F32)


def tn(left, right):
    return lax.dot_general(left, right, (((0,), (0,)), ((), ())), preferred_element_type=F32)


def lane_iota(shape):
    return lax.broadcasted_iota(I32, shape, 1)


def row_iota(shape):
    return lax.broadcasted_iota(I32, shape, 0)


def whole(array):
    return pl.BlockSpec(array.shape, lambda *_: (0,) * array.ndim)


def row_blocks(array, tile):
    return pl.BlockSpec((tile, array.shape[1]), lambda i, *_: (i, 0))


def rank_mask(adapter_col, width):
    return jnp.where(lane_iota((adapter_col.shape[0], width)) // RANK == adapter_col, 1.0, 0.0)


def turn(values):
    lanes = lane_iota(values.shape) % HEAD
    return jnp.where(
        lanes < HEAD // 2,
        -pltpu.roll(values, LANES - HEAD // 2, 1),
        pltpu.roll(values, HEAD // 2, 1),
    )


def rms(values):
    return lax.rsqrt(jnp.mean(values * values, axis=-1, keepdims=True) + NORM_EPS)


def norm_back(values, gain, grad):
    inverse = rms(values)
    weighted = grad * gain
    return inverse * weighted - values * inverse * inverse * inverse * jnp.mean(
        weighted * values, axis=-1, keepdims=True
    )


def pick_rows(place_col, slots):
    hit = place_col == lane_iota((place_col.shape[0], slots))
    return jnp.where(hit, 1.0, 0.0).astype(BF16)


def place_rows(place_row, slots):
    hit = row_iota((slots, place_row.shape[1])) == place_row
    return jnp.where(hit, 1.0, 0.0).astype(BF16)


def params(**more):
    return pltpu.CompilerParams(vmem_limit_bytes=60 * 1024 * 1024, **more)


def cost(flops, moved):
    return pl.CostEstimate(flops=int(flops), bytes_accessed=int(moved), transcendentals=0)


def xor_bit(value, bit):
    size = 2**bit
    return value + size * (1 - 2 * lax.rem(value // size, 2))


def subsets(axes):
    out = [()]
    for axis in axes:
        out += [chosen + (axis,) for chosen in out]
    return out


def flip(place, part, axes):
    for axis in axes:
        if axis == "tensor":
            part = 1 - part
        else:
            place = xor_bit(place, axis)
    return place, part


def front_kernel(
    devices, rows_ref, chunk_ref, wq_ref, wo_ref, got_ref, copies_ref, wq_out, wo_out,
    local_sem, tsend, trecv, csend, crecv, wsend, wrecv,
):
    place, part = lax.axis_index("dp"), lax.axis_index("tensor")
    plane = devices // PLANES
    depth, inside = place // plane, lax.rem(place, plane)
    core = lax.rem(place, 2)
    own = 2 * place + part
    barrier = pltpu.get_barrier_semaphore()
    for k in range(1, devices):
        pl.semaphore_signal(
            barrier, inc=1, device_id=(lax.rem(place + k, devices), part), device_id_type=MESH
        )
    pl.semaphore_signal(barrier, inc=1, device_id=(place, 1 - part), device_id_type=MESH)
    pl.semaphore_wait(barrier, devices)

    keep = [
        pltpu.make_async_copy(chunk_ref, copies_ref.at[own], local_sem.at[0]),
        pltpu.make_async_copy(rows_ref.at[place, part], got_ref.at[place], local_sem.at[1]),
    ]
    for copy in keep:
        copy.start()
    sent = []

    def chunk_copy(source, index, number, where):
        return pltpu.make_async_remote_copy(
            src_ref=source,
            dst_ref=copies_ref.at[index],
            send_sem=csend.at[number],
            recv_sem=crecv.at[index],
            device_id=where,
            device_id_type=MESH,
        )

    def send_chunk(source, index, where):
        copy = chunk_copy(source, index, len(sent), where)
        copy.start()
        sent.append(copy)

    def take_chunk(index):
        chunk_copy(chunk_ref, index, 0, (place, 1 - part)).wait_recv()

    def layer(turn):
        return lax.rem(depth + turn, PLANES)

    for turn in (2, 3, 1):
        send_chunk(chunk_ref, own, (layer(turn) * plane + inside, part))

    def weight_copy(ref, out, number, slot, where):
        return pltpu.make_async_remote_copy(
            src_ref=ref.at[slot],
            dst_ref=out.at[slot],
            send_sem=wsend.at[number],
            recv_sem=wrecv.at[number],
            device_id=where,
            device_id_type=MESH,
        )

    direct = [
        weight_copy(wq_ref, wq_out, 0, core, (place, 1 - part)),
        weight_copy(wo_ref, wo_out, 1, core, (place, 1 - part)),
    ]
    for copy in direct:
        copy.start()

    rows_sent = []
    for turn in (2, 3, 1, 0):
        for step in range(plane):
            if turn == 0 and step == 0:
                continue
            target = layer(turn) * plane + lax.rem(inside + step, plane)
            copy = pltpu.make_async_remote_copy(
                src_ref=rows_ref.at[target, part],
                dst_ref=got_ref.at[place],
                send_sem=tsend.at[len(rows_sent)],
                recv_sem=trecv.at[place],
                device_id=(target, part),
                device_id_type=MESH,
            )
            copy.start()
            rows_sent.append((copy, target))

    bits = [2**b for b in range(plane.bit_length() - 1)]
    bits = list(range(len(bits)))[::-1]
    orders = [["tensor"] + bits, bits[:-1] + ["tensor"] + bits[-1:]]
    relayed = []
    for stage in range(len(bits) + 1):
        for turn in (0, 1, 2, 3):
            order = orders[turn % 2]
            origin = layer(turn) * plane + inside
            where = flip(place, part, [order[stage]])
            for chosen in subsets(order[:stage]):
                at, side = flip(origin, part, chosen)
                index = 2 * at + side
                if turn == 0 and not chosen:
                    send_chunk(chunk_ref, index, where)
                    continue
                if stage == 0 or order[stage - 1] in chosen:
                    take_chunk(index)
                send_chunk(copies_ref.at[index], index, where)
        if stage == 0:
            partner = (xor_bit(place, 0), part)
            for number, (ref, out) in enumerate(((wq_ref, wq_out), (wo_ref, wo_out))):
                direct[number].wait_recv()
                copy = weight_copy(out, out, 2 + number, core, partner)
                copy.start()
                relayed.append(copy)
    for turn in (0, 1, 2, 3):
        order = orders[turn % 2]
        origin = layer(turn) * plane + inside
        for chosen in subsets(order):
            if order[-1] in chosen:
                at, side = flip(origin, part, chosen)
                take_chunk(2 * at + side)
    for number, (ref, out) in enumerate(((wq_ref, wq_out), (wo_ref, wo_out))):
        weight_copy(out, out, 2 + number, 1 - core, (place, 1 - part)).wait_recv()
    for copy, source in rows_sent:
        pltpu.make_async_remote_copy(
            src_ref=rows_ref.at[source, part],
            dst_ref=got_ref.at[source],
            send_sem=tsend.at[0],
            recv_sem=trecv.at[source],
            device_id=(source, part),
            device_id_type=MESH,
        ).wait_recv()
    for copy, _ in rows_sent:
        copy.wait_send()
    for copy in sent + direct + relayed:
        copy.wait_send()
    for copy in keep:
        copy.wait()


def front(rows, chunk, wq, wo, devices):
    _, _, piece, width = rows.shape
    anywhere = pl.BlockSpec(memory_space=pl.ANY)
    outs = [
        jax.ShapeDtypeStruct((devices, piece, width), BF16),
        jax.ShapeDtypeStruct((2 * devices,) + chunk.shape, BF16),
        jax.ShapeDtypeStruct(wq.shape, BF16),
        jax.ShapeDtypeStruct(wo.shape, BF16),
    ]
    return pl.pallas_call(
        functools.partial(front_kernel, devices),
        in_specs=[anywhere] * 4,
        out_specs=[anywhere] * 4,
        out_shape=outs,
        scratch_shapes=[
            pltpu.SemaphoreType.DMA((2,)),
            pltpu.SemaphoreType.DMA((devices,)),
            pltpu.SemaphoreType.DMA((devices,)),
            pltpu.SemaphoreType.DMA((2 * devices,)),
            pltpu.SemaphoreType.DMA((2 * devices,)),
            pltpu.SemaphoreType.DMA((4,)),
            pltpu.SemaphoreType.DMA((4,)),
        ],
        compiler_params=pltpu.CompilerParams(collective_id=0, has_side_effects=True),
        cost_estimate=cost(0, 100e6),
        name="front",
    )(rows, chunk, wq, wo)


def in_order(part, mine, theirs, place):
    @pl.when(part == 0)
    def _():
        place(mine, theirs)

    @pl.when(part == 1)
    def _():
        place(theirs, mine)


def project_kernel(
    part_ref, x_ref, meta_ref, cos_ref, sin_ref, gain_ref, mine_ref, theirs_ref,
    aq_ref, ak_ref, av_ref, bq_ref, bk_ref, bv_ref,
    n_ref, q_ref, kv_ref, z_ref, w_ref, bias,
):
    width = x_ref.shape[1]
    qw, kw = bq_ref.shape[0], bk_ref.shape[0]
    rank = bq_ref.shape[1]
    low = qw + 2 * kw

    @pl.when(pl.program_id(0) == 0)
    def _():
        def fill(first, second):
            at, to = 0, 0
            for size in (qw // 2, kw // 2, kw // 2):
                cut = slice(at, at + size)
                both = jnp.concatenate(
                    [first[:width, cut].astype(F32), second[:width, cut].astype(F32)], axis=1
                )
                w_ref[:, to : to + 2 * size] = both.astype(BF16)
                extra = jnp.concatenate(
                    [first[width : width + 8, cut].astype(F32), second[width : width + 8, cut].astype(F32)],
                    axis=1,
                )
                bias[:, to : to + 2 * size] = extra
                at += size
                to += 2 * size

        in_order(part_ref[0], mine_ref, theirs_ref, fill)
        for i, a_ref in enumerate((aq_ref, ak_ref, av_ref)):
            w_ref[:, low + i * rank : low + (i + 1) * rank] = a_ref[...]

    values = x_ref[...].astype(F32)
    normed = (values * rms(values) * gain_ref[...]).astype(BF16)
    n_ref[...] = normed
    base = nn(normed, w_ref[...])
    mask = rank_mask(meta_ref[:, 0:1], rank)
    lows = [(base[:, low + i * rank : low + (i + 1) * rank] * mask).astype(BF16) for i in range(3)]
    for i in range(3):
        z_ref[:, i * rank : (i + 1) * rank] = lows[i]
    cos, sin = cos_ref[...], sin_ref[...]
    queries = base[:, :qw] + bias[0:1, :qw] + ADAPTER_SCALE * nt(lows[0], bq_ref[...])
    for pair in range(qw // LANES):
        part = queries[:, pair * LANES : (pair + 1) * LANES]
        turned = (part * cos + turn(part) * sin) * HEAD**-0.5
        q_ref[:, pair * LANES : (pair + 1) * LANES] = turned.astype(BF16)
    keys = base[:, qw : qw + kw] + bias[0:1, qw : qw + kw] + ADAPTER_SCALE * nt(lows[1], bk_ref[...])
    kv_ref[:, :kw] = (keys * cos + turn(keys) * sin).astype(BF16)
    vals = base[:, qw + kw : low] + bias[0:1, qw + kw : low] + ADAPTER_SCALE * nt(lows[2], bv_ref[...])
    kv_ref[:, kw:] = vals.astype(BF16)


def project(part, x, meta, cos, sin, gain, mine, theirs, a_rows, b_rows):
    rows, width = x.shape
    b_q, b_k, _ = b_rows
    qw, kw, rank = b_q.shape[0], b_k.shape[0], b_q.shape[1]
    tile = ROW_TILE
    rest = (gain, mine, theirs, *a_rows, *b_rows)
    outs = [
        jax.ShapeDtypeStruct((rows, width), BF16),
        jax.ShapeDtypeStruct((rows, qw), BF16),
        jax.ShapeDtypeStruct((rows, 2 * kw), BF16),
        jax.ShapeDtypeStruct((rows, 3 * rank), BF16),
        jax.ShapeDtypeStruct((width, qw + 2 * kw + 3 * rank), BF16),
    ]
    return pl.pallas_call(
        project_kernel,
        grid_spec=pltpu.PrefetchScalarGridSpec(
            num_scalar_prefetch=1,
            grid=(rows // tile,),
            in_specs=[row_blocks(a, tile) for a in (x, meta, cos, sin)] + [whole(a) for a in rest],
            out_specs=[row_blocks(o, tile) for o in outs[:4]] + [whole(outs[4])],
            scratch_shapes=[pltpu.VMEM((8, qw + 2 * kw), F32)],
        ),
        out_shape=outs,
        compiler_params=params(),
        cost_estimate=cost(2 * rows * width * 1600, 9e6),
        name="project",
    )(part, x, meta, cos, sin, *rest)


def head_groups(heads, kv_heads):
    width = heads // kv_heads
    groups = {}
    for head in range(heads):
        groups.setdefault((head // width, head % 2), []).append(head)
    return [(kv, half, members) for (kv, half), members in sorted(groups.items())]


def spread_heads(tile_f32, kv, half):
    lanes = lane_iota(tile_f32.shape)
    moved = tile_f32 if kv % 2 == half else pltpu.roll(tile_f32, HEAD, 1)
    keep = (lanes >= HEAD) if half else (lanes < HEAD)
    return jnp.where(keep, moved, 0.0).astype(BF16)


def fill_heads(groups, source, keys_ref, values_ref):
    total = keys_ref.shape[1]
    for start in range(0, total, KEY_TILE):
        part = source(start).astype(F32)
        for number, (kv, half, _) in enumerate(groups):
            keys_ref[number, start : start + KEY_TILE, :] = spread_heads(part[:, :LANES], kv, half)
            values_ref[number, start : start + KEY_TILE, :] = spread_heads(
                part[:, LANES:], kv, half
            )


def attend_kernel(
    heads, kv_heads, bounds_ref, all_ref, meta_ref, metar_ref, own_ref, other_ref, column_ref,
    q_ref, o_ref, log_ref, merged_ref, slot_ref, keys, values, acc, top, total, held,
):
    step = pl.program_id(0)
    groups = head_groups(heads, kv_heads)
    rows = q_ref.shape[0]
    q_ref[...] = nn(pick_rows(meta_ref[:, 0:1], all_ref.shape[0]), all_ref[...]).astype(BF16)

    @pl.when(step == 0)
    def _():
        both = jnp.concatenate([own_ref[...], other_ref[...]], axis=0)

        def merged(start):
            picks = pick_rows(column_ref[start : start + KEY_TILE, :], both.shape[0])
            part = nn(picks, both)
            merged_ref[start : start + KEY_TILE, :] = part.astype(BF16)
            return part

        fill_heads(groups, merged, keys, values)

    acc[...] = jnp.zeros_like(acc)
    total[...] = jnp.zeros_like(total)
    top[...] = jnp.full_like(top, MASKED_SCORE)
    first, last = meta_ref[:, 1:2], meta_ref[:, 2:3]
    offsets = []
    cursor = 0
    for _, _, members in groups:
        offsets.append(cursor)
        cursor += len(members) * rows

    def one_tile(number, carry):
        start = pl.multiple_of(number * KEY_TILE, KEY_TILE)
        index = start + lane_iota((rows, KEY_TILE))
        bias = jnp.where((index >= first) & (index <= last), 0.0, MASKED_SCORE)
        for group, (_, _, members) in enumerate(groups):
            count = len(members)
            span = pl.ds(offsets[group], count * rows)
            stack = jnp.concatenate(
                [q_ref[:, (h // 2) * LANES : (h // 2 + 1) * LANES] for h in members], axis=0
            )
            scores = nt(stack, keys[group, pl.ds(start, KEY_TILE), :])
            scores = scores + jnp.concatenate([bias] * count, axis=0)
            old = top[span, :]
            new = jnp.maximum(old, jnp.max(scores, axis=1, keepdims=True))
            weights = jnp.exp(scores - new)
            shrink = jnp.exp(old - new)
            total[span, :] = total[span, :] * shrink + jnp.sum(weights, axis=1, keepdims=True)
            acc[span, :] = acc[span, :] * shrink + nn(
                weights.astype(BF16), values[group, pl.ds(start, KEY_TILE), :]
            )
            top[span, :] = new
        return carry

    lax.fori_loop(bounds_ref[0, step], bounds_ref[1, step], one_tile, 0)
    pairs = [None] * (heads // 2)
    logs = jnp.zeros((rows, LANES), F32)
    lanes = lane_iota((rows, LANES))
    for group, (_, _, members) in enumerate(groups):
        for at, head in enumerate(members):
            span = pl.ds(offsets[group] + at * rows, rows)
            sums = total[span, :]
            part = acc[span, :] / sums
            logs = jnp.where(lanes == head, top[span, :] + jnp.log(sums), logs)
            pair = head // 2
            pairs[pair] = part if pairs[pair] is None else pairs[pair] + part
    for pair, part in enumerate(pairs):
        o_ref[:, pair * LANES : (pair + 1) * LANES] = part.astype(BF16)
    log_ref[...] = jnp.transpose(logs)[: log_ref.shape[0], :]
    held[pl.ds(pl.multiple_of(step * rows, rows), rows), :] = o_ref[...]

    @pl.when(step == pl.num_programs(0) - 1)
    def _():
        slot_ref[...] = nn(place_rows(metar_ref[0:1, :], held.shape[0]), held[...]).astype(BF16)


def attend(bounds, q, meta, meta_rows, own_kv, other_kv, column, heads, kv_heads):
    rows, qw = q.shape
    tile = QUERY_TILE
    keys = 2 * rows
    groups = len(head_groups(heads, kv_heads))
    outs = [
        jax.ShapeDtypeStruct((rows, qw), BF16),
        jax.ShapeDtypeStruct((rows, qw), BF16),
        jax.ShapeDtypeStruct((16, rows), F32),
        jax.ShapeDtypeStruct((keys, own_kv.shape[1]), BF16),
        jax.ShapeDtypeStruct((rows, qw), BF16),
    ]
    return pl.pallas_call(
        functools.partial(attend_kernel, heads, kv_heads),
        grid_spec=pltpu.PrefetchScalarGridSpec(
            num_scalar_prefetch=1,
            grid=(rows // tile,),
            in_specs=[
                whole(q),
                row_blocks(meta, tile),
                whole(meta_rows),
                whole(own_kv),
                whole(other_kv),
                whole(column),
            ],
            out_specs=[
                row_blocks(outs[0], tile),
                row_blocks(outs[1], tile),
                pl.BlockSpec((16, tile), lambda i, *_: (0, i)),
                whole(outs[3]),
                whole(outs[4]),
            ],
            scratch_shapes=[
                pltpu.VMEM((groups, keys, LANES), BF16),
                pltpu.VMEM((groups, keys, LANES), BF16),
                pltpu.VMEM((heads * tile, LANES), F32),
                pltpu.VMEM((heads * tile, 1), F32),
                pltpu.VMEM((heads * tile, 1), F32),
                pltpu.VMEM((rows, qw), BF16),
            ],
        ),
        out_shape=outs,
        compiler_params=params(),
        cost_estimate=cost(heads * rows * keys * 256, 6e6),
        name="attend",
    )(bounds, q, meta, meta_rows, own_kv, other_kv, column)


def attend_back_kernel(
    heads, kv_heads, bounds_ref, q_ref, all_ref, o_ref, log_ref, meta_ref, metar_ref, cos_ref,
    sin_ref, merged_ref, column_ref, place_ref,
    gq_ref, own_ref, other_ref, keys, values, dkeys, dvalues, dq, dots, g_ref, held,
):
    step = pl.program_id(0)
    groups = head_groups(heads, kv_heads)
    rows = q_ref.shape[0]
    g_ref[...] = nn(pick_rows(meta_ref[:, 0:1], all_ref.shape[0]), all_ref[...]).astype(BF16)

    @pl.when(step == 0)
    def _():
        fill_heads(groups, lambda at: merged_ref[at : at + KEY_TILE, :], keys, values)
        dkeys[...] = jnp.zeros_like(dkeys)
        dvalues[...] = jnp.zeros_like(dvalues)

    dq[...] = jnp.zeros_like(dq)
    for pair in range(heads // 2):
        lanes = slice(pair * LANES, (pair + 1) * LANES)
        product = jnp.transpose(g_ref[:, lanes].astype(F32) * o_ref[:, lanes].astype(F32))
        dots[2 * pair : 2 * pair + 1, :] = jnp.sum(product[:HEAD], axis=0, keepdims=True)
        dots[2 * pair + 1 : 2 * pair + 2, :] = jnp.sum(product[HEAD:], axis=0, keepdims=True)
    first, last = metar_ref[1:2, :], metar_ref[2:3, :]

    def one_tile(number, carry):
        start = pl.multiple_of(number * KEY_TILE, KEY_TILE)
        index = start + row_iota((KEY_TILE, rows))
        bias = jnp.where((index >= first) & (index <= last), 0.0, MASKED_SCORE)
        for group, (_, half, members) in enumerate(groups):
            count = len(members)
            span = pl.ds(start, KEY_TILE)
            cut = [slice((h // 2) * LANES, (h // 2 + 1) * LANES) for h in members]
            stack = jnp.concatenate([q_ref[:, c] for c in cut], axis=0)
            grads = jnp.concatenate([g_ref[:, c] for c in cut], axis=0)
            logs = jnp.concatenate([log_ref[h : h + 1, :] for h in members], axis=1)
            drop = jnp.concatenate([dots[h : h + 1, :] for h in members], axis=1)
            key_part = keys[group, span, :]
            scores = nt(key_part, stack) + jnp.concatenate([bias] * count, axis=1)
            weights = jnp.exp(scores - logs)
            change = nt(values[group, span, :], grads)
            dscores = (weights * (change - drop)).astype(BF16)
            dvalues[group, span, :] += nn(weights.astype(BF16), grads)
            dkeys[group, span, :] += nn(dscores, stack)
            back = tn(dscores, key_part)
            for at, head in enumerate(members):
                dq[head // 2, :, :] += back[at * rows : (at + 1) * rows, :]
        return carry

    lax.fori_loop(bounds_ref[0, step], bounds_ref[1, step], one_tile, 0)
    cos, sin = cos_ref[...], sin_ref[...]
    for pair in range(heads // 2):
        grad = dq[pair, :, :] * HEAD**-0.5
        grad = grad * cos - turn(grad) * sin
        held[
            pl.ds(pl.multiple_of(step * rows, rows), rows), pair * LANES : (pair + 1) * LANES
        ] = grad.astype(BF16)

    @pl.when(step == pl.num_programs(0) - 1)
    def _():
        gq_ref[...] = nn(place_rows(place_ref[0:1, :], held.shape[0]), held[...]).astype(BF16)
        total = dkeys.shape[1]

        def join(ref):
            out = None
            for group, (kv, half, _) in enumerate(groups):
                part = ref[group, :, :]
                lanes = lane_iota(part.shape)
                part = jnp.where((lanes >= HEAD) if half else (lanes < HEAD), part, 0.0)
                if kv % 2 != half:
                    part = pltpu.roll(part, HEAD, 1)
                out = part if out is None else out + part
            return out.astype(BF16)

        both = jnp.concatenate([join(dkeys), join(dvalues)], axis=1)
        half_rows = own_ref.shape[0]
        for at in range(0, total, KEY_TILE):
            hit = (at + row_iota((KEY_TILE, total))) == column_ref[...]
            part = nn(jnp.where(hit, 1.0, 0.0).astype(BF16), both).astype(BF16)
            if at < half_rows:
                own_ref[at : at + KEY_TILE, :] = part
            else:
                other_ref[at - half_rows : at - half_rows + KEY_TILE, :] = part


def attend_back(
    bounds, q, grad, o, logs, meta, meta_rows, cos, sin, merged, column_row, heads, kv_heads
):
    rows, qw = q.shape
    tile = QUERY_TILE
    keys, kvw = merged.shape
    groups = len(head_groups(heads, kv_heads))
    outs = [
        jax.ShapeDtypeStruct((rows, qw), BF16),
        jax.ShapeDtypeStruct((rows, kvw), BF16),
        jax.ShapeDtypeStruct((rows, kvw), BF16),
    ]
    return pl.pallas_call(
        functools.partial(attend_back_kernel, heads, kv_heads),
        grid_spec=pltpu.PrefetchScalarGridSpec(
            num_scalar_prefetch=1,
            grid=(rows // tile,),
            in_specs=[
                row_blocks(q, tile),
                whole(grad),
                row_blocks(o, tile),
                pl.BlockSpec((16, tile), lambda i, *_: (0, i)),
                row_blocks(meta, tile),
                pl.BlockSpec((8, tile), lambda i, *_: (0, i)),
                row_blocks(cos, tile),
                row_blocks(sin, tile),
                whole(merged),
                whole(column_row),
                whole(meta_rows),
            ],
            out_specs=[whole(o) for o in outs],
            scratch_shapes=[
                pltpu.VMEM((groups, keys, LANES), BF16),
                pltpu.VMEM((groups, keys, LANES), BF16),
                pltpu.VMEM((groups, keys, LANES), F32),
                pltpu.VMEM((groups, keys, LANES), F32),
                pltpu.VMEM((heads // 2, tile, LANES), F32),
                pltpu.VMEM((16, tile), F32),
                pltpu.VMEM((tile, qw), BF16),
                pltpu.VMEM((rows, qw), BF16),
            ],
        ),
        out_shape=outs,
        compiler_params=params(),
        cost_estimate=cost(heads * rows * keys * 640, 9e6),
        name="attend_back",
    )(bounds, q, grad, o, logs, meta, meta_rows, cos, sin, merged, column_row, meta_rows)


def middle_kernel(
    part_ref, o_ref, x_ref, meta_ref, mine_ref, theirs_ref, a_ref, b_ref, gain_ref,
    y_ref, n_ref, z_ref, w_ref,
):
    width = x_ref.shape[1]
    rank = b_ref.shape[1]
    half = mine_ref.shape[0]

    @pl.when(pl.program_id(0) == 0)
    def _():
        def fill(first, second):
            w_ref[:half, :width] = first[...]
            w_ref[half:, :width] = second[...]

        in_order(part_ref[0], mine_ref, theirs_ref, fill)
        w_ref[:, width:] = a_ref[...]

    mask = rank_mask(meta_ref[:, 0:1], rank)
    base = nn(o_ref[...], w_ref[...])
    low = (base[:, width:] * mask).astype(BF16)
    z_ref[...] = low
    values = x_ref[...].astype(F32) + (base[:, :width] + ADAPTER_SCALE * nt(low, b_ref[...]))
    y_ref[...] = values
    n_ref[...] = (values * rms(values) * gain_ref[...]).astype(BF16)


def middle(part, o, x, meta, mine, theirs, a_out, b_out, gain):
    rows, width = x.shape
    rank = b_out.shape[1]
    tile = ROW_TILE
    rest = (mine, theirs, a_out, b_out, gain)
    outs = [
        jax.ShapeDtypeStruct((rows, width), F32),
        jax.ShapeDtypeStruct((rows, width), BF16),
        jax.ShapeDtypeStruct((rows, rank), BF16),
        jax.ShapeDtypeStruct((o.shape[1], width + rank), BF16),
    ]
    return pl.pallas_call(
        middle_kernel,
        grid_spec=pltpu.PrefetchScalarGridSpec(
            num_scalar_prefetch=1,
            grid=(rows // tile,),
            in_specs=[row_blocks(a, tile) for a in (o, x, meta)] + [whole(a) for a in rest],
            out_specs=[row_blocks(a, tile) for a in outs[:3]] + [whole(outs[3])],
        ),
        out_shape=outs,
        compiler_params=params(),
        cost_estimate=cost(2 * rows * width * 1100, 12e6),
        name="middle",
    )(part, o, x, meta, *rest)


def finish_kernel(ya_ref, yb_ref, y1_ref, dy_ref, meta_ref, b_ref, out_ref, gb_ref, gacc):
    step = pl.program_id(0)
    width = y1_ref.shape[1]
    rank = b_ref.shape[1]

    @pl.when(step == 0)
    def _():
        gacc[...] = jnp.zeros_like(gacc)

    mask = rank_mask(meta_ref[:, 0:1], rank)
    low = ((ya_ref[:, width:] + yb_ref[:, width:].astype(F32)) * mask).astype(BF16)
    values = y1_ref[...] + (
        (ya_ref[:, :width] + yb_ref[:, :width].astype(F32)) + ADAPTER_SCALE * nt(low, b_ref[...])
    )
    out_ref[...] = values.astype(BF16)
    gacc[...] += ADAPTER_SCALE * tn(dy_ref[...], low)

    @pl.when(step == pl.num_programs(0) - 1)
    def _():
        gb_ref[...] = gacc[...].astype(gb_ref.dtype)


def finish(y_first, y_second, y1, dy, meta, b_down):
    rows, width = y1.shape
    rank = b_down.shape[1]
    tile = ROW_TILE
    outs = [
        jax.ShapeDtypeStruct((rows, width), BF16),
        jax.ShapeDtypeStruct((width, rank), BF16),
    ]
    return pl.pallas_call(
        finish_kernel,
        grid=(rows // tile,),
        in_specs=[row_blocks(a, tile) for a in (y_first, y_second, y1, dy, meta)] + [whole(b_down)],
        out_specs=[row_blocks(outs[0], tile), whole(outs[1])],
        out_shape=outs,
        scratch_shapes=[pltpu.VMEM((width, rank), F32)],
        compiler_params=params(),
        cost_estimate=cost(2 * rows * width * 512, 11e6),
        name="finish",
    )(y_first, y_second, y1, dy, meta, b_down)


def middle_back_kernel(
    da_ref, db_ref, y1_ref, dy_ref, n_ref, o_ref, z_ref, meta_ref, a_ref, b_ref, w_ref, gain_ref,
    dy1_ref, dar_ref, ga_ref, gbo_ref, gao_ref, acc_a, acc_bo, acc_ao,
):
    step = pl.program_id(0)
    width = y1_ref.shape[1]
    rank = b_ref.shape[1]

    @pl.when(step == 0)
    def _():
        acc_a[...] = jnp.zeros_like(acc_a)
        acc_bo[...] = jnp.zeros_like(acc_bo)
        acc_ao[...] = jnp.zeros_like(acc_ao)

    mask = rank_mask(meta_ref[:, 0:1], rank)
    back = da_ref[:, width:] + db_ref[:, width:].astype(F32)
    back = (back * jnp.concatenate([mask, mask], axis=1)).astype(BF16)
    grad = da_ref[:, :width] + db_ref[:, :width].astype(F32) + nt(back, a_ref[...])
    values = y1_ref[...]
    dy1 = dy_ref[...].astype(F32) + norm_back(values, gain_ref[...], grad)
    dy1_ref[...] = dy1
    low_grad = dy1.astype(BF16)
    back_out = (ADAPTER_SCALE * nn(low_grad, b_ref[...]) * mask).astype(BF16)
    both = jnp.concatenate([low_grad, back_out], axis=1)
    dar_ref[...] = nt(both, w_ref[...]).astype(BF16)
    acc_a[...] += tn(n_ref[...], back)
    acc_bo[...] += ADAPTER_SCALE * tn(low_grad, z_ref[...])
    acc_ao[...] += tn(o_ref[...], back_out)

    @pl.when(step == pl.num_programs(0) - 1)
    def _():
        ga_ref[...] = acc_a[...].astype(ga_ref.dtype)
        gbo_ref[...] = acc_bo[...].astype(gbo_ref.dtype)
        gao_ref[...] = acc_ao[...].astype(gao_ref.dtype)


def middle_back(d_first, d_second, y1, dy, n2, o, z, meta, a_pair, b_out, w_out, gain):
    rows, width = y1.shape
    rank = b_out.shape[1]
    qw = o.shape[1]
    tile = ROW_TILE
    outs = [
        jax.ShapeDtypeStruct((rows, width), F32),
        jax.ShapeDtypeStruct((rows, qw), BF16),
        jax.ShapeDtypeStruct((width, 2 * rank), BF16),
        jax.ShapeDtypeStruct((width, rank), BF16),
        jax.ShapeDtypeStruct((qw, rank), BF16),
    ]
    return pl.pallas_call(
        middle_back_kernel,
        grid=(rows // tile,),
        in_specs=[row_blocks(a, tile) for a in (d_first, d_second, y1, dy, n2, o, z, meta)]
        + [whole(a) for a in (a_pair, b_out, w_out, gain)],
        out_specs=[row_blocks(a, tile) for a in outs[:2]] + [whole(a) for a in outs[2:]],
        out_shape=outs,
        scratch_shapes=[
            pltpu.VMEM((width, 2 * rank), F32),
            pltpu.VMEM((width, rank), F32),
            pltpu.VMEM((qw, rank), F32),
        ],
        compiler_params=params(),
        cost_estimate=cost(2 * rows * width * 1900, 20e6),
        name="middle_back",
    )(d_first, d_second, y1, dy, n2, o, z, meta, a_pair, b_out, w_out, gain)


def feed_kernel(
    theirs, n_ref, dy_ref, meta_ref, ap_ref, bd_ref, wg_hbm, wu_hbm, wd_hbm, bg_hbm, bu_hbm, ad_hbm,
    *more,
):
    if theirs:
        grad_hbm, y_ref, d_got, gbg_ref, gbu_ref, gad_ref = more[:6]
        (wga, wua, wda, raw, grads, xg, xu, dya, yacc, dacc, wsem, gsem, held, ssem, rsem) = more[6:]
    else:
        y_ref, d_ref, grad_out = more[:3]
        wga, wua, wda, raw, grads, xg, xu, dya, yacc, dacc, wsem = more[3:]
    step = pl.program_id(0)
    steps = pl.num_programs(0)
    width, half = wg_hbm.shape
    rank = bd_ref.shape[1]
    rows = n_ref.shape[0]
    tile = HIDDEN_TILE
    tiles = pl.cdiv(half, tile)
    lap = tiles * tile - half

    def loads(number):
        at = pl.multiple_of(jnp.minimum(number * tile, half - tile), LANES)
        to = pl.multiple_of(number * tile, tile)
        here, there = pl.ds(at, tile), pl.ds(to, tile)
        top, side = pl.ds(0, width), pl.ds(width, rank)
        pairs = [
            (wg_hbm.at[:, here], wga.at[top, there]),
            (wu_hbm.at[:, here], wua.at[top, there]),
            (wd_hbm.at[here, :], wda.at[there, top]),
            (bg_hbm.at[here, :], raw.at[0, there, :]),
            (bu_hbm.at[here, :], raw.at[1, there, :]),
            (ad_hbm.at[here, :], wda.at[there, side]),
        ]
        return [
            pltpu.make_async_copy(source, target, wsem.at[number, at])
            for at, (source, target) in enumerate(pairs)
        ]

    if theirs:
        place, part = lax.axis_index("dp"), lax.axis_index("tensor")

        def reply(number):
            return pltpu.make_async_remote_copy(
                src_ref=held.at[number],
                dst_ref=d_got.at[number],
                send_sem=ssem.at[number],
                recv_sem=rsem.at[number],
                device_id=(place, 1 - part),
                device_id_type=MESH,
            )

        @pl.when(step == 0)
        def _():
            barrier = pltpu.get_barrier_semaphore()
            pl.semaphore_signal(barrier, inc=1, device_id=(place, 1 - part), device_id_type=MESH)
            pl.semaphore_wait(barrier, 1)

    @pl.when(step == 0)
    def _():
        for number in range(tiles):
            for copy in loads(number):
                copy.start()
        if theirs:
            copy = pltpu.make_async_copy(grad_hbm, grads, gsem)
            copy.start()
            copy.wait()
        else:
            grads[...] = jnp.zeros_like(grads)

    mask = rank_mask(meta_ref[:, 0:1], rank)
    normed = n_ref[...]
    lows = nn(normed, ap_ref[...])
    xg[:, :width] = normed
    xu[:, :width] = normed
    xg[:, width:] = (lows[:, :rank] * mask).astype(BF16)
    xu[:, width:] = (lows[:, rank:] * mask).astype(BF16)
    dya[:, :width] = dy_ref[...]
    dya[:, width:] = (ADAPTER_SCALE * nn(dy_ref[...], bd_ref[...]) * mask).astype(BF16)
    yacc[...] = jnp.zeros_like(yacc)
    dacc[...] = jnp.zeros_like(dacc)

    def hidden(number, carry):
        span = pl.ds(pl.multiple_of(number * tile, tile), tile)

        @pl.when(step == 0)
        def _():
            for copy in loads(number):
                copy.wait()
            for at, target in enumerate((wga, wua)):
                turned = jnp.transpose(raw[at, span, :].astype(F32) * ADAPTER_SCALE)
                target[width:, span] = turned.astype(BF16)
            if lap:

                @pl.when(number == tiles - 1)
                def _():
                    edge = slice((tiles - 1) * tile, (tiles - 1) * tile + lap)
                    wga[:, edge] = jnp.zeros((width + rank, lap), BF16)
                    wua[:, edge] = jnp.zeros((width + rank, lap), BF16)
                    wda[edge, :] = jnp.zeros((lap, width + rank), BF16)

        gate = nn(xg[...], wga[:, span])
        up = nn(xu[...], wua[:, span])
        dhid = nt(dya[...], wda[span, :])
        sig = 1.0 / (1.0 + jnp.exp(-gate))
        silu = gate * sig
        hid = (silu * up).astype(BF16)
        dg = (dhid * up * (sig * (1.0 + gate * (1.0 - sig)))).astype(BF16)
        du = (dhid * silu).astype(BF16)
        yacc[...] += nn(hid, wda[span, :])
        dga = nt(dg, wga[:, span])
        dua = nt(du, wua[:, span])
        dacc[:, :width] += dga[:, :width] + dua[:, :width]
        dacc[:, width : width + rank] += dga[:, width:]
        dacc[:, width + rank :] += dua[:, width:]
        grads[0, span, :] += ADAPTER_SCALE * tn(dg, xg[:, width:])
        grads[1, span, :] += ADAPTER_SCALE * tn(du, xu[:, width:])
        grads[2, span, :] += tn(hid, dya[:, width:])
        return carry

    lax.fori_loop(0, tiles, hidden, 0)
    y_ref[...] = yacc[...].astype(y_ref.dtype)
    if not theirs:
        d_ref[...] = dacc[...]

        @pl.when(step == steps - 1)
        def _():
            grad_out[...] = grads[...]

        return
    held[step] = dacc[...].astype(BF16)
    reply(step).start()

    @pl.when(step == steps - 1)
    def _():
        last = (tiles - 1) * tile
        for at, target in enumerate((gbg_ref, gbu_ref, gad_ref)):
            target[:last, :] = grads[at, :last, :].astype(BF16)
            target[last:, :] = grads[at, last + lap : tiles * tile, :].astype(BF16)
        for number in range(held.shape[0]):
            reply(number).wait_send()
        for number in range(held.shape[0]):
            reply(number).wait_recv()


def feed(n2, dy, meta, a_pair, b_down, w_gate, w_up, w_down, b_gate, b_up, a_down, grads=None):
    rows, width = n2.shape
    half, rank = a_down.shape
    tile = ROW_TILE
    tiles = pl.cdiv(half, HIDDEN_TILE)
    padded = tiles * HIDDEN_TILE
    theirs = grads is not None
    anywhere = pl.BlockSpec(memory_space=pl.ANY)
    wide, deep = width + rank, width + 2 * rank
    args = [n2, dy, meta, a_pair, b_down, w_gate, w_up, w_down, b_gate, b_up, a_down]
    in_specs = [row_blocks(a, tile) for a in args[:3]] + [whole(a) for a in args[3:5]] + [anywhere] * 6
    scratch = [
        pltpu.VMEM((wide, padded), BF16),
        pltpu.VMEM((wide, padded), BF16),
        pltpu.VMEM((padded, wide), BF16),
        pltpu.VMEM((2, padded, rank), BF16),
        pltpu.VMEM((3, padded, rank), F32),
        pltpu.VMEM((tile, wide), BF16),
        pltpu.VMEM((tile, wide), BF16),
        pltpu.VMEM((tile, wide), BF16),
        pltpu.VMEM((tile, wide), F32),
        pltpu.VMEM((tile, deep), F32),
        pltpu.SemaphoreType.DMA((tiles, 6)),
    ]
    if theirs:
        args.append(grads)
        in_specs.append(anywhere)
        thin = jax.ShapeDtypeStruct((half, rank), BF16)
        outs = [
            jax.ShapeDtypeStruct((rows, wide), BF16),
            jax.ShapeDtypeStruct((rows // tile, tile, deep), BF16),
            thin,
            thin,
            thin,
        ]
        out_specs = [row_blocks(outs[0], tile), anywhere] + [whole(thin)] * 3
        scratch += [
            pltpu.SemaphoreType.DMA,
            pltpu.VMEM((rows // tile, tile, deep), BF16),
            pltpu.SemaphoreType.DMA((rows // tile,)),
            pltpu.SemaphoreType.DMA((rows // tile,)),
        ]
        extra = dict(collective_id=1, has_side_effects=True)
    else:
        outs = [
            jax.ShapeDtypeStruct((rows, wide), F32),
            jax.ShapeDtypeStruct((rows, deep), F32),
            jax.ShapeDtypeStruct((3, padded, rank), F32),
        ]
        out_specs = [row_blocks(outs[0], tile), row_blocks(outs[1], tile), whole(outs[2])]
        extra = {}
    return pl.pallas_call(
        functools.partial(feed_kernel, theirs),
        grid=(rows // tile,),
        in_specs=in_specs,
        out_specs=out_specs,
        out_shape=outs,
        scratch_shapes=scratch,
        compiler_params=params(**extra),
        cost_estimate=cost(2 * rows * half * (6 * width + 9 * rank), 30e6),
        name="feed_theirs" if theirs else "feed_own",
    )(*args)


def input_kernel(
    gq_ref, own_ref, got_ref, x_ref, n_ref, z_ref, dy1_ref, meta_ref, cos_ref, sin_ref,
    gain_ref, w_ref, bq_ref, bk_ref, bv_ref,
    out_ref, ga_ref, gb_ref, acc_a, acc_b,
):
    step = pl.program_id(0)
    qw, kw, rank = bq_ref.shape[0], bk_ref.shape[0], bq_ref.shape[1]

    @pl.when(step == 0)
    def _():
        acc_a[...] = jnp.zeros_like(acc_a)
        acc_b[...] = jnp.zeros_like(acc_b)

    mask = rank_mask(meta_ref[:, 0:1], rank)
    both = own_ref[...].astype(F32) + got_ref[...].astype(F32)
    dk = both[:, :kw]
    gq = gq_ref[...]
    gk = (dk * cos_ref[...] - turn(dk) * sin_ref[...]).astype(BF16)
    gv = both[:, kw:].astype(BF16)
    backs = [
        (ADAPTER_SCALE * nn(g, b[...]) * mask).astype(BF16)
        for g, b in ((gq, bq_ref), (gk, bk_ref), (gv, bv_ref))
    ]
    grads = jnp.concatenate([gq, gk, gv] + backs, axis=1)
    dn = nt(grads, w_ref[...])
    values = x_ref[...].astype(F32)
    dx = dy1_ref[...] + norm_back(values, gain_ref[...], dn)
    out_ref[...] = dx.astype(BF16)
    acc_a[...] += tn(n_ref[...], jnp.concatenate(backs, axis=1))
    low = z_ref[...]
    acc_b[:qw, :] += tn(gq, low[:, :rank])
    acc_b[qw : qw + kw, :] += tn(gk, low[:, rank : 2 * rank])
    acc_b[qw + kw :, :] += tn(gv, low[:, 2 * rank :])

    @pl.when(step == pl.num_programs(0) - 1)
    def _():
        ga_ref[...] = acc_a[...].astype(ga_ref.dtype)
        gb_ref[...] = (ADAPTER_SCALE * acc_b[...]).astype(gb_ref.dtype)


def input_back(gq, own, got, x, n1, z, dy1, meta, cos, sin, gain, w_cat, b_q, b_k, b_v):
    rows, width = x.shape
    qw, kw, rank = b_q.shape[0], b_k.shape[0], b_q.shape[1]
    tile = ROW_TILE
    outs = [
        jax.ShapeDtypeStruct((rows, width), BF16),
        jax.ShapeDtypeStruct((width, 3 * rank), BF16),
        jax.ShapeDtypeStruct((qw + 2 * kw, rank), BF16),
    ]
    return pl.pallas_call(
        input_kernel,
        grid=(rows // tile,),
        in_specs=[row_blocks(a, tile) for a in (gq, own, got, x, n1, z, dy1, meta, cos, sin)]
        + [whole(a) for a in (gain, w_cat, b_q, b_k, b_v)],
        out_specs=[row_blocks(outs[0], tile)] + [whole(a) for a in outs[1:]],
        out_shape=outs,
        scratch_shapes=[
            pltpu.VMEM((width, 3 * rank), F32),
            pltpu.VMEM((qw + 2 * kw, rank), F32),
        ],
        compiler_params=params(),
        cost_estimate=cost(2 * rows * width * 2900, 14e6),
        name="input_back",
    )(gq, own, got, x, n1, z, dy1, meta, cos, sin, gain, w_cat, b_q, b_k, b_v)


def row_tables(order_row, lengths_row, adapter_row, part, parts, each):
    total = order_row.shape[0]
    piece = each // parts
    local = total // parts
    places = jnp.arange(total, dtype=I32)
    own = (order_row % each) // piece == part
    slot = (order_row // each) * piece + order_row % piece
    column = jnp.where(own, slot, local + slot)
    upto = jnp.sum((own[None, :] & (places[None, :] <= places[:, None])).astype(I32), axis=1)
    rank = jnp.where(own, upto - 1, total)
    picks = rank[None, :] == jnp.arange(local, dtype=I32)[:, None]
    sorted_place = jnp.sum(jnp.where(picks, places[None, :], 0), axis=1)
    sorted_slot = jnp.sum(jnp.where(picks, slot[None, :], 0), axis=1)
    slot_place = jnp.sum(jnp.where(column[None, :] == places[:, None], places[None, :], 0), axis=1)
    ends = jnp.cumsum(lengths_row)
    starts = ends - lengths_row
    both = jnp.concatenate([slot_place, sorted_place])
    member = (both[:, None] >= starts[None, :]) & (both[:, None] < ends[None, :])
    first = jnp.sum(jnp.where(member, starts[None, :], 0), axis=1)
    chosen = jnp.sum(jnp.where(member, adapter_row[None, :], 0), axis=1)
    position = both - first
    sorted_first = first[total:]
    bounds = jnp.stack(
        [
            sorted_first[::QUERY_TILE] // KEY_TILE,
            sorted_place[QUERY_TILE - 1 :: QUERY_TILE] // KEY_TILE + 1,
        ]
    )
    blank = jnp.zeros_like(sorted_place)
    meta_sorted = jnp.stack([sorted_slot, sorted_first, sorted_place] + [blank] * 5, axis=1)
    meta_rows = jnp.stack([sorted_slot, sorted_first, sorted_place] + [blank] * 5, axis=0)
    meta_own = jnp.broadcast_to(chosen[:local, None], (local, 8))
    meta_other = jnp.broadcast_to(chosen[local:total, None], (local, 8))
    slot_position = position[:local]
    return (
        meta_own, meta_other, meta_sorted, meta_rows, slot_position, position[total:], column, bounds,
    )


def rope_tables(position):
    freq_index = jnp.arange(HEAD // 2, dtype=F32)
    inv_freq = jnp.power(jnp.float32(ROPE_BASE), -2.0 * freq_index / HEAD)
    angles = position.astype(F32)[:, None] * inv_freq[None, :]
    return (
        jnp.concatenate([jnp.cos(angles)] * 4, axis=1),
        jnp.concatenate([jnp.sin(angles)] * 4, axis=1),
    )


def per_device(
    tokens, cotangent, order, lengths, adapter_ids, norm_gains, w_query, w_key, w_value,
    b_query, b_key, b_value, w_out, w_gate, w_up, w_down, adapters, first_moment, second_moment,
):
    parts = lax.axis_size("tensor")
    part = lax.axis_index("tensor")
    devices = lax.axis_size("dp")
    place = lax.axis_index("dp")
    total, width = tokens.shape
    each = total // devices
    piece = each // parts
    local = total // parts
    rank = adapters.shape[1]
    own_rows = adapters.shape[0]
    swap = [(i, parts - 1 - i) for i in range(parts)]
    first_part = part == 0

    def across(values):
        return lax.ppermute(values, "tensor", swap)

    def pair(mine, theirs, axis):
        return jnp.concatenate(
            [jnp.where(first_part, mine, theirs), jnp.where(first_part, theirs, mine)], axis=axis
        )

    def give_back(values):
        got = lax.all_to_all(
            values.reshape(devices, piece, width), "dp", split_axis=0, concat_axis=0, tiled=True
        )
        theirs = across(got)
        return pair(got[:, None], theirs[:, None], 1).reshape(total, width)

    qh, kh, half = w_query.shape[1], w_key.shape[1], w_gate.shape[1]
    qw, kw, hidden = parts * qh, parts * kh, parts * half
    heads, kv_heads = qw // HEAD, kw // HEAD
    mine_qkv = jnp.concatenate(
        [
            jnp.concatenate([w_query, w_key, w_value], axis=1),
            jnp.broadcast_to(
                jnp.concatenate([b_query, b_key, b_value])[None], (32, qh + 2 * kh)
            ),
        ],
        axis=0,
    )
    lines = mine_qkv.shape[0]
    moved, copies, their_qkv, their_out = front(
        tokens.reshape(devices, parts, piece, width),
        adapters.astype(BF16),
        mine_qkv.reshape(2, lines // 2, -1),
        w_out.reshape(2, w_out.shape[0] // 2, width),
        devices,
    )
    moved = moved.reshape(local, width)
    sent = cotangent.reshape(devices, parts, piece, width)
    sent = lax.dynamic_index_in_dim(sent, part, 1, keepdims=False)
    dy = lax.all_to_all(sent, "dp", split_axis=0, concat_axis=0, tiled=True).reshape(local, width)
    dy_theirs = across(dy)

    sizes = (width, qw, width, kw, width, kw, qw, width, width, hidden, width, hidden, hidden, width)
    early = 3 * width + qw + 2 * kw
    lead = pl.cdiv(early, own_rows)
    flat = copies[:lead].reshape(lead * own_rows, rank)
    late_flat = copies.reshape(2 * devices * own_rows, rank)
    sections = []
    cursor = 0
    for number, size in enumerate(sizes):
        source = flat if number < 6 else late_flat
        sections.append(source[cursor : cursor + size])
        cursor += size
    a_q, b_q, a_k, b_k, a_v, b_v, a_o, b_o, a_g, b_g, a_u, b_u, a_d, b_d = sections

    def near(rows):
        return lax.dynamic_slice_in_dim(rows, part * half, half, 0)

    meta_own, meta_other, meta_sorted, meta_rows, slot_position, sorted_position, column, bounds = (
        row_tables(order[0], lengths[0], adapter_ids[0], part, parts, each)
    )
    cos, sin = rope_tables(slot_position)
    cos_sorted, sin_sorted = rope_tables(sorted_position)
    gain_one = norm_gains[0:1].astype(F32)
    gain_two = norm_gains[1:2].astype(F32)
    side = jnp.reshape(part, (1,)).astype(I32)
    a_pair = jnp.concatenate([a_g, a_u], axis=1)

    n1, q, kv, z, w_cat = project(
        side, moved, meta_own, cos, sin, gain_one, mine_qkv, their_qkv.reshape(mine_qkv.shape),
        (a_q, a_k, a_v), (b_q, b_k, b_v),
    )
    other_kv = across(kv)
    q_sorted, o_sorted, logs, merged, o = attend(
        bounds, q, meta_sorted, meta_rows, kv, other_kv, column[:, None], heads, kv_heads
    )
    y1, n2, z_out, w_out_cat = middle(
        side, o, moved, meta_own, w_out, their_out.reshape(w_out.shape), a_o, b_o, gain_two
    )
    n2_theirs = across(n2)
    share = (a_pair, b_d, w_gate, w_up, w_down, near(b_g), near(b_u), near(a_d))
    y_own, d_own, grads = feed(n2, dy, meta_own, *share)
    y_theirs, d_got, grad_b_g, grad_b_u, grad_a_d = feed(
        n2_theirs, dy_theirs, meta_other, *share, grads
    )
    y_got = across(y_theirs)
    d_got = d_got.reshape(local, -1)
    dy1, dar, grad_pair, grad_b_o, grad_a_o = middle_back(
        d_own, d_got, y1, dy, n2, o, z_out, meta_own, a_pair, b_o, w_out_cat, gain_two
    )
    out_rows, grad_b_d = finish(y_own, y_got, y1, dy, meta_own, b_d)
    layer_out = give_back(out_rows)
    gq, dkv_own, dkv_other = attend_back(
        bounds, q_sorted, dar, o_sorted, logs, meta_sorted, meta_rows, cos_sorted, sin_sorted,
        merged, column[None, :], heads, kv_heads,
    )
    dkv_got = across(dkv_other)
    dx_rows, grad_a_qkv, grad_b_qkv = input_back(
        gq, dkv_own, dkv_got, moved, n1, z, dy1, meta_own, cos, sin, gain_one, w_cat, b_q, b_k, b_v
    )
    input_grad = give_back(dx_rows)

    def spread(rows):
        blank = jnp.zeros_like(rows)
        return pair(rows, blank, 0)

    everything = jnp.concatenate(
        [
            grad_a_qkv[:, :rank],
            grad_b_qkv[:qw],
            grad_a_qkv[:, rank : 2 * rank],
            grad_b_qkv[qw : qw + kw],
            grad_a_qkv[:, 2 * rank :],
            grad_b_qkv[qw + kw :],
            grad_a_o,
            grad_b_o,
            grad_pair[:, :rank],
            spread(grad_b_g),
            grad_pair[:, rank:],
            spread(grad_b_u),
            spread(grad_a_d),
            grad_b_d,
        ],
        axis=0,
    )
    reduced = lax.psum_scatter(
        everything, ("dp", "tensor"), scatter_dimension=0, tiled=True
    ).astype(F32)
    moment_one = BETA_ONE * first_moment + (1.0 - BETA_ONE) * reduced
    moment_two = BETA_TWO * second_moment + (1.0 - BETA_TWO) * reduced * reduced
    corrected_one = moment_one / (1.0 - BETA_ONE**STEP)
    corrected_two = moment_two / (1.0 - BETA_TWO**STEP)
    updated = adapters - LEARN_RATE * (
        corrected_one / (jnp.sqrt(corrected_two) + ADAM_EPS) + WEIGHT_DECAY * adapters
    )
    return (
        layer_out,
        input_grad,
        reduced,
        moment_one,
        moment_two,
        updated,
        updated.astype(BF16),
    )


def solution(mesh):
    both = P(("dp", "tensor"), None)
    rows = P("dp", None)
    return jax.shard_map(
        per_device,
        mesh=mesh,
        in_specs=(rows, rows, rows, rows, rows, P())
        + (P(None, "tensor"),) * 3
        + (P("tensor"),) * 3
        + (P("tensor", None), P(None, "tensor"), P(None, "tensor"), P("tensor", None))
        + (both,) * 3,
        out_specs=(rows, rows) + (both,) * 5,
        check_vma=False,
    )
```

time: 775 us -> 670 us (0.86)
  waiting for transfers between devices: 202 us -> 58.8 us
  Pallas kernels: 204 us -> 298 us
  other arithmetic: 51 us -> 31.1 us
  starting transfers between devices: 74.3 us -> 57.9 us
  between operations: 14.8 us -> 1.63 us
    ppermute x10 -> x7, waiting for transfers between devices: 163 us -> 17.8 us  [across(): return lax.ppermute(values, 'tensor', swap)]
    pallas_call x5, Pallas kernels: 96.9 us -> 176 us  [the longest x2 100 us: feed(): pl.pallas_call(functools.partial(feed_kernel, theirs), grid=(rows // tile...]
    ppermute x10 -> x7, starting transfers between devices: 35.5 us -> 6.31 us  [across(): return lax.ppermute(values, 'tensor', swap)]
    all_to_all x2, starting transfers between devices: 20.2 us -> 35.8 us  [give_back(): lax.all_to_all(values.reshape(devices, piece, width), 'dp', split_axis=0,...]
    pallas_call x1, Pallas kernels: 41.2 us -> 53.3 us  [attend(): pl.pallas_call(functools.partial(attend_kernel, heads, kv_heads), grid_sp...]
    select_n x10 -> x5, other arithmetic: 17.9 us -> 6.39 us  [the longest x2 3.61 us: pair(): jnp.where(first_part, mine, theirs)]
    concatenate x9 -> x5, other arithmetic: 14.4 us -> 3.09 us  [the longest x1 2.45 us: per_device(): jnp.concatenate([jnp.concatenate([w_query, w_key, w_value], axis=1), jnp....]
    reshape x3 -> x2, local copies, waits for them, and re-layouts: 0.25 us -> 10.2 us  [the longest x1 7.89 us: per_device(): late_flat = copies.reshape(2 * devices * own_rows, rank)]
  transfers between devices with their start and end apart: 20 -> 11, of which waited for: 6 -> 5; matrix products, arithmetic and copies ran while one was open for 34% -> 32% of each run, Pallas kernels for 5% -> 18%
where the time goes in v2:
time: 670 us; the launch traced here: 663 us
  Pallas kernels  298 us (44%)
  blocking collectives  159 us (24%)
  waiting for transfers between devices  58.8 us (9%)
  starting transfers between devices  57.9 us (9%)
  local copies, waits for them, and re-layouts  57.1 us (9%)
  other arithmetic  31.1 us (5%)
    unnamed x1, blocking collectives  159 us
    pallas_call x2, Pallas kernels, feed(): pl.pallas_call(functools.partial(feed_kernel, theirs), grid=(rows // tile...  100 us
    pallas_call x1, Pallas kernels, front(): pl.pallas_call(functools.partial(front_kernel, devices), in_specs=[anywhe...  58.1 us
    pallas_call x1, Pallas kernels, attend(): pl.pallas_call(functools.partial(attend_kernel, heads, kv_heads), grid_sp...  53.3 us
    pallas_call x1, Pallas kernels, attend_back(): pl.pallas_call(functools.partial(attend_back_kernel, heads, kv_heads), gr...  41.5 us
    all_to_all x2, waiting for transfers between devices, give_back(): lax.all_to_all(values.reshape(devices, piece, width), 'dp', split_axis=0,...  37.9 us
    all_to_all x2, starting transfers between devices, give_back(): lax.all_to_all(values.reshape(devices, piece, width), 'dp', split_axis=0,...  35.8 us
    unnamed x77, local copies, waits for them, and re-layouts  19 us
  transfers between devices with their start and end apart: 11, of which 5 were waited for; matrix products, arithmetic and copies ran while one was open for 32% of the time, Pallas kernels for 18%

profile of v2, /device:TPU:1, one launch (start us, length us, event | category | flops | bytes accessed | tf_op | source)
XLA Modules:
  0.0 663.4 jit_solution(16813759027552080534)
XLA Ops:
  0.7 2.4 copy.68
  7.0 2.5 pad_maximum_fusion.2.mine_ref
  9.4 58.1 %front.1 = (bf16[16,48,896]{2,1,0:T(8,128)(2,1)}, bf16[32,716,128]{2,1,0:T(8,128)(2,1)}, bf16[2,464,576]{2,1,0:T(8,128)(2,1)}, bf16[2,224,896]{2,1,0:T(8,128)(2,1)}) custom-call(bf16[16,2,48,896]{3,2,1,0:T(8,128)(2,1)} %bitcast.52, bf16[716,128]{1,0:T(8,128)(2,1)} %convert_element_type.25.chunk_ref, bf16[2,464,576]{2,1,0:T(8,128)(2,1)} %bitcast.49, ...), custom_call_target="tpu_custom_call" | custom-call | bytes 100000000 | tf_op jit(solution)/shard_map/front/pallas_call | solution.py:272
  67.6 2.3 slice.102
  69.9 2.3 reshape.231
  72.2 2.2 fusion.21
  80.3 3.8 multiply_sine_fusion
  86.6 10.1 %project.1 = (bf16[768,896]{1,0:T(8,128)(2,1)}, bf16[768,896]{1,0:T(8,128)(2,1)}, bf16[768,256]{1,0:T(8,128)(2,1)}, bf16[768,384]{1,0:T(8,128)(2,1)}, bf16[896,1536]{1,0:T(8,128)(2,1)}) custom-call(s32[1]{0:T(128)} %bitcast.part_ref, bf16[768,896]{1,0:T(8,128)(2,1)} %bitcast.60, s32[768,8]{1,0:T(8,128)} %broadcast_in_dim.109.meta_ref, ...), custom_call_target="tpu_custom_call" | custom-call | flops 2202009600 | bytes 9000000 | tf_op jit(solution)/shard_map/project/pallas_call | solution.py:367
  98.4 13.6 %all-to-all-start = ((bf16[16,48,896]{2,1,0:T(8,128)(2,1)}), bf16[16,48,896]{2,1,0:T(8,128)(2,1)S(1)}, u32[]{:S(2)}, u32[]{:S(2)}) async-start(bf16[16,48,896]{2,1,0:T(8,128)(2,1)} %dynamic-slice_bitcast_fusion), calls=%async_computation | async-start | bytes 2752512 | tf_op jit(solution)/shard_map/all_to_all | solution.py:1204
  112.7 7.9 %reshape.233 = bf16[22912,128]{1,0:T(8,128)(2,1)} reshape(bf16[32,716,128]{2,1,0:T(8,128)(2,1)} %get-tuple-element.48) | data formatting | bytes 11730944 | tf_op jit(solution)/shard_map/reshape | solution.py:1211
  123.3 4.0 fusion.18
  127.4 2.3 fusion.19
  133.1 2.0 add_select_fusion.column_ref
  137.4 2.4 constant_dynamic-slice_fusion
  139.8 53.3 %attend.1 = (bf16[768,896]{1,0:T(8,128)(2,1)}, bf16[768,896]{1,0:T(8,128)(2,1)}, f32[16,768]{1,0:T(8,128)}, bf16[1536,256]{1,0:T(8,128)(2,1)}, bf16[768,896]{1,0:T(8,128)(2,1)}) custom-call(s32[2,6]{1,0:T(2,128)} %pad_add_fusion.1.bounds_ref, bf16[768,896]{1,0:T(8,128)(2,1)} %get-tuple-element.49.all_ref, s32[768,8]{1,0:T(8,128)} %copy.82.meta_ref, ...), custom_call_target="tpu_custom_call" | custom-call | flops 4227858432 | bytes 6000000 | tf_op jit(solution)/shard_map/attend/pallas_call | solution.py:497
  193.1 7.2 %middle.1 = (f32[768,896]{1,0:T(8,128)}, bf16[768,896]{1,0:T(8,128)(2,1)}, bf16[768,128]{1,0:T(8,128)(2,1)}, bf16[896,1024]{1,0:T(8,128)(2,1)}) custom-call(s32[1]{0:T(128)} %bitcast.part_ref, bf16[768,896]{1,0:T(8,128)(2,1)} %get-tuple-element.51.o_ref, bf16[768,896]{1,0:T(8,128)(2,1)} %bitcast.61, s32[768,8]{1,0:T(8,128)} %broadcast_in_dim.109.meta_ref, ...), custom_call_target="tpu_custom_call" | custom-call | flops 1513881600 | bytes 12000000 | tf_op jit(solution)/shard_map/middle/pallas_call | solution.py:703
  201.7 39.9 %feed_own.1 = (f32[768,1024]{1,0:T(8,128)}, f32[768,1152]{1,0:T(8,128)}, f32[3,2560,128]{2,1,0:T(8,128)}) custom-call(bf16[768,896]{1,0:T(8,128)(2,1)} %get-tuple-element.53.n_ref, bf16[768,896]{1,0:T(8,128)(2,1)} %bitcast.46, s32[768,8]{1,0:T(8,128)} %broadcast_in_dim.109.meta_ref, bf16[896,256]{1,0:T(8,128)(2,1)} %pad_maximum_fusion.3.ap_ref.a_ref, ...), custom_call_target="tpu_custom_call" | custom-call | flops 24385683456 | bytes 30000000 | tf_op jit(solution)/shard_map/feed_own/pallas_call | solution.py:1021
  241.7 12.4 %collective-permute-done.2.dy_ref = bf16[768,896]{1,0:T(8,128)(2,1)} collective-permute-done((bf16[768,896]{1,0:T(8,128)(2,1)S(1)}, bf16[768,896]{1,0:T(8,128)(2,1)}, u32[]{:S(2)}, u32[]{:S(2)}) %collective-permute-start.2) | collective-permute-done | bytes 1376288 | tf_op jit(solution)/shard_map/ppermute | solution.py:1167
  255.1 60.5 %feed_theirs.1 = (bf16[768,1024]{1,0:T(8,128)(2,1)}, bf16[3,256,1152]{2,1,0:T(8,128)(2,1)}, bf16[2432,128]{1,0:T(8,128)(2,1)}, bf16[2432,128]{1,0:T(8,128)(2,1)}, bf16[2432,128]{1,0:T(8,128)(2,1)}) custom-call(bf16[768,896]{1,0:T(8,128)(2,1)} %copy-done.28, bf16[768,896]{1,0:T(8,128)(2,1)} %collective-permute-done.2.dy_ref, ...), custom_call_target="tpu_custom_call" | custom-call | flops 24385683456 | bytes 30000000 | tf_op jit(solution)/shard_map/feed_theirs/pallas_call | solution.py:1021
  315.5 11.2 %middle_back.1 = (f32[768,896]{1,0:T(8,128)}, bf16[768,896]{1,0:T(8,128)(2,1)}, bf16[896,256]{1,0:T(8,128)(2,1)}, bf16[896,128]{1,0:T(8,128)(2,1)}, bf16[896,128]{1,0:T(8,128)(2,1)}) custom-call(f32[768,1152]{1,0:T(8,128)} %get-tuple-element.60.da_ref, bf16[768,1152]{1,0:T(8,128)(2,1)} %bitcast.53, f32[768,896]{1,0:T(8,128)} %get-tuple-element.57.y1_ref, ...), custom_call_target="tpu_custom_call" | custom-call | flops 2614886400 | bytes 20000000 | tf_op jit(solution)/shard_map/middle_back/pallas_call | solution.py:809
  326.7 41.5 %attend_back.1 = (bf16[768,896]{1,0:T(8,128)(2,1)}, bf16[768,256]{1,0:T(8,128)(2,1)}, bf16[768,256]{1,0:T(8,128)(2,1)}) custom-call(s32[2,6]{1,0:T(2,128)} %pad_add_fusion.1.bounds_ref, bf16[768,896]{1,0:T(8,128)(2,1)} %get-tuple-element.59.q_ref, bf16[768,896]{1,0:T(8,128)(2,1)} %get-tuple-element.64.all_ref, bf16[768,896]{1,0:T(8,128)(2,1)} %get-tuple-element.65.o_ref, ...), custom_call_target="tpu_custom_call" | custom-call | flops 10569646080 | bytes 9000000 | tf_op jit(solution)/shard_map/attend_back/pallas_call | solution.py:629
  369.7 5.4 collective-permute-done.5.got_ref
  375.8 9.7 %input_back.1 = (bf16[768,896]{1,0:T(8,128)(2,1)}, bf16[896,384]{1,0:T(8,128)(2,1)}, bf16[1152,128]{1,0:T(8,128)(2,1)}) custom-call(bf16[768,896]{1,0:T(8,128)(2,1)} %get-tuple-element.68.gq_ref, bf16[768,256]{1,0:T(8,128)(2,1)} %get-tuple-element.69.own_ref, bf16[768,256]{1,0:T(8,128)(2,1)} %copy-done.29, bf16[768,896]{1,0:T(8,128)(2,1)} %bitcast.62, ...), custom_call_target="tpu_custom_call" | custom-call | flops 3991142400 | bytes 14000000 | tf_op jit(solution)/shard_map/input_back/pallas_call | solution.py:1083
  392.0 27.9 %all-to-all-start.2 = ((bf16[16,48,896]{2,1,0:T(8,128)(2,1)}), bf16[16,48,896]{2,1,0:T(8,128)(2,1)S(1)}, u32[]{:S(2)}, u32[]{:S(2)}) async-start(bf16[16,48,896]{2,1,0:T(8,128)(2,1)} %bitcast.54), calls=%async_computation.2 | async-start | bytes 2752512 | tf_op jit(solution)/shard_map/all_to_all | solution.py:1175
  427.7 6.2 finish.1
  433.9 14.9 %all-to-all-done.2 = bf16[16,48,896]{2,1,0:T(8,128)(2,1)S(1)} async-done(((bf16[16,48,896]{2,1,0:T(8,128)(2,1)}), bf16[16,48,896]{2,1,0:T(8,128)(2,1)S(1)}, u32[]{:S(2)}, u32[]{:S(2)}) %all-to-all-start.2) | async-done | bytes 1376288 | tf_op jit(solution)/shard_map/all_to_all | solution.py:1175
  448.8 7.9 %all-to-all-start.1 = ((bf16[16,48,896]{2,1,0:T(8,128)(2,1)}), bf16[16,48,896]{2,1,0:T(8,128)(2,1)}, u32[]{:S(2)}, u32[]{:S(2)}) async-start(bf16[16,48,896]{2,1,0:T(8,128)(2,1)} %bitcast.55), calls=%async_computation.1 | async-start | bytes 2752512 | tf_op jit(solution)/shard_map/all_to_all | solution.py:1175
  462.7 23.0 %all-to-all-done.1 = bf16[16,48,896]{2,1,0:T(8,128)(2,1)} async-done(((bf16[16,48,896]{2,1,0:T(8,128)(2,1)}), bf16[16,48,896]{2,1,0:T(8,128)(2,1)}, u32[]{:S(2)}, u32[]{:S(2)}) %all-to-all-start.1) | async-done | bytes 1376288 | tf_op jit(solution)/shard_map/all_to_all | solution.py:1175
  487.2 159.2 %fusion = bf16[720,128]{1,0:T(8,128)(2,1)S(1)} fusion(bf16[22912,128]{1,0:T(8,128)(2,1)} %constant_dynamic-update-slice_fusion), kind=kCustom, calls=%all-reduce-scatter | all-reduce-scatter fusion | flops 2949121 | bytes 6049792
  646.5 2.2 collective-permute-start.7
  648.6 3.1 collective-permute-done.7
  658.4 2.0 select_bitcast_fusion.3
  (154 shorter events, 58.4 us)
Async XLA Ops:
  0.6 96.5 %copy-start = (bf16[1536,896]{1,0:T(8,128)(2,1)S(1)}, bf16[1536,896]{1,0:T(8,128)(2,1)}, u32[]{:S(2)}) copy-start(bf16[1536,896]{1,0:T(8,128)(2,1)} %param.20) | copy-start | bytes 8257540
  0.7 6.2 copy-start.22
  0.7 6.2 copy-start.27
  0.7 6.2 copy-start.26
  67.6 8.2 %copy-start.20 = (s32[1,1536]{1,0:T(1,128)S(1)}, s32[1,1536]{1,0:T(1,128)}, u32[]{:S(2)}) copy-start(s32[1,1536]{1,0:T(1,128)} %param.21) | copy-start | bytes 18436
  67.6 10.3 %copy-start.30 = (s32[1,3]{1,0:T(1,128)S(1)}, s32[1,3]{1,0:T(1,128)}, u32[]{:S(2)}) copy-start(s32[1,3]{1,0:T(1,128)} %param.22) | copy-start | bytes 40
  69.9 9.6 %copy-start.23 = (s32[1,3]{1,0:T(1,128)S(1)}, s32[1,3]{1,0:T(1,128)}, u32[]{:S(2)}) copy-start(s32[1,3]{1,0:T(1,128)} %param.23) | copy-start | bytes 40
  69.9 9.8 %copy-start.21 = (bf16[2,896]{1,0:T(2,128)(2,1)S(1)}, bf16[2,896]{1,0:T(2,128)(2,1)}, u32[]{:S(2)}) copy-start(bf16[2,896]{1,0:T(2,128)(2,1)} %param.24) | copy-start | bytes 10756
  96.7 43.1 %collective-permute-start = (bf16[768,256]{1,0:T(8,128)(2,1)}, bf16[768,256]{1,0:T(8,128)(2,1)}, u32[]{:S(2)}, u32[]{:S(2)}) collective-permute-start(bf16[768,256]{1,0:T(8,128)(2,1)} %get-tuple-element.50.own_ref), channel_id=1, source_target_pairs={{0,1},{1,0},{2,3},{3,2},{4,5},{5,4},{6,7},{7,6},{8,9},{9,8},{10,11... | collective-permute-start | bytes 1179656 | tf_op jit(solution)/shard_map/ppermute | solution.py:1167
  98.4 102.1 %all-to-all-start = ((bf16[16,48,896]{2,1,0:T(8,128)(2,1)}), bf16[16,48,896]{2,1,0:T(8,128)(2,1)S(1)}, u32[]{:S(2)}, u32[]{:S(2)}) async-start(bf16[16,48,896]{2,1,0:T(8,128)(2,1)} %dynamic-slice_bitcast_fusion), calls=%async_computation | async-start | bytes 2752512 | tf_op jit(solution)/shard_map/all_to_all | solution.py:1204
  112.6 8.8 %copy-start.19 = (s32[1,1536]{1,0:T(1,128)S(1)}, s32[1,1536]{1,0:T(1,128)}, u32[]{:S(2)}) copy-start(s32[1,1536]{1,0:T(1,128)} %get-tuple-element.97) | copy-start | bytes 18436
  112.6 9.1 %copy-start.18 = (s32[1536,1]{0,1:T(1,128)S(1)}, s32[1536,1]{0,1:T(1,128)}, u32[]{:S(2)}) copy-start(s32[1536,1]{0,1:T(1,128)} %get-tuple-element.121) | copy-start | bytes 18436
  127.4 5.7 copy-start.3
  200.2 41.4 %collective-permute-start.1 = (bf16[768,896]{1,0:T(8,128)(2,1)}, bf16[768,896]{1,0:T(8,128)(2,1)S(1)}, u32[]{:S(2)}, u32[]{:S(2)}) collective-permute-start(bf16[768,896]{1,0:T(8,128)(2,1)} %get-tuple-element.53.n_ref), channel_id=1, source_target_pairs={{0,1},{1,0},{2,3},{3,2},{4,5},{5,4},{6,7},{7,6},{8,9},{9,8},{10,11... | collective-permute-start | bytes 4128776 | tf_op jit(solution)/shard_map/ppermute | solution.py:1167
  200.5 53.6 %collective-permute-start.2 = (bf16[768,896]{1,0:T(8,128)(2,1)S(1)}, bf16[768,896]{1,0:T(8,128)(2,1)}, u32[]{:S(2)}, u32[]{:S(2)}) collective-permute-start(bf16[768,896]{1,0:T(8,128)(2,1)S(1)} %bitcast.45), channel_id=1, source_target_pairs={{0,1},{1,0},{2,3},{3,2},{4,5},{5,4},{6,7},{7,6},{8,9},{9,8},{10,11... | collective-permute-start | bytes 4128776 | tf_op jit(solution)/shard_map/ppermute | solution.py:1167
  241.7 13.4 %copy-start.28 = (bf16[768,896]{1,0:T(8,128)(2,1)}, bf16[768,896]{1,0:T(8,128)(2,1)S(1)}, u32[]{:S(2)}) copy-start(bf16[768,896]{1,0:T(8,128)(2,1)S(1)} %collective-permute-done.1.n_ref) | copy-start | bytes 4128772
  368.2 6.8 %collective-permute-start.5 = (bf16[768,256]{1,0:T(8,128)(2,1)}, bf16[768,256]{1,0:T(8,128)(2,1)S(1)}, u32[]{:S(2)}, u32[]{:S(2)}) collective-permute-start(bf16[768,256]{1,0:T(8,128)(2,1)} %get-tuple-element.70), channel_id=1, source_target_pairs={{0,1},{1,0},{2,3},{3,2},{4,5},{5,4},{6,7},{7,6},{8,9},{9,8},{10,11... | collective-permute-start | bytes 1179656 | tf_op jit(solution)/shard_map/ppermute | solution.py:1167
  368.5 59.2 %collective-permute-start.3 = (bf16[768,1024]{1,0:T(8,128)(2,1)}, bf16[768,1024]{1,0:T(8,128)(2,1)}, u32[]{:S(2)}, u32[]{:S(2)}) collective-permute-start(bf16[768,1024]{1,0:T(8,128)(2,1)} %get-tuple-element.56), channel_id=1, source_target_pairs={{0,1},{1,0},{2,3},{3,2},{4,5},{5,4},{6,7},{7,6},{8,9},{9,8},{10,11... | collective-permute-start | bytes 4718600 | tf_op jit(solution)/shard_map/ppermute | solution.py:1167
  385.6 37.4 %copy-start.16 = (bf16[896,128]{1,0:T(8,128)(2,1)S(1)}, bf16[896,128]{1,0:T(8,128)(2,1)}, u32[]{:S(2)}) copy-start(bf16[896,128]{1,0:T(8,128)(2,1)} %get-tuple-element.78) | copy-start | bytes 688132
  385.6 38.1 %copy-start.15 = (bf16[896,128]{1,0:T(8,128)(2,1)S(1)}, bf16[896,128]{1,0:T(8,128)(2,1)}, u32[]{:S(2)}) copy-start(bf16[896,128]{1,0:T(8,128)(2,1)} %get-tuple-element.79) | copy-start | bytes 688132
  385.6 38.8 %copy-start.13 = (bf16[896,256]{1,0:T(8,128)(2,1)S(1)}, bf16[896,256]{1,0:T(8,128)(2,1)}, u32[]{:S(2)}) copy-start(bf16[896,256]{1,0:T(8,128)(2,1)} %get-tuple-element.80) | copy-start | bytes 1376260
  387.3 37.8 %copy-start.7 = (bf16[2432,128]{1,0:T(8,128)(2,1)S(1)}, bf16[2432,128]{1,0:T(8,128)(2,1)}, u32[]{:S(2)}) copy-start(bf16[2432,128]{1,0:T(8,128)(2,1)} %get-tuple-element.81) | copy-start | bytes 1867780
  392.0 56.8 %all-to-all-start.2 = ((bf16[16,48,896]{2,1,0:T(8,128)(2,1)}), bf16[16,48,896]{2,1,0:T(8,128)(2,1)S(1)}, u32[]{:S(2)}, u32[]{:S(2)}) async-start(bf16[16,48,896]{2,1,0:T(8,128)(2,1)} %bitcast.54), calls=%async_computation.2 | async-start | bytes 2752512 | tf_op jit(solution)/shard_map/all_to_all | solution.py:1175
  433.9 22.9 %copy-start.6 = (bf16[2432,128]{1,0:T(8,128)(2,1)S(1)}, bf16[2432,128]{1,0:T(8,128)(2,1)}, u32[]{:S(2)}) copy-start(bf16[2432,128]{1,0:T(8,128)(2,1)} %get-tuple-element.82) | copy-start | bytes 1867780
  433.9 24.8 %copy-start.5 = (bf16[2432,128]{1,0:T(8,128)(2,1)S(1)}, bf16[2432,128]{1,0:T(8,128)(2,1)}, u32[]{:S(2)}) copy-start(bf16[2432,128]{1,0:T(8,128)(2,1)} %get-tuple-element.83) | copy-start | bytes 1867780
  448.8 36.9 %all-to-all-start.1 = ((bf16[16,48,896]{2,1,0:T(8,128)(2,1)}), bf16[16,48,896]{2,1,0:T(8,128)(2,1)}, u32[]{:S(2)}, u32[]{:S(2)}) async-start(bf16[16,48,896]{2,1,0:T(8,128)(2,1)} %bitcast.55), calls=%async_computation.1 | async-start | bytes 2752512 | tf_op jit(solution)/shard_map/all_to_all | solution.py:1175
  461.3 191.3 %copy-start.10 = (f32[716,128]{1,0:T(8,128)S(1)}, f32[716,128]{1,0:T(8,128)}, u32[]{:S(2)}) copy-start(f32[716,128]{1,0:T(8,128)} %param.35) | copy-start | bytes 1099780
  461.3 191.4 %copy-start.11 = (f32[716,128]{1,0:T(8,128)S(1)}, f32[716,128]{1,0:T(8,128)}, u32[]{:S(2)}) copy-start(f32[716,128]{1,0:T(8,128)} %param.36) | copy-start | bytes 1099780
  461.3 191.4 %copy-start.14 = (f32[716,128]{1,0:T(8,128)S(1)}, f32[716,128]{1,0:T(8,128)}, u32[]{:S(2)}) copy-start(f32[716,128]{1,0:T(8,128)} %param.37) | copy-start | bytes 1099780
  461.3 193.5 %collective-permute-start.6 = (bf16[16,48,896]{2,1,0:T(8,128)(2,1)S(1)}, bf16[16,48,896]{2,1,0:T(8,128)(2,1)}, u32[]{:S(2)}, u32[]{:S(2)}) collective-permute-start(bf16[16,48,896]{2,1,0:T(8,128)(2,1)S(1)} %all-to-all-done.2), channel_id=1, source_target_pairs={{0,1},{1,0},{2,3},{3,2},{4,5},{5,4},{6,7},{7,6},{8,9},{9,8},{10,11... | collective-permute-start | bytes 4128776 | tf_op jit(solution)/shard_map/ppermute | solution.py:1167
  485.7 172.7 %collective-permute-start.4 = (bf16[16,48,896]{2,1,0:T(8,128)(2,1)}, bf16[16,48,896]{2,1,0:T(8,128)(2,1)}, u32[]{:S(2)}, u32[]{:S(2)}) collective-permute-start(bf16[16,48,896]{2,1,0:T(8,128)(2,1)} %all-to-all-done.1), channel_id=1, source_target_pairs={{0,1},{1,0},{2,3},{3,2},{4,5},{5,4},{6,7},{7,6},{8,9},{9,8},{10,11... | collective-permute-start | bytes 4128776 | tf_op jit(solution)/shard_map/ppermute | solution.py:1167
  646.5 5.2 collective-permute-start.7
  (10 other events, 31.5 us)
